TPU v7x, 512 devices: a whole 4x8x8 slice. The times are simulated.
512 devices in a mesh: dom: 32 (over z, y_hi), cluster: 16 (over x, y_lo, core).
Axes of the slice: x: 4, y: 8 (y_hi: 4, y_lo: 2; y = y_hi * 2 + y_lo), z: 8, core: 2. Of those that a mesh axis runs over, the one named last changes fastest.
Arguments:
- features: bfloat16 [16, 24576, 512], P('cluster', 'dom'), may hold values from -6 to 6
- stale: bfloat16 [16, 1024, 512], P('cluster'), may hold values from -6 to 6
- boundary: int32 [16, 32], P('cluster', 'dom'), may hold values from 0 to 23
- skip: int32 [16, 32], P('cluster'), may hold values 0 or 1
- tile_vals: bfloat16 [16, 1024, 32, 128], P('cluster', 'dom'), may hold values from -0.4375 to 0.4375
- tile_row: int32 [16, 1024], P('cluster', 'dom'), may hold values from 0 to 5
- tile_src: int32 [16, 1024], P('cluster', 'dom'), may hold values from 0 to 33
- tile_count: int32 [16, 32], P('cluster', 'dom'), may hold values from 16 to 32, as said below
- weight: bfloat16 [512, 512], replicated, may hold values from -0.25 to 0.25
- cotangent: bfloat16 [16, 24576, 512], P('cluster', 'dom'), may hold values from -6 to 6
Outputs:
- out_features: bfloat16 [16, 24576, 512], P('cluster', 'dom')
- grad_features: bfloat16 [16, 24576, 512], P('cluster', 'dom')
- grad_weight: float32 [512, 512], P('dom')
Inputs may be any that keep to these rules, and one draw needn't show every extreme that they name: `tile_count`: every partition has at least half of its slots live; some partition has all 32 slots live.
All inputs are finite; a program needn't handle non-finite values. No bound on the sum of `skip` on one device may be relied on, other than what follows from the above.
Results may differ from a plain program's by a relative error of at most 0.02.
Values may be sent and summed in bfloat16 or wider, within the bound.
No kernel may reach another device: no remote copies, remote signals or barrier semaphores. Data moves between devices by JAX's collectives and lax.ppermute only.
A program may use at most 64 MiB of HBM per device.

v0:
```python
import jax
import jax.numpy as jnp
from jax import lax
from jax.sharding import Mesh
from jax.sharding import PartitionSpec as P

DOM = ("dom_0", "dom_1")


def laid_out(blocks, dim):
    lengths = list(blocks.shape[1:])
    lengths[dim] *= blocks.shape[0]
    return jnp.moveaxis(blocks, 0, dim).reshape(lengths)


def copy_for_each(x, axis):
    copies = jnp.broadcast_to(x, (lax.axis_size(axis), *x.shape))
    return lax.all_to_all(copies, axis, split_axis=0, concat_axis=0, tiled=True)


def collect(x, axis, dim):
    return laid_out(copy_for_each(x, axis), dim)


def padded(cells, sides, width):
    for axis, dim in sides:
        count = lax.axis_size(axis)
        head = lax.slice_in_dim(cells, 0, width, axis=dim)
        tail = lax.slice_in_dim(cells, cells.shape[dim] - width, cells.shape[dim], axis=dim)
        cells = jnp.concatenate(
            [
                lax.ppermute(tail, axis, [(i, (i + 1) % count) for i in range(count)]),
                cells,
                lax.ppermute(head, axis, [((i + 1) % count, i) for i in range(count)]),
            ],
            axis=dim,
        )
    return cells


def passed_along(x, axis, by):
    count = lax.axis_size(axis)
    return lax.ppermute(x, axis, [(i, (i + by) % count) for i in range(count)])


def sum_by_axis(x, axes, dim):
    for axis in axes:
        x = lax.psum_scatter(x, axis, scatter_dimension=dim, tiled=True)
    return x


def taken_together(x, axis):
    return copy_for_each(x, axis).astype(jnp.float32).sum(axis=0)


def silu_parts(value):
    sig = jax.nn.sigmoid(value)
    return (value * sig, sig * (1.0 + value * (1.0 - sig)))


def per_device(
    features, stale, boundary, skip, tile_vals, tile_row, tile_src, tile_count, weight, cotangent
):
    feats = features[0]
    nodes, width = feats.shape
    parts = lax.axis_size(DOM)
    blk = stale.shape[1] // parts
    tile_blocks = tile_vals[0]
    slots, _, tile_rows = tile_blocks.shape
    row_blocks = nodes // tile_rows
    start_row = boundary[0, 0] * blk
    own_block = lax.dynamic_slice_in_dim(feats, start_row, blk, 0)
    gathered = collect(own_block, DOM, 0).reshape(parts, blk, width)
    beside_all = padded(own_block[None], (("cluster", 0),), 1)
    skipped = skip[0] == 1
    fresh = jnp.where(skipped[:, None, None], stale[0].reshape(parts, blk, width), gathered)
    table = jnp.concatenate([fresh, beside_all[0:1], beside_all[2:3]], axis=0)
    active_mask = (jnp.arange(slots, dtype=jnp.int32) < tile_count[0, 0]).astype(jnp.float32)
    sources = tile_src[0]
    targets = tile_row[0]
    selected_block = jnp.take(table, sources, axis=0)
    contribution = (
        jnp.einsum("wnz,wnx->wzx", tile_blocks, selected_block, preferred_element_type=jnp.float32)
        * active_mask[:, None, None]
    )
    row_onehot_mask = (targets[:, None] == jnp.arange(row_blocks, dtype=jnp.int32)[None, :]).astype(
        jnp.float32
    )
    row_onehot_mask = row_onehot_mask * active_mask[:, None]
    aggregate_block_list = jnp.einsum(
        "xn,xij->nij", row_onehot_mask, contribution, precision=lax.Precision.HIGHEST
    )
    agg = (feats.astype(jnp.float32) + aggregate_block_list.reshape(nodes, width)).astype(
        jnp.bfloat16
    )
    zval = jnp.dot(agg, weight, preferred_element_type=jnp.float32)
    act, slope = silu_parts(zval)
    out_features = act.astype(jnp.bfloat16)
    dz = (cotangent[0].astype(jnp.float32) * slope).astype(jnp.bfloat16)
    dagg = lax.dot_general(
        dz, weight, (((1,), (1,)), ((), ())), preferred_element_type=jnp.float32
    ).astype(jnp.bfloat16)
    selected_rows = jnp.take(dagg.reshape(row_blocks, tile_rows, width), targets, axis=0)
    selected_gradient = (
        jnp.einsum("dck,dkn->dcn", tile_blocks, selected_rows, preferred_element_type=jnp.float32)
        * active_mask[:, None, None]
    )
    src_hot = (sources[:, None] == jnp.arange(parts + 2, dtype=jnp.int32)[None, :]).astype(
        jnp.float32
    )
    dsrc = jnp.einsum("ts,tbf->sbf", src_hot, selected_gradient, precision=lax.Precision.HIGHEST)
    keep = 1.0 - skipped.astype(jnp.float32)
    in_group = dsrc[:parts] * keep[:, None, None]
    from_upper = passed_along(dsrc[parts].astype(jnp.bfloat16), "cluster", -1).astype(jnp.float32)
    from_lower = passed_along(dsrc[parts + 1].astype(jnp.bfloat16), "cluster", 1).astype(
        jnp.float32
    )
    share = width // parts
    term_all = lax.dot_general(
        agg, dz, (((0,), (0,)), ((), ())), preferred_element_type=jnp.float32
    ).reshape(parts, share, width)
    stacked = jnp.concatenate([in_group, term_all], axis=1).reshape(parts * (blk + share), width)
    summed = sum_by_axis(stacked.astype(jnp.bfloat16), DOM, 0).astype(jnp.float32)
    mine = summed[:blk]
    grad_weight = taken_together(summed[blk:].astype(jnp.bfloat16), "cluster").astype(jnp.float32)
    bgrad = mine + from_upper + from_lower
    full = dagg.astype(jnp.float32)
    current = lax.dynamic_slice_in_dim(full, start_row, blk, 0)
    full = lax.dynamic_update_slice_in_dim(full, current + bgrad, start_row, 0)
    grad_features = full.astype(jnp.bfloat16)
    return (out_features[None], grad_features[None], grad_weight)


def solution(mesh):
    finer = Mesh(mesh.devices.reshape(8, 4, mesh.shape["cluster"]), ("dom_0", "dom_1", "cluster"))
    placed = (
        P("cluster", DOM, None),
        P("cluster", None, None),
        P("cluster", DOM),
        P("cluster", None),
        P("cluster", DOM, None, None),
        P("cluster", DOM),
        P("cluster", DOM),
        P("cluster", DOM),
        P(),
        P("cluster", DOM, None),
    )
    return jax.shard_map(
        per_device,
        mesh=finer,
        in_specs=placed,
        out_specs=(P("cluster", DOM, None), P("cluster", DOM, None), P(DOM, None)),
        check_vma=False,
    )
```

profile of v0, /device:TPU:1, one launch (start us, length us, event | category | flops | bytes accessed | tf_op | source)
XLA Modules:
  0.0 191.5 jit_solution(6673618662656293658)
XLA Ops:
  7.2 0.0 copy-start
  7.9 0.8 fusion.39
  8.7 0.0 copy-start.1
  8.7 1.1 broadcast_in_dim.50
  9.8 16.5 %all-to-all-start = ((bf16[32,32,512]{2,1,0:T(8,128)(2,1)}), bf16[32,32,512]{2,1,0:T(8,128)(2,1)S(1)}, u32[]{:S(2)}, u32[]{:S(2)}) async-start(bf16[32,32,512]{2,1,0:T(8,128)(2,1)} %broadcast_in_dim.50), calls=%async_computation | async-start | bytes 2097152 | tf_op jit(solution)/shard_map/all_to_all | solution.py:18
  26.3 0.0 reduce-scatter.3.cloned.1.call-start
  26.4 3.1 %collective-permute-start = (bf16[1,32,512]{2,1,0:T(8,128)(2,1)S(1)}, bf16[1,32,512]{2,1,0:T(8,128)(2,1)S(1)}, u32[]{:S(2)}, u32[]{:S(2)}) collective-permute-start(bf16[1,32,512]{2,1,0:T(8,128)(2,1)S(1)} %constant_dynamic-slice_fusion), channel_id=1, source_target_pairs={{0,1},{1,2},{2,3},{3,4},{4,5},{5,6},{6,7},{7,8},{8,9},{9,10},{10,1... | collective-permute-start | bytes 98312 | tf_op jit(solution)/shard_map/ppermute | solution.py:32
  29.6 1.9 %collective-permute-start.1 = (bf16[1,32,512]{2,1,0:T(8,128)(2,1)S(1)}, bf16[1,32,512]{2,1,0:T(8,128)(2,1)S(1)}, u32[]{:S(2)}, u32[]{:S(2)}) collective-permute-start(bf16[1,32,512]{2,1,0:T(8,128)(2,1)S(1)} %constant_dynamic-slice_fusion), channel_id=1, source_target_pairs={{1,0},{2,1},{3,2},{4,3},{5,4},{6,5},{7,6},{8,7},{9,8},{10,9},{11,1... | collective-permute-start | bytes 98312 | tf_op jit(solution)/shard_map/ppermute | solution.py:34
  32.2 0.5 compare_and_fusion.1
  32.7 0.5 convert_subtract_fusion
  33.3 0.5 compare_and_fusion
  33.8 23.7 %all-to-all-done = bf16[32,32,512]{2,1,0:T(8,128)(2,1)S(1)} async-done(((bf16[32,32,512]{2,1,0:T(8,128)(2,1)}), bf16[32,32,512]{2,1,0:T(8,128)(2,1)S(1)}, u32[]{:S(2)}, u32[]{:S(2)}) %all-to-all-start) | async-done | bytes 1048608 | tf_op jit(solution)/shard_map/all_to_all | solution.py:18
  57.5 0.2 broadcast_select_fusion
  57.7 0.1 pad_maximum_fusion.1
  57.9 0.6 gather_fusion
  58.5 0.0 copy-done.8
  58.5 6.1 %multiply_bitcast_fusion = f32[32,128,512]{1,2,0:T(8,128)} fusion(f32[32]{0:T(128)S(1)} %get-tuple-element.10, bf16[32,32,512]{2,1,0:T(8,128)(2,1)S(1)} %gather_fusion, pred[32]{0:T(512)(128)(4,1)S(1)} %copy-done.8, bf16[1,32,32,128]{3,2,1,0:T(8,128)(2,1)} %param.14), kind=kOutput, calls=%fused_computation.2 | convolution fusion | flops 136839168 | bytes 9699488 | tf_op jit(solution)/shard_map/wnz,wnx->wzx/dot_general | solution.py:83
  64.6 10.3 %copy.22 = f32[32,128,512]{2,0,1:T(8,128)} copy(f32[32,128,512]{1,2,0:T(8,128)} %multiply_bitcast_fusion) | data formatting | bytes 16777216 | tf_op jit(solution)/shard_map/mul | solution.py:83
  74.9 6.4 %fusion.22 = f32[6,128,512]{2,0,1:T(8,128)S(1)} fusion(f32[32,128,512]{2,0,1:T(8,128)} %copy.22, f32[32]{0:T(128)S(1)} %get-tuple-element.10, s32[32]{0:T(128)S(1)} %bitcast.70), kind=kOutput, calls=%fused_computation.42 | convolution fusion | flops 150995328 | bytes 9961728 | tf_op jit(solution)/shard_map/xn,xij->nij/dot_general | solution.py:90
  81.3 0.9 copy.23
  82.2 0.3 fusion.10
  82.5 0.3 copy.25
  82.8 0.8 copy-done.11
  83.7 2.0 %fusion.9 = (bf16[768,512]{1,0:T(8,128)(2,1)S(1)}, bf16[1,768,512]{2,1,0:T(8,128)(2,1)}) fusion(bf16[1,768,512]{2,1,0:T(8,128)(2,1)S(1)} %copy-done.11, bf16[768,512]{1,0:T(8,128)(2,1)S(1)} %fusion.10, bf16[512,512]{1,0:T(8,128)(2,1)S(1)} %copy-done), kind=kOutput, calls=%fused_computation.15 | convolution fusion | flops 407371776 | bytes 3670016 | tf_op jit(solution)/shard_map/dot_general | solution.py:96
  85.6 1.8 fusion.33
  87.4 1.4 convolution_convert_fusion.1
  88.8 2.8 %gather_fusion.1 = bf16[32,128,512]{2,1,0:T(8,128)(2,1)} fusion(bf16[6,128,512]{2,1,0:T(8,128)(2,1)S(1)} %bitcast.65, s32[1024]{0:T(1024)S(1)} %pad_clamp_fusion), kind=kCustom, calls=%fused_computation.1 | custom fusion | bytes 8388736 | tf_op jit(solution)/shard_map/jit(_take)/gather | solution.py:103
  91.6 3.4 %multiply_bitcast_fusion.1 = f32[32,32,512]{2,1,0:T(8,128)S(1)} fusion(bf16[32,128,512]{2,1,0:T(8,128)(2,1)} %gather_fusion.1, pred[32]{0:T(512)(128)(4,1)S(1)} %copy-done.9, f32[32]{0:T(128)S(1)} %get-tuple-element.10, bf16[1,32,32,128]{3,2,1,0:T(8,128)(2,1)S(1)} %copy-done.4), kind=kOutput, calls=%fused_computation.11 | convolution fusion | flops 136839168 | bytes 6553760 | tf_op jit(solution)/shard_map/dck,dkn->dcn/dot_general | solution.py:105
  95.0 2.7 %fusion.4 = f32[34,32,512]{2,0,1:T(8,128)S(1)} fusion(f32[32,32,512]{2,1,0:T(8,128)S(1)} %multiply_bitcast_fusion.1, s32[32]{0:T(128)S(1)} %bitcast.71), kind=kOutput, calls=%fused_computation.9 | convolution fusion | flops 213910592 | bytes 4325504 | tf_op jit(solution)/shard_map/ts,tbf->sbf/dot_general | solution.py:111
  97.7 0.3 fusion.3
  98.1 0.7 copy-done.3
  98.8 0.1 pad_maximum_fusion
  98.9 2.0 %copy.27 = bf16[32,48,512]{2,1,0:T(8,128)(2,1)} copy(bf16[32,48,512]{2,0,1:T(8,128)(2,1)S(1)} %pad_maximum_fusion) | data formatting | bytes 3145728 | tf_op jit(solution)/shard_map/concatenate | solution.py:122
  100.9 0.0 reduce-scatter.3.cloned.1.call-update
  101.0 0.0 reduce-scatter.5.cloned.1.call-start
  101.0 36.8 %reduce-scatter.3.cloned.1.call-done = bf16[192,512]{1,0:T(8,128)(2,1)} async-done(((bf16[1536,512]{1,0:T(8,128)(2,1)}), bf16[192,512]{1,0:T(8,128)(2,1)}) %reduce-scatter.3.cloned.1.call-update) | async-done | bytes 196624 | tf_op jit(solution)/shard_map/reduce_scatter | solution.py:48
  137.8 0.0 reduce-scatter.5.cloned.1.call-update
  137.8 1.2 copy.36
  139.0 6.6 %collective-permute-start.2 = (bf16[32,512]{1,0:T(8,128)(2,1)S(1)}, bf16[32,512]{1,0:T(8,128)(2,1)S(1)}, u32[]{:S(2)}, u32[]{:S(2)}) collective-permute-start(bf16[32,512]{1,0:T(8,128)(2,1)S(1)} %get-tuple-element.5), channel_id=1, source_target_pairs={{0,15},{1,0},{2,1},{3,2},{4,3},{5,4},{6,5},{7,6},{8,7},{9,8},{10,9... | collective-permute-start | bytes 98312 | tf_op jit(solution)/shard_map/ppermute | solution.py:43
  145.6 3.0 %collective-permute-start.3 = (bf16[32,512]{1,0:T(8,128)(2,1)S(1)}, bf16[32,512]{1,0:T(8,128)(2,1)S(1)}, u32[]{:S(2)}, u32[]{:S(2)}) collective-permute-start(bf16[32,512]{1,0:T(8,128)(2,1)S(1)} %get-tuple-element.6), channel_id=1, source_target_pairs={{0,1},{1,2},{2,3},{3,4},{4,5},{5,6},{6,7},{7,8},{8,9},{9,10},{10,1... | collective-permute-start | bytes 98312 | tf_op jit(solution)/shard_map/ppermute | solution.py:43
  148.6 19.7 %reduce-scatter.5.cloned.1.call-done = bf16[48,512]{1,0:T(8,128)(2,1)} async-done(((bf16[192,512]{1,0:T(8,128)(2,1)}), bf16[48,512]{1,0:T(8,128)(2,1)}) %reduce-scatter.5.cloned.1.call-update) | async-done | bytes 49168 | tf_op jit(solution)/shard_map/reduce_scatter | solution.py:48
  168.3 0.7 slice.35
  169.0 0.7 broadcast_in_dim.56
  169.8 7.1 %all-to-all-start.1 = ((bf16[16,16,512]{2,1,0:T(8,128)(2,1)}), bf16[16,16,512]{2,1,0:T(8,128)(2,1)S(1)}, u32[]{:S(2)}, u32[]{:S(2)}) async-start(bf16[16,16,512]{2,1,0:T(8,128)(2,1)} %broadcast_in_dim.56), calls=%async_computation.3 | async-start | bytes 524288 | tf_op jit(solution)/shard_map/all_to_all | solution.py:18
  176.8 1.5 add_dynamic-update-slice_fusion
  178.3 2.4 %convert_bitcast_fusion = bf16[1,768,512]{2,1,0:T(8,128)(2,1)} fusion(f32[768,512]{1,0:T(8,128)} %add_dynamic-update-slice_fusion), kind=kLoop, calls=%fused_computation.28 | loop fusion | flops 393216 | bytes 2359296 | tf_op jit(solution)/shard_map/broadcast_in_dim | solution.py:131
  180.7 3.3 %all-to-all-done.1 = bf16[16,16,512]{2,1,0:T(8,128)(2,1)S(1)} async-done(((bf16[16,16,512]{2,1,0:T(8,128)(2,1)}), bf16[16,16,512]{2,1,0:T(8,128)(2,1)S(1)}, u32[]{:S(2)}, u32[]{:S(2)}) %all-to-all-start.1) | async-done | bytes 262176 | tf_op jit(solution)/shard_map/all_to_all | solution.py:18
  184.0 0.7 convert_reduce_fusion
  (32 shorter events, 0.1 us)
Async XLA Ops:
  7.2 75.7 %copy-start = (bf16[512,512]{1,0:T(8,128)(2,1)S(1)}, bf16[512,512]{1,0:T(8,128)(2,1)}, u32[]{:S(2)}) copy-start(bf16[512,512]{1,0:T(8,128)(2,1)} %param.18) | copy-start | bytes 1572868
  8.7 17.7 %copy-start.2 = (bf16[1,768,512]{2,1,0:T(8,128)(2,1)S(1)}, bf16[1,768,512]{2,1,0:T(8,128)(2,1)}, u32[]{:S(2)}) copy-start(bf16[1,768,512]{2,1,0:T(8,128)(2,1)} %param.10) | copy-start | bytes 2359300
  8.7 23.5 %copy-start.6 = (s32[1,32]{1,0:T(1,128)S(1)}, s32[1,32]{1,0:T(1,128)}, u32[]{:S(2)}) copy-start(s32[1,32]{1,0:T(1,128)} %param.16) | copy-start | bytes 388
  8.7 23.5 %copy-start.5 = (s32[1,32]{1,0:T(1,128)S(1)}, s32[1,32]{1,0:T(1,128)}, u32[]{:S(2)}) copy-start(s32[1,32]{1,0:T(1,128)} %param.15) | copy-start | bytes 388
  8.7 24.1 %copy-start.12 = (s32[1,32]{1,0:T(1,128)S(1)}, s32[1,32]{1,0:T(1,128)}, u32[]{:S(2)}) copy-start(s32[1,32]{1,0:T(1,128)} %param.13) | copy-start | bytes 388
  8.7 48.8 %copy-start.1 = (bf16[1,1024,512]{2,1,0:T(8,128)(2,1)S(1)}, bf16[1,1024,512]{2,1,0:T(8,128)(2,1)}, u32[]{:S(2)}) copy-start(bf16[1,1024,512]{2,1,0:T(8,128)(2,1)} %param.11) | copy-start | bytes 3145732
  9.8 47.7 %all-to-all-start = ((bf16[32,32,512]{2,1,0:T(8,128)(2,1)}), bf16[32,32,512]{2,1,0:T(8,128)(2,1)S(1)}, u32[]{:S(2)}, u32[]{:S(2)}) async-start(bf16[32,32,512]{2,1,0:T(8,128)(2,1)} %broadcast_in_dim.50), calls=%async_computation | async-start | bytes 2097152 | tf_op jit(solution)/shard_map/all_to_all | solution.py:18
  26.3 111.4 %reduce-scatter.3.cloned.1.call-start = ((), (), s32[]{:S(2)}) async-start(), calls=%async_computation.4 | async-start | bytes 1769472 | tf_op jit(solution)/shard_map/reduce_scatter | solution.py:48
  26.4 31.3 %collective-permute-start = (bf16[1,32,512]{2,1,0:T(8,128)(2,1)S(1)}, bf16[1,32,512]{2,1,0:T(8,128)(2,1)S(1)}, u32[]{:S(2)}, u32[]{:S(2)}) collective-permute-start(bf16[1,32,512]{2,1,0:T(8,128)(2,1)S(1)} %constant_dynamic-slice_fusion), channel_id=1, source_target_pairs={{0,1},{1,2},{2,3},{3,4},{4,5},{5,6},{6,7},{7,8},{8,9},{9,10},{10,1... | collective-permute-start | bytes 98312 | tf_op jit(solution)/shard_map/ppermute | solution.py:32
  29.6 28.1 %collective-permute-start.1 = (bf16[1,32,512]{2,1,0:T(8,128)(2,1)S(1)}, bf16[1,32,512]{2,1,0:T(8,128)(2,1)S(1)}, u32[]{:S(2)}, u32[]{:S(2)}) collective-permute-start(bf16[1,32,512]{2,1,0:T(8,128)(2,1)S(1)} %constant_dynamic-slice_fusion), channel_id=1, source_target_pairs={{1,0},{2,1},{3,2},{4,3},{5,4},{6,5},{7,6},{8,7},{9,8},{10,9},{11,1... | collective-permute-start | bytes 98312 | tf_op jit(solution)/shard_map/ppermute | solution.py:34
  57.9 0.7 copy-start.8
  82.5 1.1 copy-start.11
  88.8 2.8 %copy-start.4 = (bf16[1,32,32,128]{3,2,1,0:T(8,128)(2,1)S(1)}, bf16[1,32,32,128]{3,2,1,0:T(8,128)(2,1)}, u32[]{:S(2)}) copy-start(bf16[1,32,32,128]{3,2,1,0:T(8,128)(2,1)} %param.14) | copy-start | bytes 786436
  88.8 2.8 %copy-start.9 = (pred[32]{0:T(512)(128)(4,1)S(1)}, pred[32]{0:T(512)(128)(4,1)}, u32[]{:S(2)}) copy-start(pred[32]{0:T(512)(128)(4,1)} %get-tuple-element.9) | copy-start | bytes 100
  91.6 3.4 %copy-start.7 = (s32[1,32]{1,0:T(1,128)S(1)}, s32[1,32]{1,0:T(1,128)}, u32[]{:S(2)}) copy-start(s32[1,32]{1,0:T(1,128)} %param.16) | copy-start | bytes 388
  95.0 2.7 %copy-start.10 = (f32[32]{0:T(128)S(1)}, f32[32]{0:T(128)}, u32[]{:S(2)}) copy-start(f32[32]{0:T(128)} %convert_subtract_fusion) | copy-start | bytes 388
  97.7 1.0 copy-start.3
  101.0 67.3 %reduce-scatter.5.cloned.1.call-start = ((), (), s32[]{:S(2)}) async-start(), calls=%async_computation.5 | async-start | bytes 245760 | tf_op jit(solution)/shard_map/reduce_scatter | solution.py:48
  139.0 37.8 %collective-permute-start.2 = (bf16[32,512]{1,0:T(8,128)(2,1)S(1)}, bf16[32,512]{1,0:T(8,128)(2,1)S(1)}, u32[]{:S(2)}, u32[]{:S(2)}) collective-permute-start(bf16[32,512]{1,0:T(8,128)(2,1)S(1)} %get-tuple-element.5), channel_id=1, source_target_pairs={{0,15},{1,0},{2,1},{3,2},{4,3},{5,4},{6,5},{7,6},{8,7},{9,8},{10,9... | collective-permute-start | bytes 98312 | tf_op jit(solution)/shard_map/ppermute | solution.py:43
  145.6 31.2 %collective-permute-start.3 = (bf16[32,512]{1,0:T(8,128)(2,1)S(1)}, bf16[32,512]{1,0:T(8,128)(2,1)S(1)}, u32[]{:S(2)}, u32[]{:S(2)}) collective-permute-start(bf16[32,512]{1,0:T(8,128)(2,1)S(1)} %get-tuple-element.6), channel_id=1, source_target_pairs={{0,1},{1,2},{2,3},{3,4},{4,5},{5,6},{6,7},{7,8},{8,9},{9,10},{10,1... | collective-permute-start | bytes 98312 | tf_op jit(solution)/shard_map/ppermute | solution.py:43
  169.8 14.3 %all-to-all-start.1 = ((bf16[16,16,512]{2,1,0:T(8,128)(2,1)}), bf16[16,16,512]{2,1,0:T(8,128)(2,1)S(1)}, u32[]{:S(2)}, u32[]{:S(2)}) async-start(bf16[16,16,512]{2,1,0:T(8,128)(2,1)} %broadcast_in_dim.56), calls=%async_computation.3 | async-start | bytes 524288 | tf_op jit(solution)/shard_map/all_to_all | solution.py:18
Sparse Core Ops, SparseCore 0:
  101.1 36.6 reduce-scatter.2
  140.6 27.7 reduce-scatter.4
where the time goes:
time: 192 us; the launch traced here: 191 us
  waiting for transfers between devices  83.5 us (43%)
  starting transfers between devices  38.3 us (20%)
  matrix products  23.7 us (12%)
  local copies, waits for them, and re-layouts  23 us (12%)
  between operations  15.7 us (8%)
  other arithmetic  7.23 us (4%)
    reduce_scatter x2, waiting for transfers between devices, sum_by_axis(): x = lax.psum_scatter(x, axis, scatter_dimension=dim, tiled=True)  56.5 us
    all_to_all x2, waiting for transfers between devices, copy_for_each(): return lax.all_to_all(copies, axis, split_axis=0, concat_axis=0, tiled=True)  27 us
    all_to_all x2, starting transfers between devices, copy_for_each(): return lax.all_to_all(copies, axis, split_axis=0, concat_axis=0, tiled=True)  23.6 us
    mul x1, local copies, waits for them, and re-layouts, per_device(): jnp.einsum('wnz,wnx->wzx', tile_blocks, selected_block, preferred_element...  10.3 us
    ppermute x2, starting transfers between devices, passed_along(): return lax.ppermute(x, axis, [(i, (i + by) % count) for i in range(count)])  9.59 us
    dot_general x1, matrix products, per_device(): jnp.einsum('xn,xij->nij', row_onehot_mask, contribution, precision=lax.Pr...  6.37 us
    dot_general x1, matrix products, per_device(): jnp.einsum('wnz,wnx->wzx', tile_blocks, selected_block, preferred_element...  6.11 us
  transfers between devices with their start and end apart: 8, of which 4 were waited for; matrix products, arithmetic and copies ran while one was open for 4% of the time, Pallas kernels for 0%

commit v1 on v0

v1 whole, which is shorter than its diff:
```python
import jax
import jax.numpy as jnp
from jax import lax
from jax.experimental import pallas as pl
from jax.experimental.pallas import tpu as pltpu
from jax.sharding import Mesh
from jax.sharding import PartitionSpec as P

Z, YH = 8, 4
DOM = ("dom_0", "dom_1")
ALL = ("dom_0", "dom_1", "cluster")
f32 = jnp.float32
bf16 = jnp.bfloat16


def groups(clusters):
    at = lambda z, y, c: (z * YH + y) * clusters + c
    eights, fours = [], []
    for c in range(clusters):
        if c % 2 == 0:
            eights += [[at(z, y, c) for z in range(Z)] for y in range(YH)]
            fours += [[at(z, y, c) for y in range(YH)] for z in range(Z)]
        else:
            eights += [
                [at(2 * h + b, y, c) for b in range(2) for y in range(YH)] for h in range(Z // 2)
            ]
            fours += [
                [at(2 * h + b, y, c) for h in range(Z // 2)] for b in range(2) for y in range(YH)
            ]
    return eights, fours


def exchange(x, grouping):
    return lax.all_to_all(x, ALL, 0, 0, axis_index_groups=grouping, tiled=True)


def for_each(x, count):
    return jnp.broadcast_to(x, (count, *x.shape))


def passed_along(x, axis, by):
    count = lax.axis_size(axis)
    return lax.ppermute(x, axis, [(i, (i + by) % count) for i in range(count)])


def place_of(part, odd):
    z, y = part // YH, part % YH
    return jnp.where(odd == 1, (z % 2) * (Z // 2 * YH) + y * (Z // 2) + z // 2, part)


def before_kernel(
    src_ref, row_ref, count_ref, skip_ref, odd_ref, tiles_ref, feats_ref, stale_ref, lower_ref,
    upper_ref, base_ref, p_ref, pt_ref, ptn_ref, acc_ref,
):
    slots, blk, tr = tiles_ref.shape
    parts = skip_ref.shape[1]
    cached = parts * blk
    near = cached + 2 * blk
    total = near + cached
    acc_ref[...] = jnp.zeros_like(acc_ref)
    count = count_ref[0, 0]
    odd = odd_ref[0]

    def add_tile(t, carry):
        @pl.when(t < count)
        def _():
            s = src_ref[0, t]
            inside = jnp.minimum(s, parts - 1)
            sent = jnp.logical_and(s < parts, skip_ref[0, inside] != 1)
            block = jnp.where(sent, parts + 2 + place_of(inside, odd), s)
            rows = pl.ds(pl.multiple_of(block * blk, blk), blk)
            r = row_ref[0, t]
            acc_ref[r, rows, :] += tiles_ref[t].astype(f32)

        return carry

    lax.fori_loop(0, slots, add_tile, 0)
    near_rows = jnp.concatenate([lower_ref[...], upper_ref[...]], axis=0)
    for r in range(acc_ref.shape[0]):
        out = slice(r * tr, (r + 1) * tr)
        old = acc_ref[r, :cached, :].T.astype(bf16)
        beside = acc_ref[r, cached:near, :].astype(bf16)
        part = jnp.dot(old, stale_ref[...], preferred_element_type=f32)
        part += lax.dot_general(
            beside, near_rows, (((0,), (0,)), ((), ())), preferred_element_type=f32
        )
        base_ref[out, :] = feats_ref[out, :].astype(f32) + part
        new = acc_ref[r, near:total, :]
        p_ref[out, :] = new.T.astype(bf16)
        pt_ref[:, out] = new.astype(bf16)
        ptn_ref[:, out] = beside


def after_kernel(
    odd_ref, base_ref, p_ref, table_ref, weight_ref, cot_ref, pt_ref, ptn_ref,
    out_ref, dagg_ref, send_ref, near_ref, agg_ref, dz_ref,
):
    nodes, width = cot_ref.shape
    parts = send_ref.shape[0]
    blk = near_ref.shape[1]
    share = send_ref.shape[1] - blk
    step = 256
    for i in range(nodes // step):
        rows = slice(i * step, (i + 1) * step)
        agg = base_ref[rows, :] + jnp.dot(
            p_ref[rows, :], table_ref[...], preferred_element_type=f32
        )
        agg = agg.astype(bf16)
        agg_ref[rows, :] = agg
        z = jnp.dot(agg, weight_ref[...], preferred_element_type=f32)
        sig = jax.nn.sigmoid(z)
        out_ref[rows, :] = (z * sig).astype(bf16)
        slope = sig * (1.0 + z * (1.0 - sig))
        dz = (cot_ref[rows, :].astype(f32) * slope).astype(bf16)
        dz_ref[rows, :] = dz
        dagg_ref[rows, :] = lax.dot_general(
            dz, weight_ref[...], (((1,), (1,)), ((), ())), preferred_element_type=f32
        ).astype(bf16)
    odd = odd_ref[0]
    for i in range(width // 256):
        cols = slice(i * 256, (i + 1) * 256)
        gw = lax.dot_general(
            agg_ref[:, cols], dz_ref[...], (((0,), (0,)), ((), ())), preferred_element_type=f32
        ).astype(bf16)
        per = 256 // share
        for j in range(per):
            place = place_of(jnp.int32(i * per + j), odd)
            send_ref[place, blk:, :] = gw[j * share : (j + 1) * share, :]
    for i in range(parts * blk // step):
        rows = slice(i * step, (i + 1) * step)
        d = jnp.dot(pt_ref[rows, :], dagg_ref[...], preferred_element_type=f32).astype(bf16)
        per = step // blk
        send_ref[i * per : (i + 1) * per, :blk, :] = d.reshape(per, blk, width)
    d = jnp.dot(ptn_ref[...], dagg_ref[...], preferred_element_type=f32).astype(bf16)
    near_ref[...] = d.reshape(2, blk, width)


def per_device(
    features, stale, boundary, skip, tile_vals, tile_row, tile_src, tile_count, weight, cotangent
):
    feats = features[0]
    nodes, width = feats.shape
    parts = lax.axis_size(DOM)
    clusters = lax.axis_size("cluster")
    blk = stale.shape[1] // parts
    slots, _, tr = tile_vals.shape[1:]
    row_blocks = nodes // tr
    share = width // parts
    eights, fours = groups(clusters)
    odd = (lax.axis_index("cluster") % 2).astype(jnp.int32).reshape(1)
    start_row = boundary[0, 0] * blk
    own = lax.dynamic_slice_in_dim(feats, start_row, blk, 0)
    some = exchange(for_each(own, YH), fours).reshape(YH * blk, width)
    lower = passed_along(own, "cluster", 1)
    upper = passed_along(own, "cluster", -1)
    smem = pl.BlockSpec(memory_space=pltpu.SMEM)
    vmem = pl.BlockSpec(memory_space=pltpu.VMEM)
    base, p, pt, ptn = pl.pallas_call(
        before_kernel,
        out_shape=(
            jax.ShapeDtypeStruct((nodes, width), f32),
            jax.ShapeDtypeStruct((nodes, parts * blk), bf16),
            jax.ShapeDtypeStruct((parts * blk, nodes), bf16),
            jax.ShapeDtypeStruct((2 * blk, nodes), bf16),
        ),
        in_specs=[smem] * 5 + [vmem] * 5,
        out_specs=(vmem,) * 4,
        scratch_shapes=[pltpu.VMEM((row_blocks, (2 * parts + 2) * blk, tr), f32)],
        compiler_params=pltpu.CompilerParams(vmem_limit_bytes=24 << 20),
        cost_estimate=pl.CostEstimate(
            flops=2 * nodes * width * (parts + 2) * blk, bytes_accessed=8 << 20, transcendentals=0
        ),
        name="before",
    )(tile_src, tile_row, tile_count, skip, odd, tile_vals[0], feats, stale[0], lower, upper)
    table = exchange(for_each(some, Z), eights).reshape(parts * blk, width)
    out_features, dagg, send, near = pl.pallas_call(
        after_kernel,
        out_shape=(
            jax.ShapeDtypeStruct((nodes, width), bf16),
            jax.ShapeDtypeStruct((nodes, width), bf16),
            jax.ShapeDtypeStruct((parts, blk + share, width), bf16),
            jax.ShapeDtypeStruct((2, blk, width), bf16),
        ),
        in_specs=[smem] + [vmem] * 7,
        out_specs=(vmem,) * 4,
        scratch_shapes=[pltpu.VMEM((nodes, width), bf16), pltpu.VMEM((nodes, width), bf16)],
        compiler_params=pltpu.CompilerParams(vmem_limit_bytes=24 << 20),
        cost_estimate=pl.CostEstimate(
            flops=2 * nodes * width * (3 * width + 2 * (parts + 1) * blk),
            bytes_accessed=11 << 20,
            transcendentals=nodes * width,
        ),
        name="after",
    )(odd, base, p, table, weight, cotangent[0], pt, ptn)
    rows = blk + share
    got = exchange(send.reshape(Z, YH * rows, width), eights)
    from_upper = passed_along(near[0], "cluster", -1)
    from_lower = passed_along(near[1], "cluster", 1)
    some = got.astype(f32).sum(axis=0).astype(bf16)
    got = exchange(some.reshape(YH, rows, width), fours)
    mine = got.astype(f32).sum(axis=0)
    gw = lax.all_to_all(for_each(mine[blk:].astype(bf16), clusters), "cluster", 0, 0, tiled=True)
    grad_weight = gw.astype(f32).sum(axis=0)
    bgrad = mine[:blk] + from_upper.astype(f32) + from_lower.astype(f32)
    current = lax.dynamic_slice_in_dim(dagg, start_row, blk, 0).astype(f32)
    grad_features = lax.dynamic_update_slice_in_dim(
        dagg, (current + bgrad).astype(bf16), start_row, 0
    )
    return (out_features[None], grad_features[None], grad_weight)


def solution(mesh):
    finer = Mesh(mesh.devices.reshape(Z, YH, mesh.shape["cluster"]), ALL)
    placed = (
        P("cluster", DOM, None),
        P("cluster", None, None),
        P("cluster", DOM),
        P("cluster", None),
        P("cluster", DOM, None, None),
        P("cluster", DOM),
        P("cluster", DOM),
        P("cluster", DOM),
        P(),
        P("cluster", DOM, None),
    )
    return jax.shard_map(
        per_device,
        mesh=finer,
        in_specs=placed,
        out_specs=(P("cluster", DOM, None), P("cluster", DOM, None), P(DOM, None)),
        check_vma=False,
    )
```

time: 192 us -> 130 us (0.68)
  the two profiles are of different devices: /device:TPU:1 before, /device:TPU:128 now
where the time goes in v1:
time: 130 us
  blocking collectives  64.2 us (49%)
  starting transfers between devices  27.8 us (21%)
  local copies, waits for them, and re-layouts  14.1 us (11%)
  waiting for transfers between devices  12.5 us (10%)
  Pallas kernels  7.78 us (6%)
  between operations  2.12 us (2%)
    all_to_all x3, blocking collectives, exchange(): return lax.all_to_all(x, ALL, 0, 0, axis_index_groups=grouping, tiled=True)  64.2 us
    ppermute x4, waiting for transfers between devices, passed_along(): return lax.ppermute(x, axis, [(i, (i + by) % count) for i in range(count)])  12.5 us
    ppermute x4, starting transfers between devices, passed_along(): return lax.ppermute(x, axis, [(i, (i + by) % count) for i in range(count)])  11.9 us
    unnamed x35, local copies, waits for them, and re-layouts  11.5 us
    all_to_all x1, starting transfers between devices, exchange(): return lax.all_to_all(x, ALL, 0, 0, axis_index_groups=grouping, tiled=True)  9.06 us
    all_to_all x1, starting transfers between devices, per_device(): lax.all_to_all(for_each(mine[blk:].astype(bf16), clusters), 'cluster', 0,...  6.84 us
    pallas_call x1, Pallas kernels, per_device(): pl.pallas_call(after_kernel, out_shape=(jax.ShapeDtypeStruct((nodes, widt...  4.53 us
    pallas_call x1, Pallas kernels, per_device(): pl.pallas_call(before_kernel, out_shape=(jax.ShapeDtypeStruct((nodes, wid...  3.25 us
  transfers between devices with their start and end apart: 6, of which 2 were waited for; matrix products, arithmetic and copies ran while one was open for 0% of the time, Pallas kernels for 3%

profile of v1, /device:TPU:128, one launch (start us, length us, event | category | flops | bytes accessed | tf_op | source)
XLA Modules:
  0.0 129.5 jit_solution(13775899685926133601)
XLA Ops:
  1.3 0.8 dynamic-slice_bitcast_fusion
  2.1 15.6 %all_to_all.25 = bf16[4,32,512]{2,1,0:T(8,128)(2,1)S(1)} all-to-all(bf16[4,32,512]{2,1,0:T(8,128)(2,1)S(1)} %broadcast_in_dim.17), channel_id=1, replica_groups={{0,16,32,48},{64,80,96,112},{128,144,160,176},{192,208,224,240},{256,27..., dimensions={0} | all-to-all | bytes 262144 | tf_op jit(solution)/shard_map/all_to_all | solution.py:34
  17.7 0.0 copy-start
  17.7 0.0 copy-start.1
  17.7 0.0 copy-start.5
  17.7 0.0 copy-start.6
  17.7 0.0 copy-start.7
  17.7 1.1 broadcast_in_dim.18
  18.8 9.1 %all-to-all-start.1 = ((bf16[8,128,512]{2,1,0:T(8,128)(2,1)}), bf16[8,128,512]{2,1,0:T(8,128)(2,1)S(1)}, u32[]{:S(2)}, u32[]{:S(2)}) async-start(bf16[8,128,512]{2,1,0:T(8,128)(2,1)} %broadcast_in_dim.18), calls=%async_computation.1 | async-start | bytes 2097152 | tf_op jit(solution)/shard_map/all_to_all | solution.py:34
  27.9 1.9 %collective-permute-start.1 = (bf16[32,512]{1,0:T(8,128)(2,1)S(1)}, bf16[32,512]{1,0:T(8,128)(2,1)S(1)}, u32[]{:S(2)}, u32[]{:S(2)}) collective-permute-start(bf16[32,512]{1,0:T(8,128)(2,1)S(1)} %dynamic-slice_bitcast_fusion), channel_id=1, source_target_pairs={{0,15},{1,0},{2,1},{3,2},{4,3},{5,4},{6,5},{7,6},{8,7},{9,8},{10,9... | collective-permute-start | bytes 98312 | tf_op jit(solution)/shard_map/ppermute | solution.py:43
  29.8 2.4 %collective-permute-start = (bf16[32,512]{1,0:T(8,128)(2,1)S(1)}, bf16[32,512]{1,0:T(8,128)(2,1)S(1)}, u32[]{:S(2)}, u32[]{:S(2)}) collective-permute-start(bf16[32,512]{1,0:T(8,128)(2,1)S(1)} %dynamic-slice_bitcast_fusion), channel_id=1, source_target_pairs={{0,1},{1,2},{2,3},{3,4},{4,5},{5,6},{6,7},{7,8},{8,9},{9,10},{10,1... | collective-permute-start | bytes 98312 | tf_op jit(solution)/shard_map/ppermute | solution.py:43
  32.9 0.0 collective-permute-done.1.upper_ref
  32.9 7.1 %collective-permute-done.lower_ref = bf16[32,512]{1,0:T(8,128)(2,1)S(1)} collective-permute-done((bf16[32,512]{1,0:T(8,128)(2,1)S(1)}, bf16[32,512]{1,0:T(8,128)(2,1)S(1)}, u32[]{:S(2)}, u32[]{:S(2)}) %collective-permute-start) | collective-permute-done | bytes 32800 | tf_op jit(solution)/shard_map/ppermute | solution.py:43
  40.0 0.0 copy-done
  40.0 0.0 copy-done.1
  40.0 0.0 copy-done.5
  40.0 0.0 copy-done.6
  40.0 0.0 copy-done.7
  40.0 0.0 copy-start.4
  40.0 0.9 copy-done.4
  41.0 3.3 %before.1 = (f32[768,512]{1,0:T(8,128)S(1)}, bf16[768,1024]{1,0:T(8,128)(2,1)S(1)}, bf16[1024,768]{1,0:T(8,128)(2,1)S(1)}, bf16[64,768]{1,0:T(8,128)(2,1)S(1)}) custom-call(s32[1,32]{1,0:T(1,128)S(1)} %copy-done.5, s32[1,32]{1,0:T(1,128)S(1)} %copy-done.6, s32[1,1]{1,0:T(1,128)S(6)} %copy.15.count_ref, s32[1,32]{1,0:T(1,128)S(1)} %copy-done.7, ...), custom_call_target="tpu_custom_call" | custom-call | flops 855638016 | bytes 8388608 | tf_op jit(solution)/shard_map/before/pallas_call | solution.py:158
  44.2 0.0 copy-start.8
  44.3 1.2 copy-done.8
  45.4 1.1 copy-done.10
  46.6 1.2 copy-done.12
  47.7 0.6 copy-done.14
  48.4 0.0 all-to-all-done.1
  48.4 0.0 copy-done.3
  48.4 1.1 copy-done.2
  49.5 1.4 %copy-done.9 = f32[768,512]{1,0:T(8,128)S(1)} copy-done((f32[768,512]{1,0:T(8,128)S(1)}, f32[768,512]{1,0:T(8,128)}, u32[]{:S(2)}) %copy-start.9) | copy-done | bytes 1572888
  50.9 1.4 %copy-done.11 = bf16[768,1024]{1,0:T(8,128)(2,1)S(1)} copy-done((bf16[768,1024]{1,0:T(8,128)(2,1)S(1)}, bf16[768,1024]{1,0:T(8,128)(2,1)}, u32[]{:S(2)}) %copy-start.11) | copy-done | bytes 1572888
  52.3 1.4 %copy-done.13 = bf16[1024,768]{1,0:T(8,128)(2,1)S(1)} copy-done((bf16[1024,768]{1,0:T(8,128)(2,1)S(1)}, bf16[1024,768]{1,0:T(8,128)(2,1)}, u32[]{:S(2)}) %copy-start.13) | copy-done | bytes 1572888
  53.7 0.9 copy-done.15
  54.6 4.5 %after.1 = (bf16[768,512]{1,0:T(8,128)(2,1)}, bf16[768,512]{1,0:T(8,128)(2,1)S(1)}, bf16[32,48,512]{2,1,0:T(8,128)(2,1)S(1)}, bf16[2,32,512]{2,1,0:T(8,128)(2,1)S(1)}) custom-call(s32[1]{0:T(128)} %bitcast.odd_ref, f32[768,512]{1,0:T(8,128)S(1)} %copy-done.9, bf16[768,1024]{1,0:T(8,128)(2,1)S(1)} %copy-done.11, bf16[1024,512]{1,0:T(8,128)(2,1)S(1)} %bitcast.23, ...), custom_call_target="tpu_custom_call" | custom-call | flops 2868903936 | bytes 11534336 | tf_op jit(solution)/shard_map/after/pallas_call | solution.py:176
  59.1 33.7 %all_to_all.26 = bf16[8,192,512]{2,1,0:T(8,128)(2,1)S(1)} all-to-all(bf16[8,192,512]{2,1,0:T(8,128)(2,1)S(1)} %bitcast.22), channel_id=1, replica_groups={{0,64,128,192,256,320,384,448},{16,80,144,208,272,336,400,464},{32,96,1..., dimensions={0} | all-to-all | bytes 3145728 | tf_op jit(solution)/shard_map/all_to_all | solution.py:34
  92.9 0.3 reduce_sum.30
  93.2 14.8 %all_to_all.27 = bf16[4,48,512]{2,1,0:T(8,128)(2,1)S(1)} all-to-all(bf16[4,48,512]{2,1,0:T(8,128)(2,1)S(1)} %bitcast.29), channel_id=1, replica_groups={{0,16,32,48},{64,80,96,112},{128,144,160,176},{192,208,224,240},{256,27..., dimensions={0} | all-to-all | bytes 393216 | tf_op jit(solution)/shard_map/all_to_all | solution.py:34
  108.0 0.7 broadcast_in_dim.22
  108.7 6.8 %all-to-all-start.4 = ((bf16[16,16,512]{2,1,0:T(8,128)(2,1)}), bf16[16,16,512]{2,1,0:T(8,128)(2,1)S(1)}, u32[]{:S(2)}, u32[]{:S(2)}) async-start(bf16[16,16,512]{2,1,0:T(8,128)(2,1)} %broadcast_in_dim.22), calls=%async_computation.4 | async-start | bytes 524288 | tf_op jit(solution)/shard_map/all_to_all | solution.py:202
  115.6 5.7 %collective-permute-start.2 = (bf16[32,512]{1,0:T(8,128)(2,1)S(1)}, bf16[32,512]{1,0:T(8,128)(2,1)S(1)}, u32[]{:S(2)}, u32[]{:S(2)}) collective-permute-start(bf16[32,512]{1,0:T(8,128)(2,1)S(1)} %get-tuple-element.19), channel_id=1, source_target_pairs={{0,15},{1,0},{2,1},{3,2},{4,3},{5,4},{6,5},{7,6},{8,7},{9,8},{10,9... | collective-permute-start | bytes 98312 | tf_op jit(solution)/shard_map/ppermute | solution.py:43
  121.3 1.9 %collective-permute-start.3 = (bf16[32,512]{1,0:T(8,128)(2,1)S(1)}, bf16[32,512]{1,0:T(8,128)(2,1)S(1)}, u32[]{:S(2)}, u32[]{:S(2)}) collective-permute-start(bf16[32,512]{1,0:T(8,128)(2,1)S(1)} %get-tuple-element.20), channel_id=1, source_target_pairs={{0,1},{1,2},{2,3},{3,4},{4,5},{5,6},{6,7},{7,8},{8,9},{9,10},{10,1... | collective-permute-start | bytes 98312 | tf_op jit(solution)/shard_map/ppermute | solution.py:43
  123.2 0.1 copy.13
  123.2 0.0 collective-permute-done.2
  123.3 5.3 %collective-permute-done.3 = bf16[32,512]{1,0:T(8,128)(2,1)S(1)} collective-permute-done((bf16[32,512]{1,0:T(8,128)(2,1)S(1)}, bf16[32,512]{1,0:T(8,128)(2,1)S(1)}, u32[]{:S(2)}, u32[]{:S(2)}) %collective-permute-start.3) | collective-permute-done | bytes 32800 | tf_op jit(solution)/shard_map/ppermute | solution.py:43
  128.6 0.0 copy-start.16
  128.6 0.0 all-to-all-done.4
  128.6 0.8 convert_reduce_fusion
  129.4 0.1 copy-done.16
  (14 shorter events, 0.1 us)
Async XLA Ops:
  17.7 22.3 %copy-start = (bf16[1,768,512]{2,1,0:T(8,128)(2,1)S(1)}, bf16[1,768,512]{2,1,0:T(8,128)(2,1)}, u32[]{:S(2)}) copy-start(bf16[1,768,512]{2,1,0:T(8,128)(2,1)} %param.10) | copy-start | bytes 2359300
  17.7 22.3 %copy-start.1 = (bf16[1,1024,512]{2,1,0:T(8,128)(2,1)S(1)}, bf16[1,1024,512]{2,1,0:T(8,128)(2,1)}, u32[]{:S(2)}) copy-start(bf16[1,1024,512]{2,1,0:T(8,128)(2,1)} %param.11) | copy-start | bytes 3145732
  17.7 22.3 %copy-start.5 = (s32[1,32]{1,0:T(1,128)S(1)}, s32[1,32]{1,0:T(1,128)}, u32[]{:S(2)}) copy-start(s32[1,32]{1,0:T(1,128)} %src_ref.1) | copy-start | bytes 388
  17.7 22.3 %copy-start.6 = (s32[1,32]{1,0:T(1,128)S(1)}, s32[1,32]{1,0:T(1,128)}, u32[]{:S(2)}) copy-start(s32[1,32]{1,0:T(1,128)} %row_ref.1) | copy-start | bytes 388
  17.7 22.3 %copy-start.7 = (s32[1,32]{1,0:T(1,128)S(1)}, s32[1,32]{1,0:T(1,128)}, u32[]{:S(2)}) copy-start(s32[1,32]{1,0:T(1,128)} %skip_ref.1) | copy-start | bytes 388
  18.8 29.6 %all-to-all-start.1 = ((bf16[8,128,512]{2,1,0:T(8,128)(2,1)}), bf16[8,128,512]{2,1,0:T(8,128)(2,1)S(1)}, u32[]{:S(2)}, u32[]{:S(2)}) async-start(bf16[8,128,512]{2,1,0:T(8,128)(2,1)} %broadcast_in_dim.18), calls=%async_computation.1 | async-start | bytes 2097152 | tf_op jit(solution)/shard_map/all_to_all | solution.py:34
  27.9 5.0 %collective-permute-start.1 = (bf16[32,512]{1,0:T(8,128)(2,1)S(1)}, bf16[32,512]{1,0:T(8,128)(2,1)S(1)}, u32[]{:S(2)}, u32[]{:S(2)}) collective-permute-start(bf16[32,512]{1,0:T(8,128)(2,1)S(1)} %dynamic-slice_bitcast_fusion), channel_id=1, source_target_pairs={{0,15},{1,0},{2,1},{3,2},{4,3},{5,4},{6,5},{7,6},{8,7},{9,8},{10,9... | collective-permute-start | bytes 98312 | tf_op jit(solution)/shard_map/ppermute | solution.py:43
  29.8 10.2 %collective-permute-start = (bf16[32,512]{1,0:T(8,128)(2,1)S(1)}, bf16[32,512]{1,0:T(8,128)(2,1)S(1)}, u32[]{:S(2)}, u32[]{:S(2)}) collective-permute-start(bf16[32,512]{1,0:T(8,128)(2,1)S(1)} %dynamic-slice_bitcast_fusion), channel_id=1, source_target_pairs={{0,1},{1,2},{2,3},{3,4},{4,5},{5,6},{6,7},{7,8},{8,9},{9,10},{10,1... | collective-permute-start | bytes 98312 | tf_op jit(solution)/shard_map/ppermute | solution.py:43
  40.0 1.0 copy-start.4
  41.0 7.4 %copy-start.3 = (bf16[512,512]{1,0:T(8,128)(2,1)S(1)}, bf16[512,512]{1,0:T(8,128)(2,1)}, u32[]{:S(2)}) copy-start(bf16[512,512]{1,0:T(8,128)(2,1)} %weight_ref.1) | copy-start | bytes 1572868
  44.2 1.2 copy-start.8
  45.4 1.1 copy-start.10
  46.6 1.2 copy-start.12
  47.7 0.6 copy-start.14
  48.4 1.1 copy-start.2
  49.5 1.4 %copy-start.9 = (f32[768,512]{1,0:T(8,128)S(1)}, f32[768,512]{1,0:T(8,128)}, u32[]{:S(2)}) copy-start(f32[768,512]{1,0:T(8,128)} %copy-done.8) | copy-start | bytes 4718596
  50.9 1.4 %copy-start.11 = (bf16[768,1024]{1,0:T(8,128)(2,1)S(1)}, bf16[768,1024]{1,0:T(8,128)(2,1)}, u32[]{:S(2)}) copy-start(bf16[768,1024]{1,0:T(8,128)(2,1)} %copy-done.10) | copy-start | bytes 4718596
  52.3 1.4 %copy-start.13 = (bf16[1024,768]{1,0:T(8,128)(2,1)S(1)}, bf16[1024,768]{1,0:T(8,128)(2,1)}, u32[]{:S(2)}) copy-start(bf16[1024,768]{1,0:T(8,128)(2,1)} %copy-done.12) | copy-start | bytes 4718596
  53.7 0.9 copy-start.15
  108.7 20.0 %all-to-all-start.4 = ((bf16[16,16,512]{2,1,0:T(8,128)(2,1)}), bf16[16,16,512]{2,1,0:T(8,128)(2,1)S(1)}, u32[]{:S(2)}, u32[]{:S(2)}) async-start(bf16[16,16,512]{2,1,0:T(8,128)(2,1)} %broadcast_in_dim.22), calls=%async_computation.4 | async-start | bytes 524288 | tf_op jit(solution)/shard_map/all_to_all | solution.py:202
  115.6 7.7 %collective-permute-start.2 = (bf16[32,512]{1,0:T(8,128)(2,1)S(1)}, bf16[32,512]{1,0:T(8,128)(2,1)S(1)}, u32[]{:S(2)}, u32[]{:S(2)}) collective-permute-start(bf16[32,512]{1,0:T(8,128)(2,1)S(1)} %get-tuple-element.19), channel_id=1, source_target_pairs={{0,15},{1,0},{2,1},{3,2},{4,3},{5,4},{6,5},{7,6},{8,7},{9,8},{10,9... | collective-permute-start | bytes 98312 | tf_op jit(solution)/shard_map/ppermute | solution.py:43
  121.3 7.3 %collective-permute-start.3 = (bf16[32,512]{1,0:T(8,128)(2,1)S(1)}, bf16[32,512]{1,0:T(8,128)(2,1)S(1)}, u32[]{:S(2)}, u32[]{:S(2)}) collective-permute-start(bf16[32,512]{1,0:T(8,128)(2,1)S(1)} %get-tuple-element.20), channel_id=1, source_target_pairs={{0,1},{1,2},{2,3},{3,4},{4,5},{5,6},{6,7},{7,8},{8,9},{9,10},{10,1... | collective-permute-start | bytes 98312 | tf_op jit(solution)/shard_map/ppermute | solution.py:43
  128.6 0.9 copy-start.16

commit v2 on v1

--- a/solution.py
+++ b/solution.py
@@ -49,14 +49,13 @@
 
 
 def before_kernel(
-    src_ref, row_ref, count_ref, skip_ref, odd_ref, tiles_ref, feats_ref, stale_ref, lower_ref,
-    upper_ref, base_ref, p_ref, pt_ref, ptn_ref, acc_ref,
+    src_ref, row_ref, count_ref, skip_ref, odd_ref, tiles_ref, feats_ref, stale_ref,
+    base_ref, p_ref, pt_ref, ptn_ref, pn_ref, acc_ref,
 ):
     slots, blk, tr = tiles_ref.shape
     parts = skip_ref.shape[1]
     cached = parts * blk
     near = cached + 2 * blk
-    total = near + cached
     acc_ref[...] = jnp.zeros_like(acc_ref)
     count = count_ref[0, 0]
     odd = odd_ref[0]
@@ -75,64 +74,95 @@
         return carry
 
     lax.fori_loop(0, slots, add_tile, 0)
-    near_rows = jnp.concatenate([lower_ref[...], upper_ref[...]], axis=0)
     for r in range(acc_ref.shape[0]):
         out = slice(r * tr, (r + 1) * tr)
         old = acc_ref[r, :cached, :].T.astype(bf16)
-        beside = acc_ref[r, cached:near, :].astype(bf16)
-        part = jnp.dot(old, stale_ref[...], preferred_element_type=f32)
-        part += lax.dot_general(
-            beside, near_rows, (((0,), (0,)), ((), ())), preferred_element_type=f32
+        base_ref[out, :] = feats_ref[out, :].astype(f32) + jnp.dot(
+            old, stale_ref[...], preferred_element_type=f32
         )
-        base_ref[out, :] = feats_ref[out, :].astype(f32) + part
-        new = acc_ref[r, near:total, :]
+        beside = acc_ref[r, cached:near, :]
+        pn_ref[out, :] = beside.T.astype(bf16)
+        ptn_ref[:, out] = beside.astype(bf16)
+        new = acc_ref[r, near:, :]
         p_ref[out, :] = new.T.astype(bf16)
         pt_ref[:, out] = new.astype(bf16)
-        ptn_ref[:, out] = beside
 
 
 def after_kernel(
-    odd_ref, base_ref, p_ref, table_ref, weight_ref, cot_ref, pt_ref, ptn_ref,
-    out_ref, dagg_ref, send_ref, near_ref, agg_ref, dz_ref,
+    odd_ref, base_hbm, p_hbm, cot_hbm, weight_hbm, ptn_hbm, pt_hbm, pn_ref, table_ref, lower_ref,
+    upper_ref, out_hbm, dagg_ref, send_ref, near_ref,
+    base_ref, p_ref, cot_ref, weight_ref, ptn_ref, pt_ref, out_ref, agg_ref, dz_ref, sems, out_sems,
 ):
     nodes, width = cot_ref.shape
     parts = send_ref.shape[0]
     blk = near_ref.shape[1]
     share = send_ref.shape[1] - blk
     step = 256
-    for i in range(nodes // step):
-        rows = slice(i * step, (i + 1) * step)
-        agg = base_ref[rows, :] + jnp.dot(
-            p_ref[rows, :], table_ref[...], preferred_element_type=f32
-        )
-        agg = agg.astype(bf16)
+    steps = nodes // step
+    chunk = lambda i: slice(i * step, (i + 1) * step)
+
+    def fetch(source, target, rows, sem):
+        copy = pltpu.make_async_copy(source.at[rows, :], target.at[rows, :], sems.at[sem])
+        copy.start()
+        return copy
+
+    whole = slice(None)
+    arriving = []
+    for i in range(steps):
+        rows = chunk(i)
+        ahead = [fetch(p_hbm, p_ref, rows, 3 * i), fetch(base_hbm, base_ref, rows, 3 * i + 1)]
+        if i == 0:
+            of_weight = fetch(weight_hbm, weight_ref, whole, 3 * steps)
+        ahead.append(fetch(cot_hbm, cot_ref, rows, 3 * i + 2))
+        arriving.append(ahead)
+    late = [
+        fetch(ptn_hbm, ptn_ref, whole, 3 * steps + 1), fetch(pt_hbm, pt_ref, whole, 3 * steps + 2)
+    ]
+    near_rows = jnp.concatenate([lower_ref[...], upper_ref[...]], axis=0)
+    leaving = []
+    for i in range(steps):
+        rows = chunk(i)
+        of_p, of_base, of_cot = arriving[i]
+        of_p.wait()
+        new = jnp.dot(p_ref[rows, :], table_ref[...], preferred_element_type=f32)
+        new += jnp.dot(pn_ref[rows, :], near_rows, preferred_element_type=f32)
+        of_base.wait()
+        agg = (base_ref[rows, :] + new).astype(bf16)
         agg_ref[rows, :] = agg
+        if i == 0:
+            of_weight.wait()
         z = jnp.dot(agg, weight_ref[...], preferred_element_type=f32)
         sig = jax.nn.sigmoid(z)
         out_ref[rows, :] = (z * sig).astype(bf16)
+        copy = pltpu.make_async_copy(out_ref.at[rows, :], out_hbm.at[rows, :], out_sems.at[i])
+        copy.start()
+        leaving.append(copy)
         slope = sig * (1.0 + z * (1.0 - sig))
+        of_cot.wait()
         dz = (cot_ref[rows, :].astype(f32) * slope).astype(bf16)
         dz_ref[rows, :] = dz
         dagg_ref[rows, :] = lax.dot_general(
             dz, weight_ref[...], (((1,), (1,)), ((), ())), preferred_element_type=f32
         ).astype(bf16)
     odd = odd_ref[0]
-    for i in range(width // 256):
-        cols = slice(i * 256, (i + 1) * 256)
+    for i in range(width // step):
         gw = lax.dot_general(
-            agg_ref[:, cols], dz_ref[...], (((0,), (0,)), ((), ())), preferred_element_type=f32
+            agg_ref[:, chunk(i)], dz_ref[...], (((0,), (0,)), ((), ())), preferred_element_type=f32
         ).astype(bf16)
-        per = 256 // share
+        per = step // share
         for j in range(per):
             place = place_of(jnp.int32(i * per + j), odd)
             send_ref[place, blk:, :] = gw[j * share : (j + 1) * share, :]
+    for copy in late:
+        copy.wait()
     for i in range(parts * blk // step):
-        rows = slice(i * step, (i + 1) * step)
-        d = jnp.dot(pt_ref[rows, :], dagg_ref[...], preferred_element_type=f32).astype(bf16)
+        d = jnp.dot(pt_ref[chunk(i), :], dagg_ref[...], preferred_element_type=f32).astype(bf16)
         per = step // blk
         send_ref[i * per : (i + 1) * per, :blk, :] = d.reshape(per, blk, width)
     d = jnp.dot(ptn_ref[...], dagg_ref[...], preferred_element_type=f32).astype(bf16)
     near_ref[...] = d.reshape(2, blk, width)
+    for copy in leaving:
+        copy.wait()
 
 
 def per_device(
@@ -155,23 +185,25 @@
     upper = passed_along(own, "cluster", -1)
     smem = pl.BlockSpec(memory_space=pltpu.SMEM)
     vmem = pl.BlockSpec(memory_space=pltpu.VMEM)
-    base, p, pt, ptn = pl.pallas_call(
+    hbm = pl.BlockSpec(memory_space=pltpu.HBM)
+    base, p, pt, ptn, pn = pl.pallas_call(
         before_kernel,
         out_shape=(
             jax.ShapeDtypeStruct((nodes, width), f32),
             jax.ShapeDtypeStruct((nodes, parts * blk), bf16),
             jax.ShapeDtypeStruct((parts * blk, nodes), bf16),
             jax.ShapeDtypeStruct((2 * blk, nodes), bf16),
-        ),
-        in_specs=[smem] * 5 + [vmem] * 5,
-        out_specs=(vmem,) * 4,
+            jax.ShapeDtypeStruct((nodes, 2 * blk), bf16),
+        ),
+        in_specs=[smem] * 5 + [vmem] * 3,
+        out_specs=(vmem,) * 5,
         scratch_shapes=[pltpu.VMEM((row_blocks, (2 * parts + 2) * blk, tr), f32)],
-        compiler_params=pltpu.CompilerParams(vmem_limit_bytes=24 << 20),
+        compiler_params=pltpu.CompilerParams(vmem_limit_bytes=60 << 20),
         cost_estimate=pl.CostEstimate(
-            flops=2 * nodes * width * (parts + 2) * blk, bytes_accessed=8 << 20, transcendentals=0
+            flops=2 * nodes * width * parts * blk, bytes_accessed=8 << 20, transcendentals=0
         ),
         name="before",
-    )(tile_src, tile_row, tile_count, skip, odd, tile_vals[0], feats, stale[0], lower, upper)
+    )(tile_src, tile_row, tile_count, skip, odd, tile_vals[0], feats, stale[0])
     table = exchange(for_each(some, Z), eights).reshape(parts * blk, width)
     out_features, dagg, send, near = pl.pallas_call(
         after_kernel,
@@ -181,22 +213,35 @@
             jax.ShapeDtypeStruct((parts, blk + share, width), bf16),
             jax.ShapeDtypeStruct((2, blk, width), bf16),
         ),
-        in_specs=[smem] + [vmem] * 7,
-        out_specs=(vmem,) * 4,
-        scratch_shapes=[pltpu.VMEM((nodes, width), bf16), pltpu.VMEM((nodes, width), bf16)],
-        compiler_params=pltpu.CompilerParams(vmem_limit_bytes=24 << 20),
+        in_specs=[smem] + [hbm] * 6 + [vmem] * 4,
+        out_specs=(hbm, vmem, vmem, vmem),
+        scratch_shapes=[
+            pltpu.VMEM((nodes, width), f32),
+            pltpu.VMEM((nodes, parts * blk), bf16),
+            pltpu.VMEM((nodes, width), bf16),
+            pltpu.VMEM((width, width), bf16),
+            pltpu.VMEM((2 * blk, nodes), bf16),
+            pltpu.VMEM((parts * blk, nodes), bf16),
+            pltpu.VMEM((nodes, width), bf16),
+            pltpu.VMEM((nodes, width), bf16),
+            pltpu.VMEM((nodes, width), bf16),
+            pltpu.SemaphoreType.DMA((nodes // 256 * 3 + 3,)),
+            pltpu.SemaphoreType.DMA((nodes // 256,)),
+        ],
+        compiler_params=pltpu.CompilerParams(vmem_limit_bytes=48 << 20),
         cost_estimate=pl.CostEstimate(
             flops=2 * nodes * width * (3 * width + 2 * (parts + 1) * blk),
             bytes_accessed=11 << 20,
             transcendentals=nodes * width,
         ),
         name="after",
-    )(odd, base, p, table, weight, cotangent[0], pt, ptn)
+    )(odd, base, p, cotangent[0], weight, ptn, pt, pn, table, lower, upper)
     rows = blk + share
     got = exchange(send.reshape(Z, YH * rows, width), eights)
     from_upper = passed_along(near[0], "cluster", -1)
     from_lower = passed_along(near[1], "cluster", 1)
     some = got.astype(f32).sum(axis=0).astype(bf16)
+    some, from_upper, from_lower = lax.optimization_barrier((some, from_upper, from_lower))
     got = exchange(some.reshape(YH, rows, width), fours)
     mine = got.astype(f32).sum(axis=0)
     gw = lax.all_to_all(for_each(mine[blk:].astype(bf16), clusters), "cluster", 0, 0, tiled=True)

time: 130 us -> 124 us (0.954)
  the two profiles are of different devices: /device:TPU:128 before, /device:TPU:1 now
where the time goes in v2:
time: 124 us; the launch traced here: 123 us
  starting transfers between devices  47.9 us (39%)
  blocking collectives  31.6 us (25%)
  waiting for transfers between devices  22.5 us (18%)
  Pallas kernels  13.5 us (11%)
  local copies, waits for them, and re-layouts  4.51 us (4%)
  between operations  2.07 us (2%)
    all_to_all x2, blocking collectives, exchange(): return lax.all_to_all(x, ALL, 0, 0, axis_index_groups=grouping, tiled=True)  31.6 us
    all_to_all x1, starting transfers between devices, per_device(): lax.all_to_all(for_each(mine[blk:].astype(bf16), clusters), 'cluster', 0,...  19.6 us
    ppermute x4, starting transfers between devices, passed_along(): return lax.ppermute(x, axis, [(i, (i + by) % count) for i in range(count)])  17.3 us
    all_to_all x2, waiting for transfers between devices, exchange(): return lax.all_to_all(x, ALL, 0, 0, axis_index_groups=grouping, tiled=True)  15.4 us
    all_to_all x2, starting transfers between devices, exchange(): return lax.all_to_all(x, ALL, 0, 0, axis_index_groups=grouping, tiled=True)  11 us
    pallas_call x1, Pallas kernels, per_device(): pl.pallas_call(after_kernel, out_shape=(jax.ShapeDtypeStruct((nodes, widt...  7.52 us
    all_to_all x1, waiting for transfers between devices, per_device(): lax.all_to_all(for_each(mine[blk:].astype(bf16), clusters), 'cluster', 0,...  7.07 us
    pallas_call x1, Pallas kernels, per_device(): pl.pallas_call(before_kernel, out_shape=(jax.ShapeDtypeStruct((nodes, wid...  6.02 us
  transfers between devices with their start and end apart: 7, of which 3 were waited for; matrix products, arithmetic and copies ran while one was open for 0% of the time, Pallas kernels for 5%

profile of v2, /device:TPU:1, one launch (start us, length us, event | category | flops | bytes accessed | tf_op | source)
XLA Modules:
  0.0 123.1 jit_solution(10347513857153633009)
XLA Ops:
  1.3 0.8 dynamic-slice_bitcast_fusion
  2.1 18.2 %all_to_all.25 = bf16[4,32,512]{2,1,0:T(8,128)(2,1)S(1)} all-to-all(bf16[4,32,512]{2,1,0:T(8,128)(2,1)S(1)} %broadcast_in_dim.17), channel_id=1, replica_groups={{0,16,32,48},{64,80,96,112},{128,144,160,176},{192,208,224,240},{256,27..., dimensions={0} | all-to-all | bytes 262144 | tf_op jit(solution)/shard_map/all_to_all | solution.py:34
  20.3 1.1 broadcast_in_dim.18
  21.4 7.4 %all-to-all-start.1 = ((bf16[8,128,512]{2,1,0:T(8,128)(2,1)}), bf16[8,128,512]{2,1,0:T(8,128)(2,1)S(1)}, u32[]{:S(2)}, u32[]{:S(2)}) async-start(bf16[8,128,512]{2,1,0:T(8,128)(2,1)} %broadcast_in_dim.18), calls=%async_computation.1 | async-start | bytes 2097152 | tf_op jit(solution)/shard_map/all_to_all | solution.py:34
  28.8 0.0 copy-start
  28.8 0.0 copy-start.1
  28.8 3.9 %collective-permute-start.1 = (bf16[32,512]{1,0:T(8,128)(2,1)S(1)}, bf16[32,512]{1,0:T(8,128)(2,1)S(1)}, u32[]{:S(2)}, u32[]{:S(2)}) collective-permute-start(bf16[32,512]{1,0:T(8,128)(2,1)S(1)} %dynamic-slice_bitcast_fusion), channel_id=1, source_target_pairs={{0,15},{1,0},{2,1},{3,2},{4,3},{5,4},{6,5},{7,6},{8,7},{9,8},{10,9... | collective-permute-start | bytes 98312 | tf_op jit(solution)/shard_map/ppermute | solution.py:43
  32.7 2.5 %collective-permute-start = (bf16[32,512]{1,0:T(8,128)(2,1)S(1)}, bf16[32,512]{1,0:T(8,128)(2,1)S(1)}, u32[]{:S(2)}, u32[]{:S(2)}) collective-permute-start(bf16[32,512]{1,0:T(8,128)(2,1)S(1)} %dynamic-slice_bitcast_fusion), channel_id=1, source_target_pairs={{0,1},{1,2},{2,3},{3,4},{4,5},{5,6},{6,7},{7,8},{8,9},{9,10},{10,1... | collective-permute-start | bytes 98312 | tf_op jit(solution)/shard_map/ppermute | solution.py:43
  35.8 6.0 %before.1 = (f32[768,512]{1,0:T(8,128)}, bf16[768,1024]{1,0:T(8,128)(2,1)}, bf16[1024,768]{1,0:T(8,128)(2,1)}, bf16[64,768]{1,0:T(8,128)(2,1)}, bf16[768,64]{1,0:T(8,128)(2,1)}) custom-call(s32[1,32]{1,0:T(1,128)} %src_ref.1, s32[1,32]{1,0:T(1,128)} %row_ref.1, s32[1,1]{1,0:T(1,128)S(6)} %copy.15.count_ref, s32[1,32]{1,0:T(1,128)} %skip_ref.1, ...), custom_call_target="tpu_custom_call" | custom-call | flops 805306368 | bytes 8388608 | tf_op jit(solution)/shard_map/before/pallas_call | solution.py:189
  41.8 0.0 collective-permute-done.1.upper_ref
  41.8 0.0 collective-permute-done.lower_ref
  41.8 4.8 %all-to-all-done.1 = bf16[8,128,512]{2,1,0:T(8,128)(2,1)S(1)} async-done(((bf16[8,128,512]{2,1,0:T(8,128)(2,1)}), bf16[8,128,512]{2,1,0:T(8,128)(2,1)S(1)}, u32[]{:S(2)}, u32[]{:S(2)}) %all-to-all-start.1) | async-done | bytes 1048608 | tf_op jit(solution)/shard_map/all_to_all | solution.py:34
  46.6 0.0 copy-done
  46.6 0.0 copy-done.1
  46.6 0.0 copy-start.2
  46.6 0.9 copy-done.2
  47.5 0.0 copy-start.3
  47.5 0.9 copy-done.3
  48.4 7.5 %after.1 = (bf16[768,512]{1,0:T(8,128)(2,1)}, bf16[768,512]{1,0:T(8,128)(2,1)S(1)}, bf16[32,48,512]{2,1,0:T(8,128)(2,1)}, bf16[2,32,512]{2,1,0:T(8,128)(2,1)S(1)}) custom-call(s32[1]{0:T(128)} %bitcast.odd_ref, f32[768,512]{1,0:T(8,128)} %get-tuple-element.15.base_hbm, bf16[768,1024]{1,0:T(8,128)(2,1)} %get-tuple-element.16.p_hbm, ...), custom_call_target="tpu_custom_call" | custom-call | flops 2868903936 | bytes 11534336 | tf_op jit(solution)/shard_map/after/pallas_call | solution.py:208
  55.9 3.6 %all-to-all-start.2 = ((bf16[8,192,512]{2,1,0:T(8,128)(2,1)}), bf16[8,192,512]{2,1,0:T(8,128)(2,1)S(1)}, u32[]{:S(2)}, u32[]{:S(2)}) async-start(bf16[8,192,512]{2,1,0:T(8,128)(2,1)} %bitcast.11), calls=%async_computation.2 | async-start | bytes 3145728 | tf_op jit(solution)/shard_map/all_to_all | solution.py:34
  59.6 7.8 %collective-permute-start.3 = (bf16[32,512]{1,0:T(8,128)(2,1)S(1)}, bf16[32,512]{1,0:T(8,128)(2,1)S(1)}, u32[]{:S(2)}, u32[]{:S(2)}) collective-permute-start(bf16[32,512]{1,0:T(8,128)(2,1)S(1)} %get-tuple-element.27), channel_id=1, source_target_pairs={{0,1},{1,2},{2,3},{3,4},{4,5},{5,6},{6,7},{7,8},{8,9},{9,10},{10,1... | collective-permute-start | bytes 98312 | tf_op jit(solution)/shard_map/ppermute | solution.py:43
  67.4 3.2 %collective-permute-start.2 = (bf16[32,512]{1,0:T(8,128)(2,1)S(1)}, bf16[32,512]{1,0:T(8,128)(2,1)S(1)}, u32[]{:S(2)}, u32[]{:S(2)}) collective-permute-start(bf16[32,512]{1,0:T(8,128)(2,1)S(1)} %get-tuple-element.28), channel_id=1, source_target_pairs={{0,15},{1,0},{2,1},{3,2},{4,3},{5,4},{6,5},{7,6},{8,7},{9,8},{10,9... | collective-permute-start | bytes 98312 | tf_op jit(solution)/shard_map/ppermute | solution.py:43
  70.6 10.6 %all-to-all-done.2 = bf16[8,192,512]{2,1,0:T(8,128)(2,1)S(1)} async-done(((bf16[8,192,512]{2,1,0:T(8,128)(2,1)}), bf16[8,192,512]{2,1,0:T(8,128)(2,1)S(1)}, u32[]{:S(2)}, u32[]{:S(2)}) %all-to-all-start.2) | async-done | bytes 1572896 | tf_op jit(solution)/shard_map/all_to_all | solution.py:34
  81.2 0.3 reduce_sum.30
  81.4 0.0 collective-permute-done.3
  81.4 0.0 collective-permute-done.2
  81.5 13.4 %all_to_all.26 = bf16[4,48,512]{2,1,0:T(8,128)(2,1)S(1)} all-to-all(bf16[4,48,512]{2,1,0:T(8,128)(2,1)S(1)} %bitcast.25), channel_id=1, replica_groups={{0,16,32,48},{64,80,96,112},{128,144,160,176},{192,208,224,240},{256,27..., dimensions={0} | all-to-all | bytes 393216 | tf_op jit(solution)/shard_map/all_to_all | solution.py:34
  94.9 0.7 broadcast_in_dim.22
  95.7 19.6 %all-to-all-start.4 = ((bf16[16,16,512]{2,1,0:T(8,128)(2,1)}), bf16[16,16,512]{2,1,0:T(8,128)(2,1)S(1)}, u32[]{:S(2)}, u32[]{:S(2)}) async-start(bf16[16,16,512]{2,1,0:T(8,128)(2,1)} %broadcast_in_dim.22), calls=%async_computation.4 | async-start | bytes 524288 | tf_op jit(solution)/shard_map/all_to_all | solution.py:247
  115.2 0.1 copy.13
  115.3 0.0 copy-start.4
  115.3 7.1 %all-to-all-done.4 = bf16[16,16,512]{2,1,0:T(8,128)(2,1)S(1)} async-done(((bf16[16,16,512]{2,1,0:T(8,128)(2,1)}), bf16[16,16,512]{2,1,0:T(8,128)(2,1)S(1)}, u32[]{:S(2)}, u32[]{:S(2)}) %all-to-all-start.4) | async-done | bytes 262176 | tf_op jit(solution)/shard_map/all_to_all | solution.py:247
  122.4 0.7 convert_reduce_fusion
  123.1 0.0 copy-done.4
  (5 shorter events, 0.1 us)
Async XLA Ops:
  21.4 25.2 %all-to-all-start.1 = ((bf16[8,128,512]{2,1,0:T(8,128)(2,1)}), bf16[8,128,512]{2,1,0:T(8,128)(2,1)S(1)}, u32[]{:S(2)}, u32[]{:S(2)}) async-start(bf16[8,128,512]{2,1,0:T(8,128)(2,1)} %broadcast_in_dim.18), calls=%async_computation.1 | async-start | bytes 2097152 | tf_op jit(solution)/shard_map/all_to_all | solution.py:34
  28.8 17.8 %copy-start = (bf16[1,768,512]{2,1,0:T(8,128)(2,1)S(1)}, bf16[1,768,512]{2,1,0:T(8,128)(2,1)}, u32[]{:S(2)}) copy-start(bf16[1,768,512]{2,1,0:T(8,128)(2,1)} %param.19) | copy-start | bytes 2359300
  28.8 17.8 %copy-start.1 = (bf16[512,512]{1,0:T(8,128)(2,1)S(1)}, bf16[512,512]{1,0:T(8,128)(2,1)}, u32[]{:S(2)}) copy-start(bf16[512,512]{1,0:T(8,128)(2,1)} %weight_hbm.1) | copy-start | bytes 1572868
  28.8 13.0 %collective-permute-start.1 = (bf16[32,512]{1,0:T(8,128)(2,1)S(1)}, bf16[32,512]{1,0:T(8,128)(2,1)S(1)}, u32[]{:S(2)}, u32[]{:S(2)}) collective-permute-start(bf16[32,512]{1,0:T(8,128)(2,1)S(1)} %dynamic-slice_bitcast_fusion), channel_id=1, source_target_pairs={{0,15},{1,0},{2,1},{3,2},{4,3},{5,4},{6,5},{7,6},{8,7},{9,8},{10,9... | collective-permute-start | bytes 98312 | tf_op jit(solution)/shard_map/ppermute | solution.py:43
  32.7 9.2 %collective-permute-start = (bf16[32,512]{1,0:T(8,128)(2,1)S(1)}, bf16[32,512]{1,0:T(8,128)(2,1)S(1)}, u32[]{:S(2)}, u32[]{:S(2)}) collective-permute-start(bf16[32,512]{1,0:T(8,128)(2,1)S(1)} %dynamic-slice_bitcast_fusion), channel_id=1, source_target_pairs={{0,1},{1,2},{2,3},{3,4},{4,5},{5,6},{6,7},{7,8},{8,9},{9,10},{10,1... | collective-permute-start | bytes 98312 | tf_op jit(solution)/shard_map/ppermute | solution.py:43
  46.6 0.9 copy-start.2
  47.5 0.9 copy-start.3
  55.9 25.2 %all-to-all-start.2 = ((bf16[8,192,512]{2,1,0:T(8,128)(2,1)}), bf16[8,192,512]{2,1,0:T(8,128)(2,1)S(1)}, u32[]{:S(2)}, u32[]{:S(2)}) async-start(bf16[8,192,512]{2,1,0:T(8,128)(2,1)} %bitcast.11), calls=%async_computation.2 | async-start | bytes 3145728 | tf_op jit(solution)/shard_map/all_to_all | solution.py:34
  59.6 21.9 %collective-permute-start.3 = (bf16[32,512]{1,0:T(8,128)(2,1)S(1)}, bf16[32,512]{1,0:T(8,128)(2,1)S(1)}, u32[]{:S(2)}, u32[]{:S(2)}) collective-permute-start(bf16[32,512]{1,0:T(8,128)(2,1)S(1)} %get-tuple-element.27), channel_id=1, source_target_pairs={{0,1},{1,2},{2,3},{3,4},{4,5},{5,6},{6,7},{7,8},{8,9},{9,10},{10,1... | collective-permute-start | bytes 98312 | tf_op jit(solution)/shard_map/ppermute | solution.py:43
  67.4 14.1 %collective-permute-start.2 = (bf16[32,512]{1,0:T(8,128)(2,1)S(1)}, bf16[32,512]{1,0:T(8,128)(2,1)S(1)}, u32[]{:S(2)}, u32[]{:S(2)}) collective-permute-start(bf16[32,512]{1,0:T(8,128)(2,1)S(1)} %get-tuple-element.28), channel_id=1, source_target_pairs={{0,15},{1,0},{2,1},{3,2},{4,3},{5,4},{6,5},{7,6},{8,7},{9,8},{10,9... | collective-permute-start | bytes 98312 | tf_op jit(solution)/shard_map/ppermute | solution.py:43
  95.7 26.7 %all-to-all-start.4 = ((bf16[16,16,512]{2,1,0:T(8,128)(2,1)}), bf16[16,16,512]{2,1,0:T(8,128)(2,1)S(1)}, u32[]{:S(2)}, u32[]{:S(2)}) async-start(bf16[16,16,512]{2,1,0:T(8,128)(2,1)} %broadcast_in_dim.22), calls=%async_computation.4 | async-start | bytes 524288 | tf_op jit(solution)/shard_map/all_to_all | solution.py:247
  115.3 7.7 %copy-start.4 = (bf16[1,768,512]{2,1,0:T(8,128)(2,1)}, bf16[1,768,512]{2,1,0:T(8,128)(2,1)S(1)}, u32[]{:S(2)}) copy-start(bf16[1,768,512]{2,1,0:T(8,128)(2,1)S(1)} %fusion.4) | copy-start | bytes 2359300

commit v3 on v2

--- a/solution.py
+++ b/solution.py
@@ -44,18 +44,16 @@
 
 
 def place_of(part, odd):
-    z, y = part // YH, part % YH
-    return jnp.where(odd == 1, (z % 2) * (Z // 2 * YH) + y * (Z // 2) + z // 2, part)
+    return jnp.where(odd == 1, part, part % YH * Z + part // YH)
 
 
 def before_kernel(
     src_ref, row_ref, count_ref, skip_ref, odd_ref, tiles_ref, feats_ref, stale_ref,
-    base_ref, p_ref, pt_ref, ptn_ref, pn_ref, acc_ref,
+    base_ref, p_ref, pt_ref, acc_ref,
 ):
     slots, blk, tr = tiles_ref.shape
     parts = skip_ref.shape[1]
     cached = parts * blk
-    near = cached + 2 * blk
     acc_ref[...] = jnp.zeros_like(acc_ref)
     count = count_ref[0, 0]
     odd = odd_ref[0]
@@ -65,8 +63,9 @@
         def _():
             s = src_ref[0, t]
             inside = jnp.minimum(s, parts - 1)
-            sent = jnp.logical_and(s < parts, skip_ref[0, inside] != 1)
-            block = jnp.where(sent, parts + 2 + place_of(inside, odd), s)
+            kept = jnp.logical_and(s < parts, skip_ref[0, inside] == 1)
+            sent = parts + jnp.where(s < parts, place_of(inside, odd), s)
+            block = jnp.where(kept, s, sent)
             rows = pl.ds(pl.multiple_of(block * blk, blk), blk)
             r = row_ref[0, t]
             acc_ref[r, rows, :] += tiles_ref[t].astype(f32)
@@ -74,24 +73,23 @@
         return carry
 
     lax.fori_loop(0, slots, add_tile, 0)
+    live = pt_ref.shape[0]
     for r in range(acc_ref.shape[0]):
         out = slice(r * tr, (r + 1) * tr)
         old = acc_ref[r, :cached, :].T.astype(bf16)
         base_ref[out, :] = feats_ref[out, :].astype(f32) + jnp.dot(
             old, stale_ref[...], preferred_element_type=f32
         )
-        beside = acc_ref[r, cached:near, :]
-        pn_ref[out, :] = beside.T.astype(bf16)
-        ptn_ref[:, out] = beside.astype(bf16)
-        new = acc_ref[r, near:, :]
+        new = acc_ref[r, cached:, :]
         p_ref[out, :] = new.T.astype(bf16)
-        pt_ref[:, out] = new.astype(bf16)
+        pt_ref[:, out] = new[:live, :].astype(bf16)
 
 
 def after_kernel(
-    odd_ref, base_hbm, p_hbm, cot_hbm, weight_hbm, ptn_hbm, pt_hbm, pn_ref, table_ref, lower_ref,
-    upper_ref, out_hbm, dagg_ref, send_ref, near_ref,
-    base_ref, p_ref, cot_ref, weight_ref, ptn_ref, pt_ref, out_ref, agg_ref, dz_ref, sems, out_sems,
+    odd_ref, base_hbm, p_hbm, cot_hbm, weight_hbm, pt_hbm, table_ref, lower_ref, upper_ref,
+    out_hbm, dagg_ref, send_hbm, near_ref,
+    base_ref, p_ref, cot_ref, weight_ref, pt_ref, out_ref, send_ref, agg_ref, dz_ref, sems,
+    out_sems, send_sems,
 ):
     nodes, width = cot_ref.shape
     parts = send_ref.shape[0]
@@ -115,17 +113,18 @@
             of_weight = fetch(weight_hbm, weight_ref, whole, 3 * steps)
         ahead.append(fetch(cot_hbm, cot_ref, rows, 3 * i + 2))
         arriving.append(ahead)
-    late = [
-        fetch(ptn_hbm, ptn_ref, whole, 3 * steps + 1), fetch(pt_hbm, pt_ref, whole, 3 * steps + 2)
-    ]
+    of_pt = fetch(pt_hbm, pt_ref, whole, 3 * steps + 1)
+    cached = parts * blk
     near_rows = jnp.concatenate([lower_ref[...], upper_ref[...]], axis=0)
     leaving = []
     for i in range(steps):
         rows = chunk(i)
         of_p, of_base, of_cot = arriving[i]
         of_p.wait()
-        new = jnp.dot(p_ref[rows, :], table_ref[...], preferred_element_type=f32)
-        new += jnp.dot(pn_ref[rows, :], near_rows, preferred_element_type=f32)
+        new = jnp.dot(p_ref[rows, :cached], table_ref[...], preferred_element_type=f32)
+        new += jnp.dot(
+            p_ref[rows, cached : cached + 2 * blk], near_rows, preferred_element_type=f32
+        )
         of_base.wait()
         agg = (base_ref[rows, :] + new).astype(bf16)
         agg_ref[rows, :] = agg
@@ -153,13 +152,16 @@
         for j in range(per):
             place = place_of(jnp.int32(i * per + j), odd)
             send_ref[place, blk:, :] = gw[j * share : (j + 1) * share, :]
-    for copy in late:
-        copy.wait()
-    for i in range(parts * blk // step):
+    of_pt.wait()
+    for i in range(cached // step):
         d = jnp.dot(pt_ref[chunk(i), :], dagg_ref[...], preferred_element_type=f32).astype(bf16)
         per = step // blk
-        send_ref[i * per : (i + 1) * per, :blk, :] = d.reshape(per, blk, width)
-    d = jnp.dot(ptn_ref[...], dagg_ref[...], preferred_element_type=f32).astype(bf16)
+        blocks = slice(i * per, (i + 1) * per)
+        send_ref[blocks, :blk, :] = d.reshape(per, blk, width)
+        copy = pltpu.make_async_copy(send_ref.at[blocks], send_hbm.at[blocks], send_sems.at[i])
+        copy.start()
+        leaving.append(copy)
+    d = jnp.dot(pt_ref[cached:, :], dagg_ref[...], preferred_element_type=f32).astype(bf16)
     near_ref[...] = d.reshape(2, blk, width)
     for copy in leaving:
         copy.wait()
@@ -180,31 +182,29 @@
     odd = (lax.axis_index("cluster") % 2).astype(jnp.int32).reshape(1)
     start_row = boundary[0, 0] * blk
     own = lax.dynamic_slice_in_dim(feats, start_row, blk, 0)
-    some = exchange(for_each(own, YH), fours).reshape(YH * blk, width)
+    some = exchange(for_each(own, Z), eights).reshape(Z * blk, width)
     lower = passed_along(own, "cluster", 1)
     upper = passed_along(own, "cluster", -1)
     smem = pl.BlockSpec(memory_space=pltpu.SMEM)
     vmem = pl.BlockSpec(memory_space=pltpu.VMEM)
     hbm = pl.BlockSpec(memory_space=pltpu.HBM)
-    base, p, pt, ptn, pn = pl.pallas_call(
+    base, p, pt = pl.pallas_call(
         before_kernel,
         out_shape=(
             jax.ShapeDtypeStruct((nodes, width), f32),
-            jax.ShapeDtypeStruct((nodes, parts * blk), bf16),
-            jax.ShapeDtypeStruct((parts * blk, nodes), bf16),
-            jax.ShapeDtypeStruct((2 * blk, nodes), bf16),
-            jax.ShapeDtypeStruct((nodes, 2 * blk), bf16),
+            jax.ShapeDtypeStruct((nodes, (parts + 4) * blk), bf16),
+            jax.ShapeDtypeStruct(((parts + 2) * blk, nodes), bf16),
         ),
         in_specs=[smem] * 5 + [vmem] * 3,
-        out_specs=(vmem,) * 5,
-        scratch_shapes=[pltpu.VMEM((row_blocks, (2 * parts + 2) * blk, tr), f32)],
+        out_specs=(vmem,) * 3,
+        scratch_shapes=[pltpu.VMEM((row_blocks, (2 * parts + 4) * blk, tr), f32)],
         compiler_params=pltpu.CompilerParams(vmem_limit_bytes=60 << 20),
         cost_estimate=pl.CostEstimate(
             flops=2 * nodes * width * parts * blk, bytes_accessed=8 << 20, transcendentals=0
         ),
         name="before",
     )(tile_src, tile_row, tile_count, skip, odd, tile_vals[0], feats, stale[0])
-    table = exchange(for_each(some, Z), eights).reshape(parts * blk, width)
+    table = exchange(for_each(some, YH), fours).reshape(parts * blk, width)
     out_features, dagg, send, near = pl.pallas_call(
         after_kernel,
         out_shape=(
@@ -213,20 +213,21 @@
             jax.ShapeDtypeStruct((parts, blk + share, width), bf16),
             jax.ShapeDtypeStruct((2, blk, width), bf16),
         ),
-        in_specs=[smem] + [hbm] * 6 + [vmem] * 4,
-        out_specs=(hbm, vmem, vmem, vmem),
+        in_specs=[smem] + [hbm] * 5 + [vmem] * 3,
+        out_specs=(hbm, vmem, hbm, vmem),
         scratch_shapes=[
             pltpu.VMEM((nodes, width), f32),
-            pltpu.VMEM((nodes, parts * blk), bf16),
+            pltpu.VMEM((nodes, (parts + 4) * blk), bf16),
             pltpu.VMEM((nodes, width), bf16),
             pltpu.VMEM((width, width), bf16),
-            pltpu.VMEM((2 * blk, nodes), bf16),
-            pltpu.VMEM((parts * blk, nodes), bf16),
-            pltpu.VMEM((nodes, width), bf16),
-            pltpu.VMEM((nodes, width), bf16),
-            pltpu.VMEM((nodes, width), bf16),
-            pltpu.SemaphoreType.DMA((nodes // 256 * 3 + 3,)),
+            pltpu.VMEM(((parts + 2) * blk, nodes), bf16),
+            pltpu.VMEM((nodes, width), bf16),
+            pltpu.VMEM((parts, blk + share, width), bf16),
+            pltpu.VMEM((nodes, width), bf16),
+            pltpu.VMEM((nodes, width), bf16),
+            pltpu.SemaphoreType.DMA((nodes // 256 * 3 + 2,)),
             pltpu.SemaphoreType.DMA((nodes // 256,)),
+            pltpu.SemaphoreType.DMA((parts * blk // 256,)),
         ],
         compiler_params=pltpu.CompilerParams(vmem_limit_bytes=48 << 20),
         cost_estimate=pl.CostEstimate(
@@ -235,14 +236,14 @@
             transcendentals=nodes * width,
         ),
         name="after",
-    )(odd, base, p, cotangent[0], weight, ptn, pt, pn, table, lower, upper)
+    )(odd, base, p, cotangent[0], weight, pt, table, lower, upper)
     rows = blk + share
-    got = exchange(send.reshape(Z, YH * rows, width), eights)
+    got = exchange(send.reshape(YH, Z * rows, width), fours)
     from_upper = passed_along(near[0], "cluster", -1)
     from_lower = passed_along(near[1], "cluster", 1)
     some = got.astype(f32).sum(axis=0).astype(bf16)
     some, from_upper, from_lower = lax.optimization_barrier((some, from_upper, from_lower))
-    got = exchange(some.reshape(YH, rows, width), fours)
+    got = exchange(some.reshape(Z, rows, width), eights)
     mine = got.astype(f32).sum(axis=0)
     gw = lax.all_to_all(for_each(mine[blk:].astype(bf16), clusters), "cluster", 0, 0, tiled=True)
     grad_weight = gw.astype(f32).sum(axis=0)

time: 124 us -> 117 us (0.944)
  starting transfers between devices: 47.9 us -> 36.1 us
  blocking collectives: 31.6 us -> 35.6 us
  waiting for transfers between devices: 22.5 us -> 25.3 us
  local copies, waits for them, and re-layouts: 4.51 us -> 2.66 us
    all_to_all x1, starting transfers between devices: 19.6 us -> 7.67 us  [per_device(): lax.all_to_all(for_each(mine[blk:].astype(bf16), clusters), 'cluster', 0,...]
    all_to_all x2, blocking collectives: 31.6 us -> 35.6 us  [exchange(): return lax.all_to_all(x, ALL, 0, 0, axis_index_groups=grouping, tiled=True)]
    ppermute x4, waiting for transfers between devices: 0.01 us -> 3.37 us  [passed_along(): return lax.ppermute(x, axis, [(i, (i + by) % count) for i in range(count)])]
    unnamed x11 -> x7, local copies, waits for them, and re-layouts: 1.89 us -> 0.07 us
  transfers between devices with their start and end apart: 7 -> 7, of which waited for: 3 -> 5; matrix products, arithmetic and copies ran while one was open for 0% -> 0% of each run, Pallas kernels for 5% -> 5%
where the time goes in v3:
time: 117 us; the launch traced here: 116 us
  starting transfers between devices  36.1 us (31%)
  blocking collectives  35.6 us (30%)
  waiting for transfers between devices  25.3 us (22%)
  Pallas kernels  13.1 us (11%)
  local copies, waits for them, and re-layouts  2.66 us (2%)
  between operations  2.05 us (2%)
  other arithmetic  1.17 us (1%)
    all_to_all x2, blocking collectives, exchange(): return lax.all_to_all(x, ALL, 0, 0, axis_index_groups=grouping, tiled=True)  35.6 us
    ppermute x4, starting transfers between devices, passed_along(): return lax.ppermute(x, axis, [(i, (i + by) % count) for i in range(count)])  16.2 us
    all_to_all x2, waiting for transfers between devices, exchange(): return lax.all_to_all(x, ALL, 0, 0, axis_index_groups=grouping, tiled=True)  14.9 us
    all_to_all x2, starting transfers between devices, exchange(): return lax.all_to_all(x, ALL, 0, 0, axis_index_groups=grouping, tiled=True)  12.2 us
    all_to_all x1, starting transfers between devices, per_device(): lax.all_to_all(for_each(mine[blk:].astype(bf16), clusters), 'cluster', 0,...  7.67 us
    all_to_all x1, waiting for transfers between devices, per_device(): lax.all_to_all(for_each(mine[blk:].astype(bf16), clusters), 'cluster', 0,...  7.07 us
    pallas_call x1, Pallas kernels, per_device(): pl.pallas_call(after_kernel, out_shape=(jax.ShapeDtypeStruct((nodes, widt...  7.07 us
    pallas_call x1, Pallas kernels, per_device(): pl.pallas_call(before_kernel, out_shape=(jax.ShapeDtypeStruct((nodes, wid...  6.01 us
  transfers between devices with their start and end apart: 7, of which 5 were waited for; matrix products, arithmetic and copies ran while one was open for 0% of the time, Pallas kernels for 5%

profile of v3, /device:TPU:1, one launch (start us, length us, event | category | flops | bytes accessed | tf_op | source)
XLA Modules:
  0.0 115.9 jit_solution(3185982663529813482)
XLA Ops:
  1.3 0.8 dynamic-slice_bitcast_fusion
  2.1 18.2 %all_to_all.25 = bf16[8,32,512]{2,1,0:T(8,128)(2,1)S(1)} all-to-all(bf16[8,32,512]{2,1,0:T(8,128)(2,1)S(1)} %broadcast_in_dim.17), channel_id=1, replica_groups={{0,64,128,192,256,320,384,448},{16,80,144,208,272,336,400,464},{32,96,1..., dimensions={0} | all-to-all | bytes 524288 | tf_op jit(solution)/shard_map/all_to_all | solution.py:34
  20.3 1.1 broadcast_in_dim.18
  21.3 8.6 %all-to-all-start.1 = ((bf16[4,256,512]{2,1,0:T(8,128)(2,1)}), bf16[4,256,512]{2,1,0:T(8,128)(2,1)S(1)}, u32[]{:S(2)}, u32[]{:S(2)}) async-start(bf16[4,256,512]{2,1,0:T(8,128)(2,1)} %broadcast_in_dim.18), calls=%async_computation.1 | async-start | bytes 2097152 | tf_op jit(solution)/shard_map/all_to_all | solution.py:34
  30.0 0.0 copy-start
  30.0 0.0 copy-start.1
  30.0 5.1 %collective-permute-start.1 = (bf16[32,512]{1,0:T(8,128)(2,1)S(1)}, bf16[32,512]{1,0:T(8,128)(2,1)S(1)}, u32[]{:S(2)}, u32[]{:S(2)}) collective-permute-start(bf16[32,512]{1,0:T(8,128)(2,1)S(1)} %dynamic-slice_bitcast_fusion), channel_id=1, source_target_pairs={{0,15},{1,0},{2,1},{3,2},{4,3},{5,4},{6,5},{7,6},{8,7},{9,8},{10,9... | collective-permute-start | bytes 98312 | tf_op jit(solution)/shard_map/ppermute | solution.py:43
  35.1 2.4 %collective-permute-start = (bf16[32,512]{1,0:T(8,128)(2,1)S(1)}, bf16[32,512]{1,0:T(8,128)(2,1)S(1)}, u32[]{:S(2)}, u32[]{:S(2)}) collective-permute-start(bf16[32,512]{1,0:T(8,128)(2,1)S(1)} %dynamic-slice_bitcast_fusion), channel_id=1, source_target_pairs={{0,1},{1,2},{2,3},{3,4},{4,5},{5,6},{6,7},{7,8},{8,9},{9,10},{10,1... | collective-permute-start | bytes 98312 | tf_op jit(solution)/shard_map/ppermute | solution.py:43
  38.1 6.0 %before.1 = (f32[768,512]{1,0:T(8,128)}, bf16[768,1152]{1,0:T(8,128)(2,1)}, bf16[1088,768]{1,0:T(8,128)(2,1)}) custom-call(s32[1,32]{1,0:T(1,128)} %src_ref.1, s32[1,32]{1,0:T(1,128)} %row_ref.1, s32[1,1]{1,0:T(1,128)S(6)} %copy.15.count_ref, s32[1,32]{1,0:T(1,128)} %skip_ref.1, s32[1]{0:T(128)} %bitcast.odd_ref, bf16[32,32,128]{2,1,0:T(8,128)(2,1)} %bitcast.29, ...), custom_call_target="tpu_custom_call" | custom-call | flops 805306368 | bytes 8388608 | tf_op jit(solution)/shard_map/before/pallas_call | solution.py:191
  44.1 1.2 %collective-permute-done.1.upper_ref = bf16[32,512]{1,0:T(8,128)(2,1)S(1)} collective-permute-done((bf16[32,512]{1,0:T(8,128)(2,1)S(1)}, bf16[32,512]{1,0:T(8,128)(2,1)S(1)}, u32[]{:S(2)}, u32[]{:S(2)}) %collective-permute-start.1) | collective-permute-done | bytes 32800 | tf_op jit(solution)/shard_map/ppermute | solution.py:43
  45.3 0.0 collective-permute-done.lower_ref
  45.3 2.2 %all-to-all-done.1 = bf16[4,256,512]{2,1,0:T(8,128)(2,1)S(1)} async-done(((bf16[4,256,512]{2,1,0:T(8,128)(2,1)}), bf16[4,256,512]{2,1,0:T(8,128)(2,1)S(1)}, u32[]{:S(2)}, u32[]{:S(2)}) %all-to-all-start.1) | async-done | bytes 1048608 | tf_op jit(solution)/shard_map/all_to_all | solution.py:34
  47.6 0.0 copy-done
  47.6 0.0 copy-done.1
  47.6 7.1 %after.1 = (bf16[768,512]{1,0:T(8,128)(2,1)}, bf16[768,512]{1,0:T(8,128)(2,1)S(1)}, bf16[32,48,512]{2,1,0:T(8,128)(2,1)}, bf16[2,32,512]{2,1,0:T(8,128)(2,1)S(1)}) custom-call(s32[1]{0:T(128)} %bitcast.odd_ref, f32[768,512]{1,0:T(8,128)} %get-tuple-element.13.base_hbm, bf16[768,1152]{1,0:T(8,128)(2,1)} %get-tuple-element.14.p_hbm, ...), custom_call_target="tpu_custom_call" | custom-call | flops 2868903936 | bytes 11534336 | tf_op jit(solution)/shard_map/after/pallas_call | solution.py:208
  54.7 3.6 %all-to-all-start.2 = ((bf16[4,384,512]{2,1,0:T(8,128)(2,1)}), bf16[4,384,512]{2,1,0:T(8,128)(2,1)S(1)}, u32[]{:S(2)}, u32[]{:S(2)}) async-start(bf16[4,384,512]{2,1,0:T(8,128)(2,1)} %bitcast.11), calls=%async_computation.2 | async-start | bytes 3145728 | tf_op jit(solution)/shard_map/all_to_all | solution.py:34
  58.3 6.8 %collective-permute-start.3 = (bf16[32,512]{1,0:T(8,128)(2,1)S(1)}, bf16[32,512]{1,0:T(8,128)(2,1)S(1)}, u32[]{:S(2)}, u32[]{:S(2)}) collective-permute-start(bf16[32,512]{1,0:T(8,128)(2,1)S(1)} %get-tuple-element.23), channel_id=1, source_target_pairs={{0,1},{1,2},{2,3},{3,4},{4,5},{5,6},{6,7},{7,8},{8,9},{9,10},{10,1... | collective-permute-start | bytes 98312 | tf_op jit(solution)/shard_map/ppermute | solution.py:43
  65.1 1.9 %collective-permute-start.2 = (bf16[32,512]{1,0:T(8,128)(2,1)S(1)}, bf16[32,512]{1,0:T(8,128)(2,1)S(1)}, u32[]{:S(2)}, u32[]{:S(2)}) collective-permute-start(bf16[32,512]{1,0:T(8,128)(2,1)S(1)} %get-tuple-element.24), channel_id=1, source_target_pairs={{0,15},{1,0},{2,1},{3,2},{4,3},{5,4},{6,5},{7,6},{8,7},{9,8},{10,9... | collective-permute-start | bytes 98312 | tf_op jit(solution)/shard_map/ppermute | solution.py:43
  67.0 12.6 %all-to-all-done.2 = bf16[4,384,512]{2,1,0:T(8,128)(2,1)S(1)} async-done(((bf16[4,384,512]{2,1,0:T(8,128)(2,1)}), bf16[4,384,512]{2,1,0:T(8,128)(2,1)S(1)}, u32[]{:S(2)}, u32[]{:S(2)}) %all-to-all-start.2) | async-done | bytes 1572896 | tf_op jit(solution)/shard_map/all_to_all | solution.py:34
  79.6 0.4 reduce_sum.30
  80.1 0.0 collective-permute-done.3
  80.1 2.1 %collective-permute-done.2 = bf16[32,512]{1,0:T(8,128)(2,1)S(1)} collective-permute-done((bf16[32,512]{1,0:T(8,128)(2,1)S(1)}, bf16[32,512]{1,0:T(8,128)(2,1)S(1)}, u32[]{:S(2)}, u32[]{:S(2)}) %collective-permute-start.2) | collective-permute-done | bytes 32800 | tf_op jit(solution)/shard_map/ppermute | solution.py:43
  82.2 17.4 %all_to_all.26 = bf16[8,48,512]{2,1,0:T(8,128)(2,1)S(1)} all-to-all(bf16[8,48,512]{2,1,0:T(8,128)(2,1)S(1)} %bitcast.25), channel_id=1, replica_groups={{0,64,128,192,256,320,384,448},{16,80,144,208,272,336,400,464},{32,96,1..., dimensions={0} | all-to-all | bytes 786432 | tf_op jit(solution)/shard_map/all_to_all | solution.py:34
  99.6 0.1 convert_reduce_fusion
  99.7 0.7 broadcast_in_dim.22
  100.4 7.7 %all-to-all-start.4 = ((bf16[16,16,512]{2,1,0:T(8,128)(2,1)}), bf16[16,16,512]{2,1,0:T(8,128)(2,1)S(1)}, u32[]{:S(2)}, u32[]{:S(2)}) async-start(bf16[16,16,512]{2,1,0:T(8,128)(2,1)} %broadcast_in_dim.22), calls=%async_computation.4 | async-start | bytes 524288 | tf_op jit(solution)/shard_map/all_to_all | solution.py:248
  108.1 0.1 copy.13
  108.2 0.0 copy-start.2
  108.2 7.1 %all-to-all-done.4 = bf16[16,16,512]{2,1,0:T(8,128)(2,1)S(1)} async-done(((bf16[16,16,512]{2,1,0:T(8,128)(2,1)}), bf16[16,16,512]{2,1,0:T(8,128)(2,1)S(1)}, u32[]{:S(2)}, u32[]{:S(2)}) %all-to-all-start.4) | async-done | bytes 262176 | tf_op jit(solution)/shard_map/all_to_all | solution.py:248
  115.3 0.7 convert_reduce_fusion.1
  115.9 0.0 copy-done.2
  (4 shorter events, 0.1 us)
Async XLA Ops:
  21.3 26.3 %all-to-all-start.1 = ((bf16[4,256,512]{2,1,0:T(8,128)(2,1)}), bf16[4,256,512]{2,1,0:T(8,128)(2,1)S(1)}, u32[]{:S(2)}, u32[]{:S(2)}) async-start(bf16[4,256,512]{2,1,0:T(8,128)(2,1)} %broadcast_in_dim.18), calls=%async_computation.1 | async-start | bytes 2097152 | tf_op jit(solution)/shard_map/all_to_all | solution.py:34
  30.0 17.6 %copy-start = (bf16[1,768,512]{2,1,0:T(8,128)(2,1)S(1)}, bf16[1,768,512]{2,1,0:T(8,128)(2,1)}, u32[]{:S(2)}) copy-start(bf16[1,768,512]{2,1,0:T(8,128)(2,1)} %param.19) | copy-start | bytes 2359300
  30.0 17.6 %copy-start.1 = (bf16[512,512]{1,0:T(8,128)(2,1)S(1)}, bf16[512,512]{1,0:T(8,128)(2,1)}, u32[]{:S(2)}) copy-start(bf16[512,512]{1,0:T(8,128)(2,1)} %weight_hbm.1) | copy-start | bytes 1572868
  30.0 15.4 %collective-permute-start.1 = (bf16[32,512]{1,0:T(8,128)(2,1)S(1)}, bf16[32,512]{1,0:T(8,128)(2,1)S(1)}, u32[]{:S(2)}, u32[]{:S(2)}) collective-permute-start(bf16[32,512]{1,0:T(8,128)(2,1)S(1)} %dynamic-slice_bitcast_fusion), channel_id=1, source_target_pairs={{0,15},{1,0},{2,1},{3,2},{4,3},{5,4},{6,5},{7,6},{8,7},{9,8},{10,9... | collective-permute-start | bytes 98312 | tf_op jit(solution)/shard_map/ppermute | solution.py:43
  35.1 10.3 %collective-permute-start = (bf16[32,512]{1,0:T(8,128)(2,1)S(1)}, bf16[32,512]{1,0:T(8,128)(2,1)S(1)}, u32[]{:S(2)}, u32[]{:S(2)}) collective-permute-start(bf16[32,512]{1,0:T(8,128)(2,1)S(1)} %dynamic-slice_bitcast_fusion), channel_id=1, source_target_pairs={{0,1},{1,2},{2,3},{3,4},{4,5},{5,6},{6,7},{7,8},{8,9},{9,10},{10,1... | collective-permute-start | bytes 98312 | tf_op jit(solution)/shard_map/ppermute | solution.py:43
  54.7 24.9 %all-to-all-start.2 = ((bf16[4,384,512]{2,1,0:T(8,128)(2,1)}), bf16[4,384,512]{2,1,0:T(8,128)(2,1)S(1)}, u32[]{:S(2)}, u32[]{:S(2)}) async-start(bf16[4,384,512]{2,1,0:T(8,128)(2,1)} %bitcast.11), calls=%async_computation.2 | async-start | bytes 3145728 | tf_op jit(solution)/shard_map/all_to_all | solution.py:34
  58.3 21.8 %collective-permute-start.3 = (bf16[32,512]{1,0:T(8,128)(2,1)S(1)}, bf16[32,512]{1,0:T(8,128)(2,1)S(1)}, u32[]{:S(2)}, u32[]{:S(2)}) collective-permute-start(bf16[32,512]{1,0:T(8,128)(2,1)S(1)} %get-tuple-element.23), channel_id=1, source_target_pairs={{0,1},{1,2},{2,3},{3,4},{4,5},{5,6},{6,7},{7,8},{8,9},{9,10},{10,1... | collective-permute-start | bytes 98312 | tf_op jit(solution)/shard_map/ppermute | solution.py:43
  65.1 17.1 %collective-permute-start.2 = (bf16[32,512]{1,0:T(8,128)(2,1)S(1)}, bf16[32,512]{1,0:T(8,128)(2,1)S(1)}, u32[]{:S(2)}, u32[]{:S(2)}) collective-permute-start(bf16[32,512]{1,0:T(8,128)(2,1)S(1)} %get-tuple-element.24), channel_id=1, source_target_pairs={{0,15},{1,0},{2,1},{3,2},{4,3},{5,4},{6,5},{7,6},{8,7},{9,8},{10,9... | collective-permute-start | bytes 98312 | tf_op jit(solution)/shard_map/ppermute | solution.py:43
  100.4 14.8 %all-to-all-start.4 = ((bf16[16,16,512]{2,1,0:T(8,128)(2,1)}), bf16[16,16,512]{2,1,0:T(8,128)(2,1)S(1)}, u32[]{:S(2)}, u32[]{:S(2)}) async-start(bf16[16,16,512]{2,1,0:T(8,128)(2,1)} %broadcast_in_dim.22), calls=%async_computation.4 | async-start | bytes 524288 | tf_op jit(solution)/shard_map/all_to_all | solution.py:248
  108.2 7.7 %copy-start.2 = (bf16[1,768,512]{2,1,0:T(8,128)(2,1)}, bf16[1,768,512]{2,1,0:T(8,128)(2,1)S(1)}, u32[]{:S(2)}) copy-start(bf16[1,768,512]{2,1,0:T(8,128)(2,1)S(1)} %fusion.4) | copy-start | bytes 2359300

commit v4 on v3

--- a/solution.py
+++ b/solution.py
@@ -86,10 +86,9 @@
 
 
 def after_kernel(
-    odd_ref, base_hbm, p_hbm, cot_hbm, weight_hbm, pt_hbm, table_ref, lower_ref, upper_ref,
-    out_hbm, dagg_ref, send_hbm, near_ref,
-    base_ref, p_ref, cot_ref, weight_ref, pt_ref, out_ref, send_ref, agg_ref, dz_ref, sems,
-    out_sems, send_sems,
+    odd_ref, base_hbm, p_hbm, pt_hbm, cot_ref, weight_ref, table_ref, lower_ref, upper_ref,
+    out_hbm, dagg_ref, send_ref, near_ref,
+    base_ref, p_ref, pt_ref, out_ref, agg_ref, dz_ref, sems, out_sems,
 ):
     nodes, width = cot_ref.shape
     parts = send_ref.shape[0]
@@ -108,28 +107,30 @@
     arriving = []
     for i in range(steps):
         rows = chunk(i)
-        ahead = [fetch(p_hbm, p_ref, rows, 3 * i), fetch(base_hbm, base_ref, rows, 3 * i + 1)]
-        if i == 0:
-            of_weight = fetch(weight_hbm, weight_ref, whole, 3 * steps)
-        ahead.append(fetch(cot_hbm, cot_ref, rows, 3 * i + 2))
-        arriving.append(ahead)
-    of_pt = fetch(pt_hbm, pt_ref, whole, 3 * steps + 1)
+        arriving.append(
+            (fetch(p_hbm, p_ref, rows, 2 * i), fetch(base_hbm, base_ref, rows, 2 * i + 1))
+        )
+    of_pt = fetch(pt_hbm, pt_ref, whole, 2 * steps)
     cached = parts * blk
     near_rows = jnp.concatenate([lower_ref[...], upper_ref[...]], axis=0)
     leaving = []
     for i in range(steps):
         rows = chunk(i)
-        of_p, of_base, of_cot = arriving[i]
-        of_p.wait()
+        of_p, of_base = arriving[i]
+        if i == 0:
+            of_p.wait()
+            of_base.wait()
+        if i == 1:
+            for a, b in arriving[1:]:
+                a.wait()
+                b.wait()
+            of_pt.wait()
         new = jnp.dot(p_ref[rows, :cached], table_ref[...], preferred_element_type=f32)
         new += jnp.dot(
             p_ref[rows, cached : cached + 2 * blk], near_rows, preferred_element_type=f32
         )
-        of_base.wait()
         agg = (base_ref[rows, :] + new).astype(bf16)
         agg_ref[rows, :] = agg
-        if i == 0:
-            of_weight.wait()
         z = jnp.dot(agg, weight_ref[...], preferred_element_type=f32)
         sig = jax.nn.sigmoid(z)
         out_ref[rows, :] = (z * sig).astype(bf16)
@@ -137,7 +138,6 @@
         copy.start()
         leaving.append(copy)
         slope = sig * (1.0 + z * (1.0 - sig))
-        of_cot.wait()
         dz = (cot_ref[rows, :].astype(f32) * slope).astype(bf16)
         dz_ref[rows, :] = dz
         dagg_ref[rows, :] = lax.dot_general(
@@ -152,19 +152,24 @@
         for j in range(per):
             place = place_of(jnp.int32(i * per + j), odd)
             send_ref[place, blk:, :] = gw[j * share : (j + 1) * share, :]
-    of_pt.wait()
     for i in range(cached // step):
         d = jnp.dot(pt_ref[chunk(i), :], dagg_ref[...], preferred_element_type=f32).astype(bf16)
         per = step // blk
         blocks = slice(i * per, (i + 1) * per)
         send_ref[blocks, :blk, :] = d.reshape(per, blk, width)
-        copy = pltpu.make_async_copy(send_ref.at[blocks], send_hbm.at[blocks], send_sems.at[i])
-        copy.start()
-        leaving.append(copy)
     d = jnp.dot(pt_ref[cached:, :], dagg_ref[...], preferred_element_type=f32).astype(bf16)
     near_ref[...] = d.reshape(2, blk, width)
     for copy in leaving:
         copy.wait()
+
+
+def last_kernel(got_ref, mine_ref, gw_ref):
+    blk = mine_ref.shape[0]
+    total = got_ref[0].astype(f32)
+    for i in range(1, got_ref.shape[0]):
+        total += got_ref[i].astype(f32)
+    mine_ref[...] = total[:blk, :]
+    gw_ref[...] = jnp.broadcast_to(total[blk:, :].astype(bf16)[None], gw_ref.shape)
 
 
 def per_device(
@@ -213,21 +218,17 @@
             jax.ShapeDtypeStruct((parts, blk + share, width), bf16),
             jax.ShapeDtypeStruct((2, blk, width), bf16),
         ),
-        in_specs=[smem] + [hbm] * 5 + [vmem] * 3,
-        out_specs=(hbm, vmem, hbm, vmem),
+        in_specs=[smem] + [hbm] * 3 + [vmem] * 5,
+        out_specs=(hbm, vmem, vmem, vmem),
         scratch_shapes=[
             pltpu.VMEM((nodes, width), f32),
             pltpu.VMEM((nodes, (parts + 4) * blk), bf16),
-            pltpu.VMEM((nodes, width), bf16),
-            pltpu.VMEM((width, width), bf16),
             pltpu.VMEM(((parts + 2) * blk, nodes), bf16),
             pltpu.VMEM((nodes, width), bf16),
-            pltpu.VMEM((parts, blk + share, width), bf16),
             pltpu.VMEM((nodes, width), bf16),
             pltpu.VMEM((nodes, width), bf16),
-            pltpu.SemaphoreType.DMA((nodes // 256 * 3 + 2,)),
+            pltpu.SemaphoreType.DMA((nodes // 256 * 2 + 1,)),
             pltpu.SemaphoreType.DMA((nodes // 256,)),
-            pltpu.SemaphoreType.DMA((parts * blk // 256,)),
         ],
         compiler_params=pltpu.CompilerParams(vmem_limit_bytes=48 << 20),
         cost_estimate=pl.CostEstimate(
@@ -236,18 +237,29 @@
             transcendentals=nodes * width,
         ),
         name="after",
-    )(odd, base, p, cotangent[0], weight, pt, table, lower, upper)
+    )(odd, base, p, pt, cotangent[0], weight, table, lower, upper)
     rows = blk + share
     got = exchange(send.reshape(YH, Z * rows, width), fours)
+    got, near = lax.optimization_barrier((got, near))
     from_upper = passed_along(near[0], "cluster", -1)
     from_lower = passed_along(near[1], "cluster", 1)
     some = got.astype(f32).sum(axis=0).astype(bf16)
-    some, from_upper, from_lower = lax.optimization_barrier((some, from_upper, from_lower))
     got = exchange(some.reshape(Z, rows, width), eights)
-    mine = got.astype(f32).sum(axis=0)
-    gw = lax.all_to_all(for_each(mine[blk:].astype(bf16), clusters), "cluster", 0, 0, tiled=True)
+    got, from_upper, from_lower = lax.optimization_barrier((got, from_upper, from_lower))
+    mine, gw = pl.pallas_call(
+        last_kernel,
+        out_shape=(
+            jax.ShapeDtypeStruct((blk, width), f32),
+            jax.ShapeDtypeStruct((clusters, share, width), bf16),
+        ),
+        in_specs=[vmem],
+        out_specs=(vmem, vmem),
+        compiler_params=pltpu.CompilerParams(vmem_limit_bytes=8 << 20),
+        name="last",
+    )(got)
+    gw = lax.all_to_all(gw, "cluster", 0, 0, tiled=True)
     grad_weight = gw.astype(f32).sum(axis=0)
-    bgrad = mine[:blk] + from_upper.astype(f32) + from_lower.astype(f32)
+    bgrad = mine + from_upper.astype(f32) + from_lower.astype(f32)
     current = lax.dynamic_slice_in_dim(dagg, start_row, blk, 0).astype(f32)
     grad_features = lax.dynamic_update_slice_in_dim(
         dagg, (current + bgrad).astype(bf16), start_row, 0

time: 117 us -> 115 us (0.983)
  waiting for transfers between devices: 25.3 us -> 14.3 us
  blocking collectives: 35.6 us -> 42.4 us
  starting transfers between devices: 36.1 us -> 40 us
    all_to_all x2, waiting for transfers between devices: 14.9 us -> 2.25 us  [exchange(): return lax.all_to_all(x, ALL, 0, 0, axis_index_groups=grouping, tiled=True)]
    all_to_all x2, blocking collectives: 35.6 us -> 42.4 us  [exchange(): return lax.all_to_all(x, ALL, 0, 0, axis_index_groups=grouping, tiled=True)]
    all_to_all x2, starting transfers between devices: 12.2 us -> 16.1 us  [exchange(): return lax.all_to_all(x, ALL, 0, 0, axis_index_groups=grouping, tiled=True)]
    ppermute x4, starting transfers between devices: 16.2 us -> 14.3 us  [passed_along(): return lax.ppermute(x, axis, [(i, (i + by) % count) for i in range(count)])]
    all_to_all x1, starting transfers between devices: 7.67 us -> 9.53 us  [per_device(): gw = lax.all_to_all(gw, 'cluster', 0, 0, tiled=True)]
    ppermute x4, waiting for transfers between devices: 3.37 us -> 4.93 us  [passed_along(): return lax.ppermute(x, axis, [(i, (i + by) % count) for i in range(count)])]
    pallas_call x1, Pallas kernels: 7.07 us -> 5.74 us  [per_device(): pl.pallas_call(after_kernel, out_shape=(jax.ShapeDtypeStruct((nodes, widt...]
  transfers between devices with their start and end apart: 7 -> 7, of which waited for: 5 -> 4; matrix products, arithmetic and copies ran while one was open for 0% -> 0% of each run, Pallas kernels for 5% -> 5%
where the time goes in v4:
time: 115 us
  blocking collectives  42.4 us (37%)
  starting transfers between devices  40 us (35%)
  waiting for transfers between devices  14.3 us (12%)
  Pallas kernels  12.4 us (11%)
  between operations  2.02 us (2%)
  local copies, waits for them, and re-layouts  1.95 us (2%)
  other arithmetic  1.75 us (2%)
    all_to_all x2, blocking collectives, exchange(): return lax.all_to_all(x, ALL, 0, 0, axis_index_groups=grouping, tiled=True)  42.4 us
    all_to_all x2, starting transfers between devices, exchange(): return lax.all_to_all(x, ALL, 0, 0, axis_index_groups=grouping, tiled=True)  16.1 us
    ppermute x4, starting transfers between devices, passed_along(): return lax.ppermute(x, axis, [(i, (i + by) % count) for i in range(count)])  14.3 us
    all_to_all x1, starting transfers between devices, per_device(): gw = lax.all_to_all(gw, 'cluster', 0, 0, tiled=True)  9.53 us
    all_to_all x1, waiting for transfers between devices, per_device(): gw = lax.all_to_all(gw, 'cluster', 0, 0, tiled=True)  7.07 us
    pallas_call x1, Pallas kernels, per_device(): pl.pallas_call(before_kernel, out_shape=(jax.ShapeDtypeStruct((nodes, wid...  5.89 us
    pallas_call x1, Pallas kernels, per_device(): pl.pallas_call(after_kernel, out_shape=(jax.ShapeDtypeStruct((nodes, widt...  5.74 us
    ppermute x4, waiting for transfers between devices, passed_along(): return lax.ppermute(x, axis, [(i, (i + by) % count) for i in range(count)])  4.93 us
  transfers between devices with their start and end apart: 7, of which 4 were waited for; matrix products, arithmetic and copies ran while one was open for 0% of the time, Pallas kernels for 5%

profile of v4, /device:TPU:1, one launch (start us, length us, event | category | flops | bytes accessed | tf_op | source)
XLA Modules:
  0.0 114.8 jit_solution(8520859031987784937)
XLA Ops:
  1.3 0.8 dynamic-slice_bitcast_fusion
  2.1 18.2 %all_to_all.25 = bf16[8,32,512]{2,1,0:T(8,128)(2,1)S(1)} all-to-all(bf16[8,32,512]{2,1,0:T(8,128)(2,1)S(1)} %broadcast_in_dim.14), channel_id=1, replica_groups={{0,64,128,192,256,320,384,448},{16,80,144,208,272,336,400,464},{32,96,1..., dimensions={0} | all-to-all | bytes 524288 | tf_op jit(solution)/shard_map/all_to_all | solution.py:34
  20.3 1.1 broadcast_in_dim.15
  21.4 8.6 %all-to-all-start.1 = ((bf16[4,256,512]{2,1,0:T(8,128)(2,1)}), bf16[4,256,512]{2,1,0:T(8,128)(2,1)S(1)}, u32[]{:S(2)}, u32[]{:S(2)}) async-start(bf16[4,256,512]{2,1,0:T(8,128)(2,1)} %broadcast_in_dim.15), calls=%async_computation.1 | async-start | bytes 2097152 | tf_op jit(solution)/shard_map/all_to_all | solution.py:34
  30.0 0.0 copy-start
  30.0 0.0 copy-start.1
  30.0 5.1 %collective-permute-start.1 = (bf16[32,512]{1,0:T(8,128)(2,1)S(1)}, bf16[32,512]{1,0:T(8,128)(2,1)S(1)}, u32[]{:S(2)}, u32[]{:S(2)}) collective-permute-start(bf16[32,512]{1,0:T(8,128)(2,1)S(1)} %dynamic-slice_bitcast_fusion), channel_id=1, source_target_pairs={{0,15},{1,0},{2,1},{3,2},{4,3},{5,4},{6,5},{7,6},{8,7},{9,8},{10,9... | collective-permute-start | bytes 98312 | tf_op jit(solution)/shard_map/ppermute | solution.py:43
  35.1 2.4 %collective-permute-start = (bf16[32,512]{1,0:T(8,128)(2,1)S(1)}, bf16[32,512]{1,0:T(8,128)(2,1)S(1)}, u32[]{:S(2)}, u32[]{:S(2)}) collective-permute-start(bf16[32,512]{1,0:T(8,128)(2,1)S(1)} %dynamic-slice_bitcast_fusion), channel_id=1, source_target_pairs={{0,1},{1,2},{2,3},{3,4},{4,5},{5,6},{6,7},{7,8},{8,9},{9,10},{10,1... | collective-permute-start | bytes 98312 | tf_op jit(solution)/shard_map/ppermute | solution.py:43
  38.1 5.9 %before.1 = (f32[768,512]{1,0:T(8,128)}, bf16[768,1152]{1,0:T(8,128)(2,1)}, bf16[1088,768]{1,0:T(8,128)(2,1)}) custom-call(s32[1,32]{1,0:T(1,128)} %src_ref.1, s32[1,32]{1,0:T(1,128)} %row_ref.1, s32[1,1]{1,0:T(1,128)S(6)} %copy.15.count_ref, s32[1,32]{1,0:T(1,128)} %skip_ref.1, s32[1]{0:T(128)} %bitcast.odd_ref, bf16[32,32,128]{2,1,0:T(8,128)(2,1)} %bitcast.29, ...), custom_call_target="tpu_custom_call" | custom-call | flops 805306368 | bytes 8388608 | tf_op jit(solution)/shard_map/before/pallas_call | solution.py:196
  44.0 1.3 %collective-permute-done.1.upper_ref = bf16[32,512]{1,0:T(8,128)(2,1)S(1)} collective-permute-done((bf16[32,512]{1,0:T(8,128)(2,1)S(1)}, bf16[32,512]{1,0:T(8,128)(2,1)S(1)}, u32[]{:S(2)}, u32[]{:S(2)}) %collective-permute-start.1) | collective-permute-done | bytes 32800 | tf_op jit(solution)/shard_map/ppermute | solution.py:43
  45.4 0.0 collective-permute-done.lower_ref
  45.4 2.2 %all-to-all-done.1 = bf16[4,256,512]{2,1,0:T(8,128)(2,1)S(1)} async-done(((bf16[4,256,512]{2,1,0:T(8,128)(2,1)}), bf16[4,256,512]{2,1,0:T(8,128)(2,1)S(1)}, u32[]{:S(2)}, u32[]{:S(2)}) %all-to-all-start.1) | async-done | bytes 1048608 | tf_op jit(solution)/shard_map/all_to_all | solution.py:34
  47.6 0.0 copy-done
  47.6 0.0 copy-done.1
  47.6 5.7 %after.1 = (bf16[768,512]{1,0:T(8,128)(2,1)}, bf16[768,512]{1,0:T(8,128)(2,1)S(1)}, bf16[32,48,512]{2,1,0:T(8,128)(2,1)S(1)}, bf16[2,32,512]{2,1,0:T(8,128)(2,1)S(1)}) custom-call(s32[1]{0:T(128)} %bitcast.odd_ref, f32[768,512]{1,0:T(8,128)} %get-tuple-element.17.base_hbm, bf16[768,1152]{1,0:T(8,128)(2,1)} %get-tuple-element.18.p_hbm, ...), custom_call_target="tpu_custom_call" | custom-call | flops 2868903936 | bytes 11534336 | tf_op jit(solution)/shard_map/after/pallas_call | solution.py:213
  53.4 24.2 %all_to_all.26 = bf16[4,384,512]{2,1,0:T(8,128)(2,1)S(1)} all-to-all(bf16[4,384,512]{2,1,0:T(8,128)(2,1)S(1)} %bitcast.22), channel_id=1, replica_groups={{0,16,32,48},{64,80,96,112},{128,144,160,176},{192,208,224,240},{256,27..., dimensions={0} | all-to-all | bytes 3145728 | tf_op jit(solution)/shard_map/all_to_all | solution.py:34
  77.6 1.1 reduce_sum.21
  78.7 7.5 %all-to-all-start.3 = ((bf16[8,48,512]{2,1,0:T(8,128)(2,1)}), bf16[8,48,512]{2,1,0:T(8,128)(2,1)S(1)}, u32[]{:S(2)}, u32[]{:S(2)}) async-start(bf16[8,48,512]{2,1,0:T(8,128)(2,1)} %bitcast.12), calls=%async_computation.3 | async-start | bytes 786432 | tf_op jit(solution)/shard_map/all_to_all | solution.py:34
  86.2 4.9 %collective-permute-start.3 = (bf16[32,512]{1,0:T(8,128)(2,1)S(1)}, bf16[32,512]{1,0:T(8,128)(2,1)S(1)}, u32[]{:S(2)}, u32[]{:S(2)}) collective-permute-start(bf16[32,512]{1,0:T(8,128)(2,1)S(1)} %get-tuple-element.31), channel_id=1, source_target_pairs={{0,1},{1,2},{2,3},{3,4},{4,5},{5,6},{6,7},{7,8},{8,9},{9,10},{10,1... | collective-permute-start | bytes 98312 | tf_op jit(solution)/shard_map/ppermute | solution.py:43
  91.1 1.9 %collective-permute-start.2 = (bf16[32,512]{1,0:T(8,128)(2,1)S(1)}, bf16[32,512]{1,0:T(8,128)(2,1)S(1)}, u32[]{:S(2)}, u32[]{:S(2)}) collective-permute-start(bf16[32,512]{1,0:T(8,128)(2,1)S(1)} %get-tuple-element.32), channel_id=1, source_target_pairs={{0,15},{1,0},{2,1},{3,2},{4,3},{5,4},{6,5},{7,6},{8,7},{9,8},{10,9... | collective-permute-start | bytes 98312 | tf_op jit(solution)/shard_map/ppermute | solution.py:43
  93.1 0.0 collective-permute-done.3
  93.1 3.6 %collective-permute-done.2 = bf16[32,512]{1,0:T(8,128)(2,1)S(1)} collective-permute-done((bf16[32,512]{1,0:T(8,128)(2,1)S(1)}, bf16[32,512]{1,0:T(8,128)(2,1)S(1)}, u32[]{:S(2)}, u32[]{:S(2)}) %collective-permute-start.2) | collective-permute-done | bytes 32800 | tf_op jit(solution)/shard_map/ppermute | solution.py:43
  96.7 0.0 all-to-all-done.3.got_ref
  96.7 0.7 last.1
  97.4 9.5 %all-to-all-start.4 = ((bf16[16,16,512]{2,1,0:T(8,128)(2,1)}), bf16[16,16,512]{2,1,0:T(8,128)(2,1)S(1)}, u32[]{:S(2)}, u32[]{:S(2)}) async-start(bf16[16,16,512]{2,1,0:T(8,128)(2,1)} %get-tuple-element.30), calls=%async_computation.4 | async-start | bytes 524288 | tf_op jit(solution)/shard_map/all_to_all | solution.py:260
  106.9 0.1 copy.13
  107.0 0.0 copy-start.2
  107.0 7.1 %all-to-all-done.4 = bf16[16,16,512]{2,1,0:T(8,128)(2,1)S(1)} async-done(((bf16[16,16,512]{2,1,0:T(8,128)(2,1)}), bf16[16,16,512]{2,1,0:T(8,128)(2,1)S(1)}, u32[]{:S(2)}, u32[]{:S(2)}) %all-to-all-start.4) | async-done | bytes 262176 | tf_op jit(solution)/shard_map/all_to_all | solution.py:260
  114.1 0.7 convert_reduce_fusion
  114.8 0.0 copy-done.2
  (3 shorter events, 0.0 us)
Async XLA Ops:
  21.4 26.3 %all-to-all-start.1 = ((bf16[4,256,512]{2,1,0:T(8,128)(2,1)}), bf16[4,256,512]{2,1,0:T(8,128)(2,1)S(1)}, u32[]{:S(2)}, u32[]{:S(2)}) async-start(bf16[4,256,512]{2,1,0:T(8,128)(2,1)} %broadcast_in_dim.15), calls=%async_computation.1 | async-start | bytes 2097152 | tf_op jit(solution)/shard_map/all_to_all | solution.py:34
  30.0 17.6 %copy-start = (bf16[1,768,512]{2,1,0:T(8,128)(2,1)S(1)}, bf16[1,768,512]{2,1,0:T(8,128)(2,1)}, u32[]{:S(2)}) copy-start(bf16[1,768,512]{2,1,0:T(8,128)(2,1)} %param.19) | copy-start | bytes 2359300
  30.0 17.6 %copy-start.1 = (bf16[512,512]{1,0:T(8,128)(2,1)S(1)}, bf16[512,512]{1,0:T(8,128)(2,1)}, u32[]{:S(2)}) copy-start(bf16[512,512]{1,0:T(8,128)(2,1)} %weight_ref.1) | copy-start | bytes 1572868
  30.0 15.4 %collective-permute-start.1 = (bf16[32,512]{1,0:T(8,128)(2,1)S(1)}, bf16[32,512]{1,0:T(8,128)(2,1)S(1)}, u32[]{:S(2)}, u32[]{:S(2)}) collective-permute-start(bf16[32,512]{1,0:T(8,128)(2,1)S(1)} %dynamic-slice_bitcast_fusion), channel_id=1, source_target_pairs={{0,15},{1,0},{2,1},{3,2},{4,3},{5,4},{6,5},{7,6},{8,7},{9,8},{10,9... | collective-permute-start | bytes 98312 | tf_op jit(solution)/shard_map/ppermute | solution.py:43
  35.1 10.3 %collective-permute-start = (bf16[32,512]{1,0:T(8,128)(2,1)S(1)}, bf16[32,512]{1,0:T(8,128)(2,1)S(1)}, u32[]{:S(2)}, u32[]{:S(2)}) collective-permute-start(bf16[32,512]{1,0:T(8,128)(2,1)S(1)} %dynamic-slice_bitcast_fusion), channel_id=1, source_target_pairs={{0,1},{1,2},{2,3},{3,4},{4,5},{5,6},{6,7},{7,8},{8,9},{9,10},{10,1... | collective-permute-start | bytes 98312 | tf_op jit(solution)/shard_map/ppermute | solution.py:43
  78.7 18.0 %all-to-all-start.3 = ((bf16[8,48,512]{2,1,0:T(8,128)(2,1)}), bf16[8,48,512]{2,1,0:T(8,128)(2,1)S(1)}, u32[]{:S(2)}, u32[]{:S(2)}) async-start(bf16[8,48,512]{2,1,0:T(8,128)(2,1)} %bitcast.12), calls=%async_computation.3 | async-start | bytes 786432 | tf_op jit(solution)/shard_map/all_to_all | solution.py:34
  86.2 6.8 %collective-permute-start.3 = (bf16[32,512]{1,0:T(8,128)(2,1)S(1)}, bf16[32,512]{1,0:T(8,128)(2,1)S(1)}, u32[]{:S(2)}, u32[]{:S(2)}) collective-permute-start(bf16[32,512]{1,0:T(8,128)(2,1)S(1)} %get-tuple-element.31), channel_id=1, source_target_pairs={{0,1},{1,2},{2,3},{3,4},{4,5},{5,6},{6,7},{7,8},{8,9},{9,10},{10,1... | collective-permute-start | bytes 98312 | tf_op jit(solution)/shard_map/ppermute | solution.py:43
  91.1 5.5 %collective-permute-start.2 = (bf16[32,512]{1,0:T(8,128)(2,1)S(1)}, bf16[32,512]{1,0:T(8,128)(2,1)S(1)}, u32[]{:S(2)}, u32[]{:S(2)}) collective-permute-start(bf16[32,512]{1,0:T(8,128)(2,1)S(1)} %get-tuple-element.32), channel_id=1, source_target_pairs={{0,15},{1,0},{2,1},{3,2},{4,3},{5,4},{6,5},{7,6},{8,7},{9,8},{10,9... | collective-permute-start | bytes 98312 | tf_op jit(solution)/shard_map/ppermute | solution.py:43
  97.4 16.7 %all-to-all-start.4 = ((bf16[16,16,512]{2,1,0:T(8,128)(2,1)}), bf16[16,16,512]{2,1,0:T(8,128)(2,1)S(1)}, u32[]{:S(2)}, u32[]{:S(2)}) async-start(bf16[16,16,512]{2,1,0:T(8,128)(2,1)} %get-tuple-element.30), calls=%async_computation.4 | async-start | bytes 524288 | tf_op jit(solution)/shard_map/all_to_all | solution.py:260
  107.0 7.7 %copy-start.2 = (bf16[1,768,512]{2,1,0:T(8,128)(2,1)}, bf16[1,768,512]{2,1,0:T(8,128)(2,1)S(1)}, u32[]{:S(2)}) copy-start(bf16[1,768,512]{2,1,0:T(8,128)(2,1)S(1)} %fusion.1) | copy-start | bytes 2359300

commit v5 on v4

--- a/solution.py
+++ b/solution.py
@@ -38,9 +38,13 @@
     return jnp.broadcast_to(x, (count, *x.shape))
 
 
-def passed_along(x, axis, by):
+def swapped(x, axis, first):
     count = lax.axis_size(axis)
-    return lax.ppermute(x, axis, [(i, (i + by) % count) for i in range(count)])
+    pairs = []
+    for i in range(first, first + count, 2):
+        a, b = i % count, (i + 1) % count
+        pairs += [(a, b), (b, a)]
+    return lax.ppermute(x, axis, pairs)
 
 
 def place_of(part, odd):
@@ -64,7 +68,8 @@
             s = src_ref[0, t]
             inside = jnp.minimum(s, parts - 1)
             kept = jnp.logical_and(s < parts, skip_ref[0, inside] == 1)
-            sent = parts + jnp.where(s < parts, place_of(inside, odd), s)
+            beside = jnp.where(odd == 1, s, 2 * parts + 1 - s)
+            sent = parts + jnp.where(s < parts, place_of(inside, odd), beside)
             block = jnp.where(kept, s, sent)
             rows = pl.ds(pl.multiple_of(block * blk, blk), blk)
             r = row_ref[0, t]
@@ -86,7 +91,7 @@
 
 
 def after_kernel(
-    odd_ref, base_hbm, p_hbm, pt_hbm, cot_ref, weight_ref, table_ref, lower_ref, upper_ref,
+    odd_ref, base_hbm, p_hbm, pt_hbm, cot_ref, weight_ref, table_ref, inner_ref, outer_ref,
     out_hbm, dagg_ref, send_ref, near_ref,
     base_ref, p_ref, pt_ref, out_ref, agg_ref, dz_ref, sems, out_sems,
 ):
@@ -112,7 +117,7 @@
         )
     of_pt = fetch(pt_hbm, pt_ref, whole, 2 * steps)
     cached = parts * blk
-    near_rows = jnp.concatenate([lower_ref[...], upper_ref[...]], axis=0)
+    near_rows = jnp.concatenate([inner_ref[...], outer_ref[...]], axis=0)
     leaving = []
     for i in range(steps):
         rows = chunk(i)
@@ -188,8 +193,8 @@
     start_row = boundary[0, 0] * blk
     own = lax.dynamic_slice_in_dim(feats, start_row, blk, 0)
     some = exchange(for_each(own, Z), eights).reshape(Z * blk, width)
-    lower = passed_along(own, "cluster", 1)
-    upper = passed_along(own, "cluster", -1)
+    inner = swapped(own, "cluster", 0)
+    outer = swapped(own, "cluster", 1)
     smem = pl.BlockSpec(memory_space=pltpu.SMEM)
     vmem = pl.BlockSpec(memory_space=pltpu.VMEM)
     hbm = pl.BlockSpec(memory_space=pltpu.HBM)
@@ -237,15 +242,15 @@
             transcendentals=nodes * width,
         ),
         name="after",
-    )(odd, base, p, pt, cotangent[0], weight, table, lower, upper)
+    )(odd, base, p, pt, cotangent[0], weight, table, inner, outer)
     rows = blk + share
     got = exchange(send.reshape(YH, Z * rows, width), fours)
     got, near = lax.optimization_barrier((got, near))
-    from_upper = passed_along(near[0], "cluster", -1)
-    from_lower = passed_along(near[1], "cluster", 1)
+    from_inner = swapped(near[0], "cluster", 0)
+    from_outer = swapped(near[1], "cluster", 1)
     some = got.astype(f32).sum(axis=0).astype(bf16)
     got = exchange(some.reshape(Z, rows, width), eights)
-    got, from_upper, from_lower = lax.optimization_barrier((got, from_upper, from_lower))
+    got, from_inner, from_outer = lax.optimization_barrier((got, from_inner, from_outer))
     mine, gw = pl.pallas_call(
         last_kernel,
         out_shape=(
@@ -259,7 +264,7 @@
     )(got)
     gw = lax.all_to_all(gw, "cluster", 0, 0, tiled=True)
     grad_weight = gw.astype(f32).sum(axis=0)
-    bgrad = mine + from_upper.astype(f32) + from_lower.astype(f32)
+    bgrad = mine + from_inner.astype(f32) + from_outer.astype(f32)
     current = lax.dynamic_slice_in_dim(dagg, start_row, blk, 0).astype(f32)
     grad_features = lax.dynamic_update_slice_in_dim(
         dagg, (current + bgrad).astype(bf16), start_row, 0

time: 115 us -> 115 us (level)
  waiting for transfers between devices: 14.3 us -> 13 us
    all_to_all x1, starting transfers between devices: 9.53 us -> 10.7 us  [per_device(): gw = lax.all_to_all(gw, 'cluster', 0, 0, tiled=True)]
  transfers between devices with their start and end apart: 7 -> 7, of which waited for: 4 -> 6; matrix products, arithmetic and copies ran while one was open for 0% -> 0% of each run, Pallas kernels for 5% -> 5%
where the time goes in v5:
time: 115 us
  blocking collectives  43.2 us (38%)
  starting transfers between devices  40.4 us (35%)
  waiting for transfers between devices  13 us (11%)
  Pallas kernels  12.5 us (11%)
  between operations  2.02 us (2%)
  local copies, waits for them, and re-layouts  1.95 us (2%)
  other arithmetic  1.75 us (2%)
    all_to_all x2, blocking collectives, exchange(): return lax.all_to_all(x, ALL, 0, 0, axis_index_groups=grouping, tiled=True)  43.2 us
    all_to_all x2, starting transfers between devices, exchange(): return lax.all_to_all(x, ALL, 0, 0, axis_index_groups=grouping, tiled=True)  15.4 us
    ppermute x4, starting transfers between devices, swapped(): return lax.ppermute(x, axis, pairs)  14.3 us
    all_to_all x1, starting transfers between devices, per_device(): gw = lax.all_to_all(gw, 'cluster', 0, 0, tiled=True)  10.7 us
    all_to_all x1, waiting for transfers between devices, per_device(): gw = lax.all_to_all(gw, 'cluster', 0, 0, tiled=True)  7.07 us
    pallas_call x1, Pallas kernels, per_device(): pl.pallas_call(before_kernel, out_shape=(jax.ShapeDtypeStruct((nodes, wid...  5.99 us
    pallas_call x1, Pallas kernels, per_device(): pl.pallas_call(after_kernel, out_shape=(jax.ShapeDtypeStruct((nodes, widt...  5.74 us
    ppermute x4, waiting for transfers between devices, swapped(): return lax.ppermute(x, axis, pairs)  3.88 us
  transfers between devices with their start and end apart: 7, of which 6 were waited for; matrix products, arithmetic and copies ran while one was open for 0% of the time, Pallas kernels for 5%

profile of v5, /device:TPU:1, one launch (start us, length us, event | category | flops | bytes accessed | tf_op | source)
XLA Modules:
  0.0 114.8 jit_solution(28682982534451141)
XLA Ops:
  1.3 0.8 dynamic-slice_bitcast_fusion
  2.1 18.2 %all_to_all.25 = bf16[8,32,512]{2,1,0:T(8,128)(2,1)S(1)} all-to-all(bf16[8,32,512]{2,1,0:T(8,128)(2,1)S(1)} %broadcast_in_dim.14), channel_id=1, replica_groups={{0,64,128,192,256,320,384,448},{16,80,144,208,272,336,400,464},{32,96,1..., dimensions={0} | all-to-all | bytes 524288 | tf_op jit(solution)/shard_map/all_to_all | solution.py:34
  20.3 1.1 broadcast_in_dim.15
  21.4 8.6 %all-to-all-start.1 = ((bf16[4,256,512]{2,1,0:T(8,128)(2,1)}), bf16[4,256,512]{2,1,0:T(8,128)(2,1)S(1)}, u32[]{:S(2)}, u32[]{:S(2)}) async-start(bf16[4,256,512]{2,1,0:T(8,128)(2,1)} %broadcast_in_dim.15), calls=%async_computation.1 | async-start | bytes 2097152 | tf_op jit(solution)/shard_map/all_to_all | solution.py:34
  30.0 0.0 copy-start
  30.0 0.0 copy-start.1
  30.0 5.6 %collective-permute-start.1 = (bf16[32,512]{1,0:T(8,128)(2,1)S(1)}, bf16[32,512]{1,0:T(8,128)(2,1)S(1)}, u32[]{:S(2)}, u32[]{:S(2)}) collective-permute-start(bf16[32,512]{1,0:T(8,128)(2,1)S(1)} %dynamic-slice_bitcast_fusion), channel_id=1, source_target_pairs={{1,2},{2,1},{3,4},{4,3},{5,6},{6,5},{7,8},{8,7},{9,10},{10,9},{11,... | collective-permute-start | bytes 98312 | tf_op jit(solution)/shard_map/ppermute | solution.py:47
  35.5 2.0 %collective-permute-start = (bf16[32,512]{1,0:T(8,128)(2,1)S(1)}, bf16[32,512]{1,0:T(8,128)(2,1)S(1)}, u32[]{:S(2)}, u32[]{:S(2)}) collective-permute-start(bf16[32,512]{1,0:T(8,128)(2,1)S(1)} %dynamic-slice_bitcast_fusion), channel_id=1, source_target_pairs={{0,1},{1,0},{2,3},{3,2},{4,5},{5,4},{6,7},{7,6},{8,9},{9,8},{10,11... | collective-permute-start | bytes 98312 | tf_op jit(solution)/shard_map/ppermute | solution.py:47
  38.2 6.0 %before.1 = (f32[768,512]{1,0:T(8,128)}, bf16[768,1152]{1,0:T(8,128)(2,1)}, bf16[1088,768]{1,0:T(8,128)(2,1)}) custom-call(s32[1,32]{1,0:T(1,128)} %src_ref.1, s32[1,32]{1,0:T(1,128)} %row_ref.1, s32[1,1]{1,0:T(1,128)S(6)} %copy.15.count_ref, s32[1,32]{1,0:T(1,128)} %skip_ref.1, s32[1]{0:T(128)} %bitcast.odd_ref, bf16[32,32,128]{2,1,0:T(8,128)(2,1)} %bitcast.29, ...), custom_call_target="tpu_custom_call" | custom-call | flops 805306368 | bytes 8388608 | tf_op jit(solution)/shard_map/before/pallas_call | solution.py:201
  44.2 2.7 %collective-permute-done.1.outer_ref = bf16[32,512]{1,0:T(8,128)(2,1)S(1)} collective-permute-done((bf16[32,512]{1,0:T(8,128)(2,1)S(1)}, bf16[32,512]{1,0:T(8,128)(2,1)S(1)}, u32[]{:S(2)}, u32[]{:S(2)}) %collective-permute-start.1) | collective-permute-done | bytes 32800 | tf_op jit(solution)/shard_map/ppermute | solution.py:47
  46.9 0.0 collective-permute-done.inner_ref
  46.9 0.7 all-to-all-done.1
  47.6 0.0 copy-done
  47.6 0.0 copy-done.1
  47.6 5.7 %after.1 = (bf16[768,512]{1,0:T(8,128)(2,1)}, bf16[768,512]{1,0:T(8,128)(2,1)S(1)}, bf16[32,48,512]{2,1,0:T(8,128)(2,1)S(1)}, bf16[2,32,512]{2,1,0:T(8,128)(2,1)S(1)}) custom-call(s32[1]{0:T(128)} %bitcast.odd_ref, f32[768,512]{1,0:T(8,128)} %get-tuple-element.17.base_hbm, bf16[768,1152]{1,0:T(8,128)(2,1)} %get-tuple-element.18.p_hbm, ...), custom_call_target="tpu_custom_call" | custom-call | flops 2868903936 | bytes 11534336 | tf_op jit(solution)/shard_map/after/pallas_call | solution.py:218
  53.4 25.0 %all_to_all.26 = bf16[4,384,512]{2,1,0:T(8,128)(2,1)S(1)} all-to-all(bf16[4,384,512]{2,1,0:T(8,128)(2,1)S(1)} %bitcast.22), channel_id=1, replica_groups={{0,16,32,48},{64,80,96,112},{128,144,160,176},{192,208,224,240},{256,27..., dimensions={0} | all-to-all | bytes 3145728 | tf_op jit(solution)/shard_map/all_to_all | solution.py:34
  78.4 1.1 reduce_sum.21
  79.4 6.8 %all-to-all-start.3 = ((bf16[8,48,512]{2,1,0:T(8,128)(2,1)}), bf16[8,48,512]{2,1,0:T(8,128)(2,1)S(1)}, u32[]{:S(2)}, u32[]{:S(2)}) async-start(bf16[8,48,512]{2,1,0:T(8,128)(2,1)} %bitcast.12), calls=%async_computation.3 | async-start | bytes 786432 | tf_op jit(solution)/shard_map/all_to_all | solution.py:34
  86.2 4.9 %collective-permute-start.3 = (bf16[32,512]{1,0:T(8,128)(2,1)S(1)}, bf16[32,512]{1,0:T(8,128)(2,1)S(1)}, u32[]{:S(2)}, u32[]{:S(2)}) collective-permute-start(bf16[32,512]{1,0:T(8,128)(2,1)S(1)} %get-tuple-element.31), channel_id=1, source_target_pairs={{1,2},{2,1},{3,4},{4,3},{5,6},{6,5},{7,8},{8,7},{9,10},{10,9},{11,... | collective-permute-start | bytes 98312 | tf_op jit(solution)/shard_map/ppermute | solution.py:47
  91.1 1.9 %collective-permute-start.2 = (bf16[32,512]{1,0:T(8,128)(2,1)S(1)}, bf16[32,512]{1,0:T(8,128)(2,1)S(1)}, u32[]{:S(2)}, u32[]{:S(2)}) collective-permute-start(bf16[32,512]{1,0:T(8,128)(2,1)S(1)} %get-tuple-element.32), channel_id=1, source_target_pairs={{0,1},{1,0},{2,3},{3,2},{4,5},{5,4},{6,7},{7,6},{8,9},{9,8},{10,11... | collective-permute-start | bytes 98312 | tf_op jit(solution)/shard_map/ppermute | solution.py:47
  93.1 0.5 collective-permute-done.3
  93.5 0.7 collective-permute-done.2
  94.2 1.3 %all-to-all-done.3.got_ref = bf16[8,48,512]{2,1,0:T(8,128)(2,1)S(1)} async-done(((bf16[8,48,512]{2,1,0:T(8,128)(2,1)}), bf16[8,48,512]{2,1,0:T(8,128)(2,1)S(1)}, u32[]{:S(2)}, u32[]{:S(2)}) %all-to-all-start.3) | async-done | bytes 393248 | tf_op jit(solution)/shard_map/all_to_all | solution.py:34
  95.5 0.7 last.1
  96.2 10.7 %all-to-all-start.4 = ((bf16[16,16,512]{2,1,0:T(8,128)(2,1)}), bf16[16,16,512]{2,1,0:T(8,128)(2,1)S(1)}, u32[]{:S(2)}, u32[]{:S(2)}) async-start(bf16[16,16,512]{2,1,0:T(8,128)(2,1)} %get-tuple-element.30), calls=%async_computation.4 | async-start | bytes 524288 | tf_op jit(solution)/shard_map/all_to_all | solution.py:265
  106.9 0.1 copy.13
  107.0 0.0 copy-start.2
  107.0 7.1 %all-to-all-done.4 = bf16[16,16,512]{2,1,0:T(8,128)(2,1)S(1)} async-done(((bf16[16,16,512]{2,1,0:T(8,128)(2,1)}), bf16[16,16,512]{2,1,0:T(8,128)(2,1)S(1)}, u32[]{:S(2)}, u32[]{:S(2)}) %all-to-all-start.4) | async-done | bytes 262176 | tf_op jit(solution)/shard_map/all_to_all | solution.py:265
  114.1 0.7 convert_reduce_fusion
  114.8 0.0 copy-done.2
  (3 shorter events, 0.0 us)
Async XLA Ops:
  21.4 26.3 %all-to-all-start.1 = ((bf16[4,256,512]{2,1,0:T(8,128)(2,1)}), bf16[4,256,512]{2,1,0:T(8,128)(2,1)S(1)}, u32[]{:S(2)}, u32[]{:S(2)}) async-start(bf16[4,256,512]{2,1,0:T(8,128)(2,1)} %broadcast_in_dim.15), calls=%async_computation.1 | async-start | bytes 2097152 | tf_op jit(solution)/shard_map/all_to_all | solution.py:34
  30.0 17.6 %copy-start = (bf16[1,768,512]{2,1,0:T(8,128)(2,1)S(1)}, bf16[1,768,512]{2,1,0:T(8,128)(2,1)}, u32[]{:S(2)}) copy-start(bf16[1,768,512]{2,1,0:T(8,128)(2,1)} %param.19) | copy-start | bytes 2359300
  30.0 17.6 %copy-start.1 = (bf16[512,512]{1,0:T(8,128)(2,1)S(1)}, bf16[512,512]{1,0:T(8,128)(2,1)}, u32[]{:S(2)}) copy-start(bf16[512,512]{1,0:T(8,128)(2,1)} %weight_ref.1) | copy-start | bytes 1572868
  30.0 16.9 %collective-permute-start.1 = (bf16[32,512]{1,0:T(8,128)(2,1)S(1)}, bf16[32,512]{1,0:T(8,128)(2,1)S(1)}, u32[]{:S(2)}, u32[]{:S(2)}) collective-permute-start(bf16[32,512]{1,0:T(8,128)(2,1)S(1)} %dynamic-slice_bitcast_fusion), channel_id=1, source_target_pairs={{1,2},{2,1},{3,4},{4,3},{5,6},{6,5},{7,8},{8,7},{9,10},{10,9},{11,... | collective-permute-start | bytes 98312 | tf_op jit(solution)/shard_map/ppermute | solution.py:47
  35.5 11.3 %collective-permute-start = (bf16[32,512]{1,0:T(8,128)(2,1)S(1)}, bf16[32,512]{1,0:T(8,128)(2,1)S(1)}, u32[]{:S(2)}, u32[]{:S(2)}) collective-permute-start(bf16[32,512]{1,0:T(8,128)(2,1)S(1)} %dynamic-slice_bitcast_fusion), channel_id=1, source_target_pairs={{0,1},{1,0},{2,3},{3,2},{4,5},{5,4},{6,7},{7,6},{8,9},{9,8},{10,11... | collective-permute-start | bytes 98312 | tf_op jit(solution)/shard_map/ppermute | solution.py:47
  79.4 16.1 %all-to-all-start.3 = ((bf16[8,48,512]{2,1,0:T(8,128)(2,1)}), bf16[8,48,512]{2,1,0:T(8,128)(2,1)S(1)}, u32[]{:S(2)}, u32[]{:S(2)}) async-start(bf16[8,48,512]{2,1,0:T(8,128)(2,1)} %bitcast.12), calls=%async_computation.3 | async-start | bytes 786432 | tf_op jit(solution)/shard_map/all_to_all | solution.py:34
  86.2 7.3 %collective-permute-start.3 = (bf16[32,512]{1,0:T(8,128)(2,1)S(1)}, bf16[32,512]{1,0:T(8,128)(2,1)S(1)}, u32[]{:S(2)}, u32[]{:S(2)}) collective-permute-start(bf16[32,512]{1,0:T(8,128)(2,1)S(1)} %get-tuple-element.31), channel_id=1, source_target_pairs={{1,2},{2,1},{3,4},{4,3},{5,6},{6,5},{7,8},{8,7},{9,10},{10,9},{11,... | collective-permute-start | bytes 98312 | tf_op jit(solution)/shard_map/ppermute | solution.py:47
  91.1 3.1 %collective-permute-start.2 = (bf16[32,512]{1,0:T(8,128)(2,1)S(1)}, bf16[32,512]{1,0:T(8,128)(2,1)S(1)}, u32[]{:S(2)}, u32[]{:S(2)}) collective-permute-start(bf16[32,512]{1,0:T(8,128)(2,1)S(1)} %get-tuple-element.32), channel_id=1, source_target_pairs={{0,1},{1,0},{2,3},{3,2},{4,5},{5,4},{6,7},{7,6},{8,9},{9,8},{10,11... | collective-permute-start | bytes 98312 | tf_op jit(solution)/shard_map/ppermute | solution.py:47
  96.2 17.9 %all-to-all-start.4 = ((bf16[16,16,512]{2,1,0:T(8,128)(2,1)}), bf16[16,16,512]{2,1,0:T(8,128)(2,1)S(1)}, u32[]{:S(2)}, u32[]{:S(2)}) async-start(bf16[16,16,512]{2,1,0:T(8,128)(2,1)} %get-tuple-element.30), calls=%async_computation.4 | async-start | bytes 524288 | tf_op jit(solution)/shard_map/all_to_all | solution.py:265
  107.0 7.7 %copy-start.2 = (bf16[1,768,512]{2,1,0:T(8,128)(2,1)}, bf16[1,768,512]{2,1,0:T(8,128)(2,1)S(1)}, u32[]{:S(2)}) copy-start(bf16[1,768,512]{2,1,0:T(8,128)(2,1)S(1)} %fusion.1) | copy-start | bytes 2359300

commit v6 on v5

--- a/solution.py
+++ b/solution.py
@@ -195,6 +195,7 @@
     some = exchange(for_each(own, Z), eights).reshape(Z * blk, width)
     inner = swapped(own, "cluster", 0)
     outer = swapped(own, "cluster", 1)
+    some, inner, outer = lax.optimization_barrier((some, inner, outer))
     smem = pl.BlockSpec(memory_space=pltpu.SMEM)
     vmem = pl.BlockSpec(memory_space=pltpu.VMEM)
     hbm = pl.BlockSpec(memory_space=pltpu.HBM)
@@ -245,12 +246,8 @@
     )(odd, base, p, pt, cotangent[0], weight, table, inner, outer)
     rows = blk + share
     got = exchange(send.reshape(YH, Z * rows, width), fours)
-    got, near = lax.optimization_barrier((got, near))
-    from_inner = swapped(near[0], "cluster", 0)
-    from_outer = swapped(near[1], "cluster", 1)
     some = got.astype(f32).sum(axis=0).astype(bf16)
     got = exchange(some.reshape(Z, rows, width), eights)
-    got, from_inner, from_outer = lax.optimization_barrier((got, from_inner, from_outer))
     mine, gw = pl.pallas_call(
         last_kernel,
         out_shape=(
@@ -262,7 +259,10 @@
         compiler_params=pltpu.CompilerParams(vmem_limit_bytes=8 << 20),
         name="last",
     )(got)
+    gw, near = lax.optimization_barrier((gw, near))
     gw = lax.all_to_all(gw, "cluster", 0, 0, tiled=True)
+    from_inner = swapped(near[0], "cluster", 0)
+    from_outer = swapped(near[1], "cluster", 1)
     grad_weight = gw.astype(f32).sum(axis=0)
     bgrad = mine + from_inner.astype(f32) + from_outer.astype(f32)
     current = lax.dynamic_slice_in_dim(dagg, start_row, blk, 0).astype(f32)

time: 115 us -> 115 us (level); the launches traced: 115 us -> 113 us
  blocking collectives: 43.2 us -> 40.9 us
  starting transfers between devices: 40.4 us -> 38.9 us
  waiting for transfers between devices: 13 us -> 14.2 us
    all_to_all x2, waiting for transfers between devices: 2.01 us -> 11.1 us  [exchange(): return lax.all_to_all(x, ALL, 0, 0, axis_index_groups=grouping, tiled=True)]
    all_to_all x1, waiting for transfers between devices: 7.07 us -> 0.01 us  [per_device(): gw = lax.all_to_all(gw, 'cluster', 0, 0, tiled=True)]
    all_to_all x1, starting transfers between devices: 10.7 us -> 7.9 us  [per_device(): gw = lax.all_to_all(gw, 'cluster', 0, 0, tiled=True)]
    all_to_all x2, starting transfers between devices: 15.4 us -> 18.1 us  [exchange(): return lax.all_to_all(x, ALL, 0, 0, axis_index_groups=grouping, tiled=True)]
    all_to_all x2, blocking collectives: 43.2 us -> 40.9 us  [exchange(): return lax.all_to_all(x, ALL, 0, 0, axis_index_groups=grouping, tiled=True)]
    ppermute x4, starting transfers between devices: 14.3 us -> 13 us  [swapped(): return lax.ppermute(x, axis, pairs)]
  transfers between devices with their start and end apart: 7 -> 7, of which waited for: 6 -> 4; matrix products, arithmetic and copies ran while one was open for 0% -> 0% of each run, Pallas kernels for 5% -> 5%
where the time goes in v6:
time: 115 us; the launch traced here: 113 us
  blocking collectives  40.9 us (36%)
  starting transfers between devices  38.9 us (34%)
  waiting for transfers between devices  14.2 us (12%)
  Pallas kernels  12.6 us (11%)
  local copies, waits for them, and re-layouts  2.75 us (2%)
  between operations  2.14 us (2%)
  other arithmetic  1.22 us (1%)
    all_to_all x2, blocking collectives, exchange(): return lax.all_to_all(x, ALL, 0, 0, axis_index_groups=grouping, tiled=True)  40.9 us
    all_to_all x2, starting transfers between devices, exchange(): return lax.all_to_all(x, ALL, 0, 0, axis_index_groups=grouping, tiled=True)  18.1 us
    ppermute x4, starting transfers between devices, swapped(): return lax.ppermute(x, axis, pairs)  13 us
    all_to_all x2, waiting for transfers between devices, exchange(): return lax.all_to_all(x, ALL, 0, 0, axis_index_groups=grouping, tiled=True)  11.1 us
    all_to_all x1, starting transfers between devices, per_device(): gw = lax.all_to_all(gw, 'cluster', 0, 0, tiled=True)  7.9 us
    pallas_call x1, Pallas kernels, per_device(): pl.pallas_call(before_kernel, out_shape=(jax.ShapeDtypeStruct((nodes, wid...  6.11 us
    pallas_call x1, Pallas kernels, per_device(): pl.pallas_call(after_kernel, out_shape=(jax.ShapeDtypeStruct((nodes, widt...  5.74 us
    ppermute x4, waiting for transfers between devices, swapped(): return lax.ppermute(x, axis, pairs)  3.03 us
  transfers between devices with their start and end apart: 7, of which 4 were waited for; matrix products, arithmetic and copies ran while one was open for 0% of the time, Pallas kernels for 5%

profile of v6, /device:TPU:1, one launch (start us, length us, event | category | flops | bytes accessed | tf_op | source)
XLA Modules:
  0.0 112.7 jit_solution(3250895557508627164)
XLA Ops:
  1.3 0.8 dynamic-slice_bitcast_fusion
  2.0 0.7 broadcast_in_dim.14
  2.8 9.5 %all-to-all-start = ((bf16[8,32,512]{2,1,0:T(8,128)(2,1)}), bf16[8,32,512]{2,1,0:T(8,128)(2,1)S(1)}, u32[]{:S(2)}, u32[]{:S(2)}) async-start(bf16[8,32,512]{2,1,0:T(8,128)(2,1)} %broadcast_in_dim.14), calls=%async_computation | async-start | bytes 524288 | tf_op jit(solution)/shard_map/all_to_all | solution.py:34
  12.2 5.4 %collective-permute-start.1 = (bf16[32,512]{1,0:T(8,128)(2,1)S(1)}, bf16[32,512]{1,0:T(8,128)(2,1)S(1)}, u32[]{:S(2)}, u32[]{:S(2)}) collective-permute-start(bf16[32,512]{1,0:T(8,128)(2,1)S(1)} %dynamic-slice_bitcast_fusion), channel_id=1, source_target_pairs={{1,2},{2,1},{3,4},{4,3},{5,6},{6,5},{7,8},{8,7},{9,10},{10,9},{11,... | collective-permute-start | bytes 98312 | tf_op jit(solution)/shard_map/ppermute | solution.py:47
  17.7 1.9 %collective-permute-start = (bf16[32,512]{1,0:T(8,128)(2,1)S(1)}, bf16[32,512]{1,0:T(8,128)(2,1)S(1)}, u32[]{:S(2)}, u32[]{:S(2)}) collective-permute-start(bf16[32,512]{1,0:T(8,128)(2,1)S(1)} %dynamic-slice_bitcast_fusion), channel_id=1, source_target_pairs={{0,1},{1,0},{2,3},{3,2},{4,5},{5,4},{6,7},{7,6},{8,9},{9,8},{10,11... | collective-permute-start | bytes 98312 | tf_op jit(solution)/shard_map/ppermute | solution.py:47
  19.6 0.0 collective-permute-done.1.outer_ref
  19.6 1.2 %collective-permute-done.inner_ref = bf16[32,512]{1,0:T(8,128)(2,1)S(1)} collective-permute-done((bf16[32,512]{1,0:T(8,128)(2,1)S(1)}, bf16[32,512]{1,0:T(8,128)(2,1)S(1)}, u32[]{:S(2)}, u32[]{:S(2)}) %collective-permute-start) | collective-permute-done | bytes 32800 | tf_op jit(solution)/shard_map/ppermute | solution.py:47
  20.8 0.4 all-to-all-done
  21.2 1.1 broadcast_in_dim.15
  22.3 8.6 %all-to-all-start.1 = ((bf16[4,256,512]{2,1,0:T(8,128)(2,1)}), bf16[4,256,512]{2,1,0:T(8,128)(2,1)S(1)}, u32[]{:S(2)}, u32[]{:S(2)}) async-start(bf16[4,256,512]{2,1,0:T(8,128)(2,1)} %broadcast_in_dim.15), calls=%async_computation.1 | async-start | bytes 2097152 | tf_op jit(solution)/shard_map/all_to_all | solution.py:34
  30.9 0.0 copy-start
  30.9 0.0 copy-start.1
  31.6 6.1 %before.1 = (f32[768,512]{1,0:T(8,128)}, bf16[768,1152]{1,0:T(8,128)(2,1)}, bf16[1088,768]{1,0:T(8,128)(2,1)}) custom-call(s32[1,32]{1,0:T(1,128)} %src_ref.1, s32[1,32]{1,0:T(1,128)} %row_ref.1, s32[1,1]{1,0:T(1,128)S(6)} %copy.15.count_ref, s32[1,32]{1,0:T(1,128)} %skip_ref.1, s32[1]{0:T(128)} %bitcast.odd_ref, bf16[32,32,128]{2,1,0:T(8,128)(2,1)} %bitcast.30, ...), custom_call_target="tpu_custom_call" | custom-call | flops 805306368 | bytes 8388608 | tf_op jit(solution)/shard_map/before/pallas_call | solution.py:202
  37.8 10.7 %all-to-all-done.1 = bf16[4,256,512]{2,1,0:T(8,128)(2,1)S(1)} async-done(((bf16[4,256,512]{2,1,0:T(8,128)(2,1)}), bf16[4,256,512]{2,1,0:T(8,128)(2,1)S(1)}, u32[]{:S(2)}, u32[]{:S(2)}) %all-to-all-start.1) | async-done | bytes 1048608 | tf_op jit(solution)/shard_map/all_to_all | solution.py:34
  48.5 0.0 copy-done
  48.5 0.0 copy-done.1
  48.5 5.7 %after.1 = (bf16[768,512]{1,0:T(8,128)(2,1)}, bf16[768,512]{1,0:T(8,128)(2,1)S(1)}, bf16[32,48,512]{2,1,0:T(8,128)(2,1)S(1)}, bf16[2,32,512]{2,1,0:T(8,128)(2,1)S(1)}) custom-call(s32[1]{0:T(128)} %bitcast.odd_ref, f32[768,512]{1,0:T(8,128)} %get-tuple-element.17.base_hbm, bf16[768,1152]{1,0:T(8,128)(2,1)} %get-tuple-element.18.p_hbm, ...), custom_call_target="tpu_custom_call" | custom-call | flops 2868903936 | bytes 11534336 | tf_op jit(solution)/shard_map/after/pallas_call | solution.py:219
  54.2 24.5 %all_to_all.25 = bf16[4,384,512]{2,1,0:T(8,128)(2,1)S(1)} all-to-all(bf16[4,384,512]{2,1,0:T(8,128)(2,1)S(1)} %bitcast.22), channel_id=1, replica_groups={{0,16,32,48},{64,80,96,112},{128,144,160,176},{192,208,224,240},{256,27..., dimensions={0} | all-to-all | bytes 3145728 | tf_op jit(solution)/shard_map/all_to_all | solution.py:34
  78.8 0.4 reduce_sum.21
  79.2 16.4 %all_to_all.26.got_ref = bf16[8,48,512]{2,1,0:T(8,128)(2,1)S(1)} all-to-all(bf16[8,48,512]{2,1,0:T(8,128)(2,1)S(1)} %bitcast.26), channel_id=1, replica_groups={{0,64,128,192,256,320,384,448},{16,80,144,208,272,336,400,464},{32,96,1..., dimensions={0} | all-to-all | bytes 786432 | tf_op jit(solution)/shard_map/all_to_all | solution.py:34
  95.6 0.7 last.1
  96.4 7.9 %all-to-all-start.4 = ((bf16[16,16,512]{2,1,0:T(8,128)(2,1)}), bf16[16,16,512]{2,1,0:T(8,128)(2,1)S(1)}, u32[]{:S(2)}, u32[]{:S(2)}) async-start(bf16[16,16,512]{2,1,0:T(8,128)(2,1)} %get-tuple-element.30), calls=%async_computation.4 | async-start | bytes 524288 | tf_op jit(solution)/shard_map/all_to_all | solution.py:263
  104.3 2.0 %collective-permute-start.2 = (bf16[32,512]{1,0:T(8,128)(2,1)S(1)}, bf16[32,512]{1,0:T(8,128)(2,1)S(1)}, u32[]{:S(2)}, u32[]{:S(2)}) collective-permute-start(bf16[32,512]{1,0:T(8,128)(2,1)S(1)} %get-tuple-element.31), channel_id=1, source_target_pairs={{0,1},{1,0},{2,3},{3,2},{4,5},{5,4},{6,7},{7,6},{8,9},{9,8},{10,11... | collective-permute-start | bytes 98312 | tf_op jit(solution)/shard_map/ppermute | solution.py:47
  106.3 3.6 %collective-permute-start.3 = (bf16[32,512]{1,0:T(8,128)(2,1)S(1)}, bf16[32,512]{1,0:T(8,128)(2,1)S(1)}, u32[]{:S(2)}, u32[]{:S(2)}) collective-permute-start(bf16[32,512]{1,0:T(8,128)(2,1)S(1)} %get-tuple-element.32), channel_id=1, source_target_pairs={{1,2},{2,1},{3,4},{4,3},{5,6},{6,5},{7,8},{8,7},{9,10},{10,9},{11,... | collective-permute-start | bytes 98312 | tf_op jit(solution)/shard_map/ppermute | solution.py:47
  109.9 0.1 copy.13
  109.9 0.0 collective-permute-done.2
  109.9 1.9 %collective-permute-done.3 = bf16[32,512]{1,0:T(8,128)(2,1)S(1)} collective-permute-done((bf16[32,512]{1,0:T(8,128)(2,1)S(1)}, bf16[32,512]{1,0:T(8,128)(2,1)S(1)}, u32[]{:S(2)}, u32[]{:S(2)}) %collective-permute-start.3) | collective-permute-done | bytes 32800 | tf_op jit(solution)/shard_map/ppermute | solution.py:47
  111.8 0.0 copy-start.2
  111.9 0.0 all-to-all-done.4
  111.9 0.8 convert_reduce_fusion
  112.6 0.1 copy-done.2
  (2 shorter events, 0.0 us)
Async XLA Ops:
  2.8 18.4 %all-to-all-start = ((bf16[8,32,512]{2,1,0:T(8,128)(2,1)}), bf16[8,32,512]{2,1,0:T(8,128)(2,1)S(1)}, u32[]{:S(2)}, u32[]{:S(2)}) async-start(bf16[8,32,512]{2,1,0:T(8,128)(2,1)} %broadcast_in_dim.14), calls=%async_computation | async-start | bytes 524288 | tf_op jit(solution)/shard_map/all_to_all | solution.py:34
  12.2 7.4 %collective-permute-start.1 = (bf16[32,512]{1,0:T(8,128)(2,1)S(1)}, bf16[32,512]{1,0:T(8,128)(2,1)S(1)}, u32[]{:S(2)}, u32[]{:S(2)}) collective-permute-start(bf16[32,512]{1,0:T(8,128)(2,1)S(1)} %dynamic-slice_bitcast_fusion), channel_id=1, source_target_pairs={{1,2},{2,1},{3,4},{4,3},{5,6},{6,5},{7,8},{8,7},{9,10},{10,9},{11,... | collective-permute-start | bytes 98312 | tf_op jit(solution)/shard_map/ppermute | solution.py:47
  17.7 3.1 %collective-permute-start = (bf16[32,512]{1,0:T(8,128)(2,1)S(1)}, bf16[32,512]{1,0:T(8,128)(2,1)S(1)}, u32[]{:S(2)}, u32[]{:S(2)}) collective-permute-start(bf16[32,512]{1,0:T(8,128)(2,1)S(1)} %dynamic-slice_bitcast_fusion), channel_id=1, source_target_pairs={{0,1},{1,0},{2,3},{3,2},{4,5},{5,4},{6,7},{7,6},{8,9},{9,8},{10,11... | collective-permute-start | bytes 98312 | tf_op jit(solution)/shard_map/ppermute | solution.py:47
  22.3 26.2 %all-to-all-start.1 = ((bf16[4,256,512]{2,1,0:T(8,128)(2,1)}), bf16[4,256,512]{2,1,0:T(8,128)(2,1)S(1)}, u32[]{:S(2)}, u32[]{:S(2)}) async-start(bf16[4,256,512]{2,1,0:T(8,128)(2,1)} %broadcast_in_dim.15), calls=%async_computation.1 | async-start | bytes 2097152 | tf_op jit(solution)/shard_map/all_to_all | solution.py:34
  30.9 17.6 %copy-start = (bf16[1,768,512]{2,1,0:T(8,128)(2,1)S(1)}, bf16[1,768,512]{2,1,0:T(8,128)(2,1)}, u32[]{:S(2)}) copy-start(bf16[1,768,512]{2,1,0:T(8,128)(2,1)} %param.19) | copy-start | bytes 2359300
  30.9 17.6 %copy-start.1 = (bf16[512,512]{1,0:T(8,128)(2,1)S(1)}, bf16[512,512]{1,0:T(8,128)(2,1)}, u32[]{:S(2)}) copy-start(bf16[512,512]{1,0:T(8,128)(2,1)} %weight_ref.1) | copy-start | bytes 1572868
  96.4 15.5 %all-to-all-start.4 = ((bf16[16,16,512]{2,1,0:T(8,128)(2,1)}), bf16[16,16,512]{2,1,0:T(8,128)(2,1)S(1)}, u32[]{:S(2)}, u32[]{:S(2)}) async-start(bf16[16,16,512]{2,1,0:T(8,128)(2,1)} %get-tuple-element.30), calls=%async_computation.4 | async-start | bytes 524288 | tf_op jit(solution)/shard_map/all_to_all | solution.py:263
  104.3 5.7 %collective-permute-start.2 = (bf16[32,512]{1,0:T(8,128)(2,1)S(1)}, bf16[32,512]{1,0:T(8,128)(2,1)S(1)}, u32[]{:S(2)}, u32[]{:S(2)}) collective-permute-start(bf16[32,512]{1,0:T(8,128)(2,1)S(1)} %get-tuple-element.31), channel_id=1, source_target_pairs={{0,1},{1,0},{2,3},{3,2},{4,5},{5,4},{6,7},{7,6},{8,9},{9,8},{10,11... | collective-permute-start | bytes 98312 | tf_op jit(solution)/shard_map/ppermute | solution.py:47
  106.3 5.5 %collective-permute-start.3 = (bf16[32,512]{1,0:T(8,128)(2,1)S(1)}, bf16[32,512]{1,0:T(8,128)(2,1)S(1)}, u32[]{:S(2)}, u32[]{:S(2)}) collective-permute-start(bf16[32,512]{1,0:T(8,128)(2,1)S(1)} %get-tuple-element.32), channel_id=1, source_target_pairs={{1,2},{2,1},{3,4},{4,3},{5,6},{6,5},{7,8},{8,7},{9,10},{10,9},{11,... | collective-permute-start | bytes 98312 | tf_op jit(solution)/shard_map/ppermute | solution.py:47
  111.8 0.9 copy-start.2

commit v7 on v6

--- a/solution.py
+++ b/solution.py
@@ -53,7 +53,7 @@
 
 def before_kernel(
     src_ref, row_ref, count_ref, skip_ref, odd_ref, tiles_ref, feats_ref, stale_ref,
-    base_ref, p_ref, pt_ref, acc_ref,
+    p_ref, pt_ref, acc_ref,
 ):
     slots, blk, tr = tiles_ref.shape
     parts = skip_ref.shape[1]
@@ -79,21 +79,23 @@
 
     lax.fori_loop(0, slots, add_tile, 0)
     live = pt_ref.shape[0]
+    wide = acc_ref.shape[1] - cached
     for r in range(acc_ref.shape[0]):
         out = slice(r * tr, (r + 1) * tr)
         old = acc_ref[r, :cached, :].T.astype(bf16)
-        base_ref[out, :] = feats_ref[out, :].astype(f32) + jnp.dot(
+        base = feats_ref[out, :].astype(f32) + jnp.dot(
             old, stale_ref[...], preferred_element_type=f32
         )
+        p_ref[out, wide:] = base.astype(bf16)
         new = acc_ref[r, cached:, :]
-        p_ref[out, :] = new.T.astype(bf16)
+        p_ref[out, :wide] = new.T.astype(bf16)
         pt_ref[:, out] = new[:live, :].astype(bf16)
 
 
 def after_kernel(
-    odd_ref, base_hbm, p_hbm, pt_hbm, cot_ref, weight_ref, table_ref, inner_ref, outer_ref,
+    odd_ref, p_hbm, pt_hbm, cot_ref, weight_ref, table_ref, inner_ref, outer_ref,
     out_hbm, dagg_ref, send_ref, near_ref,
-    base_ref, p_ref, pt_ref, out_ref, agg_ref, dz_ref, sems, out_sems,
+    p_ref, pt_ref, out_ref, agg_ref, dz_ref, sems, out_sems,
 ):
     nodes, width = cot_ref.shape
     parts = send_ref.shape[0]
@@ -108,33 +110,25 @@
         copy.start()
         return copy
 
-    whole = slice(None)
-    arriving = []
-    for i in range(steps):
-        rows = chunk(i)
-        arriving.append(
-            (fetch(p_hbm, p_ref, rows, 2 * i), fetch(base_hbm, base_ref, rows, 2 * i + 1))
-        )
-    of_pt = fetch(pt_hbm, pt_ref, whole, 2 * steps)
+    arriving = [fetch(p_hbm, p_ref, chunk(i), i) for i in range(steps)]
+    of_pt = fetch(pt_hbm, pt_ref, slice(None), steps)
     cached = parts * blk
+    wide = p_ref.shape[1] - width
     near_rows = jnp.concatenate([inner_ref[...], outer_ref[...]], axis=0)
     leaving = []
     for i in range(steps):
         rows = chunk(i)
-        of_p, of_base = arriving[i]
         if i == 0:
-            of_p.wait()
-            of_base.wait()
+            arriving[0].wait()
         if i == 1:
-            for a, b in arriving[1:]:
-                a.wait()
-                b.wait()
+            for copy in arriving[1:]:
+                copy.wait()
             of_pt.wait()
         new = jnp.dot(p_ref[rows, :cached], table_ref[...], preferred_element_type=f32)
         new += jnp.dot(
             p_ref[rows, cached : cached + 2 * blk], near_rows, preferred_element_type=f32
         )
-        agg = (base_ref[rows, :] + new).astype(bf16)
+        agg = (p_ref[rows, wide:].astype(f32) + new).astype(bf16)
         agg_ref[rows, :] = agg
         z = jnp.dot(agg, weight_ref[...], preferred_element_type=f32)
         sig = jax.nn.sigmoid(z)
@@ -199,15 +193,14 @@
     smem = pl.BlockSpec(memory_space=pltpu.SMEM)
     vmem = pl.BlockSpec(memory_space=pltpu.VMEM)
     hbm = pl.BlockSpec(memory_space=pltpu.HBM)
-    base, p, pt = pl.pallas_call(
+    p, pt = pl.pallas_call(
         before_kernel,
         out_shape=(
-            jax.ShapeDtypeStruct((nodes, width), f32),
-            jax.ShapeDtypeStruct((nodes, (parts + 4) * blk), bf16),
+            jax.ShapeDtypeStruct((nodes, (parts + 4) * blk + width), bf16),
             jax.ShapeDtypeStruct(((parts + 2) * blk, nodes), bf16),
         ),
         in_specs=[smem] * 5 + [vmem] * 3,
-        out_specs=(vmem,) * 3,
+        out_specs=(vmem,) * 2,
         scratch_shapes=[pltpu.VMEM((row_blocks, (2 * parts + 4) * blk, tr), f32)],
         compiler_params=pltpu.CompilerParams(vmem_limit_bytes=60 << 20),
         cost_estimate=pl.CostEstimate(
@@ -224,16 +217,15 @@
             jax.ShapeDtypeStruct((parts, blk + share, width), bf16),
             jax.ShapeDtypeStruct((2, blk, width), bf16),
         ),
-        in_specs=[smem] + [hbm] * 3 + [vmem] * 5,
+        in_specs=[smem] + [hbm] * 2 + [vmem] * 5,
         out_specs=(hbm, vmem, vmem, vmem),
         scratch_shapes=[
-            pltpu.VMEM((nodes, width), f32),
-            pltpu.VMEM((nodes, (parts + 4) * blk), bf16),
+            pltpu.VMEM((nodes, (parts + 4) * blk + width), bf16),
             pltpu.VMEM(((parts + 2) * blk, nodes), bf16),
             pltpu.VMEM((nodes, width), bf16),
             pltpu.VMEM((nodes, width), bf16),
             pltpu.VMEM((nodes, width), bf16),
-            pltpu.SemaphoreType.DMA((nodes // 256 * 2 + 1,)),
+            pltpu.SemaphoreType.DMA((nodes // 256 + 1,)),
             pltpu.SemaphoreType.DMA((nodes // 256,)),
         ],
         compiler_params=pltpu.CompilerParams(vmem_limit_bytes=48 << 20),
@@ -243,7 +235,7 @@
             transcendentals=nodes * width,
         ),
         name="after",
-    )(odd, base, p, pt, cotangent[0], weight, table, inner, outer)
+    )(odd, p, pt, cotangent[0], weight, table, inner, outer)
     rows = blk + share
     got = exchange(send.reshape(YH, Z * rows, width), fours)
     some = got.astype(f32).sum(axis=0).astype(bf16)
@@ -261,8 +253,8 @@
     )(got)
     gw, near = lax.optimization_barrier((gw, near))
     gw = lax.all_to_all(gw, "cluster", 0, 0, tiled=True)
+    from_outer = swapped(near[1], "cluster", 1)
     from_inner = swapped(near[0], "cluster", 0)
-    from_outer = swapped(near[1], "cluster", 1)
     grad_weight = gw.astype(f32).sum(axis=0)
     bgrad = mine + from_inner.astype(f32) + from_outer.astype(f32)
     current = lax.dynamic_slice_in_dim(dagg, start_row, blk, 0).astype(f32)

time: 115 us -> 114 us (level)
  no operation moved by 1% of the time
where the time goes in v7:
time: 114 us; the launch traced here: 112 us
  blocking collectives  40.9 us (36%)
  starting transfers between devices  38.9 us (34%)
  waiting for transfers between devices  14.6 us (13%)
  Pallas kernels  11.9 us (10%)
  local copies, waits for them, and re-layouts  2.69 us (2%)
  between operations  2.14 us (2%)
  other arithmetic  1.24 us (1%)
    all_to_all x2, blocking collectives, exchange(): return lax.all_to_all(x, ALL, 0, 0, axis_index_groups=grouping, tiled=True)  40.9 us
    all_to_all x2, starting transfers between devices, exchange(): return lax.all_to_all(x, ALL, 0, 0, axis_index_groups=grouping, tiled=True)  18.1 us
    ppermute x4, starting transfers between devices, swapped(): return lax.ppermute(x, axis, pairs)  13 us
    all_to_all x2, waiting for transfers between devices, exchange(): return lax.all_to_all(x, ALL, 0, 0, axis_index_groups=grouping, tiled=True)  11.5 us
    all_to_all x1, starting transfers between devices, per_device(): gw = lax.all_to_all(gw, 'cluster', 0, 0, tiled=True)  7.91 us
    pallas_call x1, Pallas kernels, per_device(): pl.pallas_call(before_kernel, out_shape=(jax.ShapeDtypeStruct((nodes, (pa...  5.7 us
    pallas_call x1, Pallas kernels, per_device(): pl.pallas_call(after_kernel, out_shape=(jax.ShapeDtypeStruct((nodes, widt...  5.47 us
    ppermute x4, waiting for transfers between devices, swapped(): return lax.ppermute(x, axis, pairs)  3.03 us
  transfers between devices with their start and end apart: 7, of which 4 were waited for; matrix products, arithmetic and copies ran while one was open for 0% of the time, Pallas kernels for 5%

profile of v7, /device:TPU:1, one launch (start us, length us, event | category | flops | bytes accessed | tf_op | source)
XLA Modules:
  0.0 112.4 jit_solution(11317742135238408917)
XLA Ops:
  1.3 0.8 dynamic-slice_bitcast_fusion
  2.0 0.7 broadcast_in_dim.14
  2.8 9.5 %all-to-all-start = ((bf16[8,32,512]{2,1,0:T(8,128)(2,1)}), bf16[8,32,512]{2,1,0:T(8,128)(2,1)S(1)}, u32[]{:S(2)}, u32[]{:S(2)}) async-start(bf16[8,32,512]{2,1,0:T(8,128)(2,1)} %broadcast_in_dim.14), calls=%async_computation | async-start | bytes 524288 | tf_op jit(solution)/shard_map/all_to_all | solution.py:34
  12.2 5.4 %collective-permute-start.1 = (bf16[32,512]{1,0:T(8,128)(2,1)S(1)}, bf16[32,512]{1,0:T(8,128)(2,1)S(1)}, u32[]{:S(2)}, u32[]{:S(2)}) collective-permute-start(bf16[32,512]{1,0:T(8,128)(2,1)S(1)} %dynamic-slice_bitcast_fusion), channel_id=1, source_target_pairs={{1,2},{2,1},{3,4},{4,3},{5,6},{6,5},{7,8},{8,7},{9,10},{10,9},{11,... | collective-permute-start | bytes 98312 | tf_op jit(solution)/shard_map/ppermute | solution.py:47
  17.7 1.9 %collective-permute-start = (bf16[32,512]{1,0:T(8,128)(2,1)S(1)}, bf16[32,512]{1,0:T(8,128)(2,1)S(1)}, u32[]{:S(2)}, u32[]{:S(2)}) collective-permute-start(bf16[32,512]{1,0:T(8,128)(2,1)S(1)} %dynamic-slice_bitcast_fusion), channel_id=1, source_target_pairs={{0,1},{1,0},{2,3},{3,2},{4,5},{5,4},{6,7},{7,6},{8,9},{9,8},{10,11... | collective-permute-start | bytes 98312 | tf_op jit(solution)/shard_map/ppermute | solution.py:47
  19.6 0.0 collective-permute-done.1.outer_ref
  19.6 1.2 %collective-permute-done.inner_ref = bf16[32,512]{1,0:T(8,128)(2,1)S(1)} collective-permute-done((bf16[32,512]{1,0:T(8,128)(2,1)S(1)}, bf16[32,512]{1,0:T(8,128)(2,1)S(1)}, u32[]{:S(2)}, u32[]{:S(2)}) %collective-permute-start) | collective-permute-done | bytes 32800 | tf_op jit(solution)/shard_map/ppermute | solution.py:47
  20.8 0.4 all-to-all-done
  21.2 1.0 broadcast_in_dim.15
  22.2 8.6 %all-to-all-start.1 = ((bf16[4,256,512]{2,1,0:T(8,128)(2,1)}), bf16[4,256,512]{2,1,0:T(8,128)(2,1)S(1)}, u32[]{:S(2)}, u32[]{:S(2)}) async-start(bf16[4,256,512]{2,1,0:T(8,128)(2,1)} %broadcast_in_dim.15), calls=%async_computation.1 | async-start | bytes 2097152 | tf_op jit(solution)/shard_map/all_to_all | solution.py:34
  30.8 0.0 copy-start
  30.8 0.0 copy-start.1
  31.6 5.7 %before.1 = (bf16[768,1664]{1,0:T(8,128)(2,1)}, bf16[1088,768]{1,0:T(8,128)(2,1)}) custom-call(s32[1,32]{1,0:T(1,128)} %src_ref.1, s32[1,32]{1,0:T(1,128)} %row_ref.1, s32[1,1]{1,0:T(1,128)S(6)} %copy.15.count_ref, s32[1,32]{1,0:T(1,128)} %skip_ref.1, s32[1]{0:T(128)} %bitcast.odd_ref, bf16[32,32,128]{2,1,0:T(8,128)(2,1)} %bitcast.30, ...), custom_call_target="tpu_custom_call" | custom-call | flops 805306368 | bytes 8388608 | tf_op jit(solution)/shard_map/before/pallas_call | solution.py:196
  37.3 11.1 %all-to-all-done.1 = bf16[4,256,512]{2,1,0:T(8,128)(2,1)S(1)} async-done(((bf16[4,256,512]{2,1,0:T(8,128)(2,1)}), bf16[4,256,512]{2,1,0:T(8,128)(2,1)S(1)}, u32[]{:S(2)}, u32[]{:S(2)}) %all-to-all-start.1) | async-done | bytes 1048608 | tf_op jit(solution)/shard_map/all_to_all | solution.py:34
  48.4 0.0 copy-done
  48.5 0.0 copy-done.1
  48.5 5.5 %after.1 = (bf16[768,512]{1,0:T(8,128)(2,1)}, bf16[768,512]{1,0:T(8,128)(2,1)S(1)}, bf16[32,48,512]{2,1,0:T(8,128)(2,1)S(1)}, bf16[2,32,512]{2,1,0:T(8,128)(2,1)S(1)}) custom-call(s32[1]{0:T(128)} %bitcast.odd_ref, bf16[768,1664]{1,0:T(8,128)(2,1)} %get-tuple-element.16.p_hbm, bf16[1088,768]{1,0:T(8,128)(2,1)} %get-tuple-element.17.pt_hbm, ...), custom_call_target="tpu_custom_call" | custom-call | flops 2868903936 | bytes 11534336 | tf_op jit(solution)/shard_map/after/pallas_call | solution.py:212
  53.9 24.5 %all_to_all.25 = bf16[4,384,512]{2,1,0:T(8,128)(2,1)S(1)} all-to-all(bf16[4,384,512]{2,1,0:T(8,128)(2,1)S(1)} %bitcast.22), channel_id=1, replica_groups={{0,16,32,48},{64,80,96,112},{128,144,160,176},{192,208,224,240},{256,27..., dimensions={0} | all-to-all | bytes 3145728 | tf_op jit(solution)/shard_map/all_to_all | solution.py:34
  78.5 0.4 reduce_sum.21
  78.9 16.4 %all_to_all.26.got_ref = bf16[8,48,512]{2,1,0:T(8,128)(2,1)S(1)} all-to-all(bf16[8,48,512]{2,1,0:T(8,128)(2,1)S(1)} %bitcast.26), channel_id=1, replica_groups={{0,64,128,192,256,320,384,448},{16,80,144,208,272,336,400,464},{32,96,1..., dimensions={0} | all-to-all | bytes 786432 | tf_op jit(solution)/shard_map/all_to_all | solution.py:34
  95.3 0.7 last.1
  96.0 7.9 %all-to-all-start.4 = ((bf16[16,16,512]{2,1,0:T(8,128)(2,1)}), bf16[16,16,512]{2,1,0:T(8,128)(2,1)S(1)}, u32[]{:S(2)}, u32[]{:S(2)}) async-start(bf16[16,16,512]{2,1,0:T(8,128)(2,1)} %get-tuple-element.28), calls=%async_computation.4 | async-start | bytes 524288 | tf_op jit(solution)/shard_map/all_to_all | solution.py:255
  104.0 2.0 %collective-permute-start.2 = (bf16[32,512]{1,0:T(8,128)(2,1)S(1)}, bf16[32,512]{1,0:T(8,128)(2,1)S(1)}, u32[]{:S(2)}, u32[]{:S(2)}) collective-permute-start(bf16[32,512]{1,0:T(8,128)(2,1)S(1)} %get-tuple-element.29), channel_id=1, source_target_pairs={{0,1},{1,0},{2,3},{3,2},{4,5},{5,4},{6,7},{7,6},{8,9},{9,8},{10,11... | collective-permute-start | bytes 98312 | tf_op jit(solution)/shard_map/ppermute | solution.py:47
  106.0 3.6 %collective-permute-start.3 = (bf16[32,512]{1,0:T(8,128)(2,1)S(1)}, bf16[32,512]{1,0:T(8,128)(2,1)S(1)}, u32[]{:S(2)}, u32[]{:S(2)}) collective-permute-start(bf16[32,512]{1,0:T(8,128)(2,1)S(1)} %get-tuple-element.30), channel_id=1, source_target_pairs={{1,2},{2,1},{3,4},{4,3},{5,6},{6,5},{7,8},{8,7},{9,10},{10,9},{11,... | collective-permute-start | bytes 98312 | tf_op jit(solution)/shard_map/ppermute | solution.py:47
  109.6 0.1 copy.13
  109.6 0.0 collective-permute-done.2
  109.6 1.9 %collective-permute-done.3 = bf16[32,512]{1,0:T(8,128)(2,1)S(1)} collective-permute-done((bf16[32,512]{1,0:T(8,128)(2,1)S(1)}, bf16[32,512]{1,0:T(8,128)(2,1)S(1)}, u32[]{:S(2)}, u32[]{:S(2)}) %collective-permute-start.3) | collective-permute-done | bytes 32800 | tf_op jit(solution)/shard_map/ppermute | solution.py:47
  111.5 0.0 copy-start.2
  111.5 0.0 all-to-all-done.4
  111.5 0.8 convert_reduce_fusion
  112.3 0.1 copy-done.2
  (2 shorter events, 0.0 us)
Async XLA Ops:
  2.8 18.4 %all-to-all-start = ((bf16[8,32,512]{2,1,0:T(8,128)(2,1)}), bf16[8,32,512]{2,1,0:T(8,128)(2,1)S(1)}, u32[]{:S(2)}, u32[]{:S(2)}) async-start(bf16[8,32,512]{2,1,0:T(8,128)(2,1)} %broadcast_in_dim.14), calls=%async_computation | async-start | bytes 524288 | tf_op jit(solution)/shard_map/all_to_all | solution.py:34
  12.2 7.4 %collective-permute-start.1 = (bf16[32,512]{1,0:T(8,128)(2,1)S(1)}, bf16[32,512]{1,0:T(8,128)(2,1)S(1)}, u32[]{:S(2)}, u32[]{:S(2)}) collective-permute-start(bf16[32,512]{1,0:T(8,128)(2,1)S(1)} %dynamic-slice_bitcast_fusion), channel_id=1, source_target_pairs={{1,2},{2,1},{3,4},{4,3},{5,6},{6,5},{7,8},{8,7},{9,10},{10,9},{11,... | collective-permute-start | bytes 98312 | tf_op jit(solution)/shard_map/ppermute | solution.py:47
  17.7 3.1 %collective-permute-start = (bf16[32,512]{1,0:T(8,128)(2,1)S(1)}, bf16[32,512]{1,0:T(8,128)(2,1)S(1)}, u32[]{:S(2)}, u32[]{:S(2)}) collective-permute-start(bf16[32,512]{1,0:T(8,128)(2,1)S(1)} %dynamic-slice_bitcast_fusion), channel_id=1, source_target_pairs={{0,1},{1,0},{2,3},{3,2},{4,5},{5,4},{6,7},{7,6},{8,9},{9,8},{10,11... | collective-permute-start | bytes 98312 | tf_op jit(solution)/shard_map/ppermute | solution.py:47
  22.2 26.2 %all-to-all-start.1 = ((bf16[4,256,512]{2,1,0:T(8,128)(2,1)}), bf16[4,256,512]{2,1,0:T(8,128)(2,1)S(1)}, u32[]{:S(2)}, u32[]{:S(2)}) async-start(bf16[4,256,512]{2,1,0:T(8,128)(2,1)} %broadcast_in_dim.15), calls=%async_computation.1 | async-start | bytes 2097152 | tf_op jit(solution)/shard_map/all_to_all | solution.py:34
  30.8 17.6 %copy-start = (bf16[1,768,512]{2,1,0:T(8,128)(2,1)S(1)}, bf16[1,768,512]{2,1,0:T(8,128)(2,1)}, u32[]{:S(2)}) copy-start(bf16[1,768,512]{2,1,0:T(8,128)(2,1)} %param.19) | copy-start | bytes 2359300
  30.8 17.6 %copy-start.1 = (bf16[512,512]{1,0:T(8,128)(2,1)S(1)}, bf16[512,512]{1,0:T(8,128)(2,1)}, u32[]{:S(2)}) copy-start(bf16[512,512]{1,0:T(8,128)(2,1)} %weight_ref.1) | copy-start | bytes 1572868
  96.0 15.5 %all-to-all-start.4 = ((bf16[16,16,512]{2,1,0:T(8,128)(2,1)}), bf16[16,16,512]{2,1,0:T(8,128)(2,1)S(1)}, u32[]{:S(2)}, u32[]{:S(2)}) async-start(bf16[16,16,512]{2,1,0:T(8,128)(2,1)} %get-tuple-element.28), calls=%async_computation.4 | async-start | bytes 524288 | tf_op jit(solution)/shard_map/all_to_all | solution.py:255
  104.0 5.7 %collective-permute-start.2 = (bf16[32,512]{1,0:T(8,128)(2,1)S(1)}, bf16[32,512]{1,0:T(8,128)(2,1)S(1)}, u32[]{:S(2)}, u32[]{:S(2)}) collective-permute-start(bf16[32,512]{1,0:T(8,128)(2,1)S(1)} %get-tuple-element.29), channel_id=1, source_target_pairs={{0,1},{1,0},{2,3},{3,2},{4,5},{5,4},{6,7},{7,6},{8,9},{9,8},{10,11... | collective-permute-start | bytes 98312 | tf_op jit(solution)/shard_map/ppermute | solution.py:47
  106.0 5.5 %collective-permute-start.3 = (bf16[32,512]{1,0:T(8,128)(2,1)S(1)}, bf16[32,512]{1,0:T(8,128)(2,1)S(1)}, u32[]{:S(2)}, u32[]{:S(2)}) collective-permute-start(bf16[32,512]{1,0:T(8,128)(2,1)S(1)} %get-tuple-element.30), channel_id=1, source_target_pairs={{1,2},{2,1},{3,4},{4,3},{5,6},{6,5},{7,8},{8,7},{9,10},{10,9},{11,... | collective-permute-start | bytes 98312 | tf_op jit(solution)/shard_map/ppermute | solution.py:47
  111.5 0.9 copy-start.2

commit v8 on v7

--- a/solution.py
+++ b/solution.py
@@ -17,7 +17,7 @@
     at = lambda z, y, c: (z * YH + y) * clusters + c
     eights, fours = [], []
     for c in range(clusters):
-        if c % 2 == 0:
+        if c % 2 == 1:
             eights += [[at(z, y, c) for z in range(Z)] for y in range(YH)]
             fours += [[at(z, y, c) for y in range(YH)] for z in range(Z)]
         else:
@@ -48,7 +48,7 @@
 
 
 def place_of(part, odd):
-    return jnp.where(odd == 1, part, part % YH * Z + part // YH)
+    return jnp.where(odd == 0, part, part % YH * Z + part // YH)
 
 
 def before_kernel(

time: 114 us -> 116 us (1.018)
  starting transfers between devices: 38.9 us -> 42.5 us
  blocking collectives: 40.9 us -> 39.7 us
    all_to_all x1, starting transfers between devices: 7.91 us -> 11.1 us  [per_device(): gw = lax.all_to_all(gw, 'cluster', 0, 0, tiled=True)]
    all_to_all x2, blocking collectives: 40.9 us -> 39.7 us  [exchange(): return lax.all_to_all(x, ALL, 0, 0, axis_index_groups=grouping, tiled=True)]
where the time goes in v8:
time: 116 us; the launch traced here: 114 us
  starting transfers between devices  42.5 us (37%)
  blocking collectives  39.7 us (34%)
  waiting for transfers between devices  14 us (12%)
  Pallas kernels  11.9 us (10%)
  local copies, waits for them, and re-layouts  2.69 us (2%)
  between operations  2.14 us (2%)
  other arithmetic  1.24 us (1%)
    all_to_all x2, blocking collectives, exchange(): return lax.all_to_all(x, ALL, 0, 0, axis_index_groups=grouping, tiled=True)  39.7 us
    all_to_all x2, starting transfers between devices, exchange(): return lax.all_to_all(x, ALL, 0, 0, axis_index_groups=grouping, tiled=True)  18.2 us
    ppermute x4, starting transfers between devices, swapped(): return lax.ppermute(x, axis, pairs)  13.3 us
    all_to_all x2, waiting for transfers between devices, exchange(): return lax.all_to_all(x, ALL, 0, 0, axis_index_groups=grouping, tiled=True)  11.3 us
    all_to_all x1, starting transfers between devices, per_device(): gw = lax.all_to_all(gw, 'cluster', 0, 0, tiled=True)  11.1 us
    pallas_call x1, Pallas kernels, per_device(): pl.pallas_call(before_kernel, out_shape=(jax.ShapeDtypeStruct((nodes, (pa...  5.65 us
    pallas_call x1, Pallas kernels, per_device(): pl.pallas_call(after_kernel, out_shape=(jax.ShapeDtypeStruct((nodes, widt...  5.47 us
    ppermute x4, waiting for transfers between devices, swapped(): return lax.ppermute(x, axis, pairs)  2.7 us
  transfers between devices with their start and end apart: 7, of which 4 were waited for; matrix products, arithmetic and copies ran while one was open for 0% of the time, Pallas kernels for 5%

profile of v8, /device:TPU:1, one launch (start us, length us, event | category | flops | bytes accessed | tf_op | source)
XLA Modules:
  0.0 114.2 jit_solution(3400160452110749520)
XLA Ops:
  1.3 0.8 dynamic-slice_bitcast_fusion
  2.0 0.7 broadcast_in_dim.14
  2.8 10.9 %all-to-all-start = ((bf16[8,32,512]{2,1,0:T(8,128)(2,1)}), bf16[8,32,512]{2,1,0:T(8,128)(2,1)S(1)}, u32[]{:S(2)}, u32[]{:S(2)}) async-start(bf16[8,32,512]{2,1,0:T(8,128)(2,1)} %broadcast_in_dim.14), calls=%async_computation | async-start | bytes 524288 | tf_op jit(solution)/shard_map/all_to_all | solution.py:34
  13.6 1.9 %collective-permute-start.1 = (bf16[32,512]{1,0:T(8,128)(2,1)S(1)}, bf16[32,512]{1,0:T(8,128)(2,1)S(1)}, u32[]{:S(2)}, u32[]{:S(2)}) collective-permute-start(bf16[32,512]{1,0:T(8,128)(2,1)S(1)} %dynamic-slice_bitcast_fusion), channel_id=1, source_target_pairs={{1,2},{2,1},{3,4},{4,3},{5,6},{6,5},{7,8},{8,7},{9,10},{10,9},{11,... | collective-permute-start | bytes 98312 | tf_op jit(solution)/shard_map/ppermute | solution.py:47
  15.6 5.8 %collective-permute-start = (bf16[32,512]{1,0:T(8,128)(2,1)S(1)}, bf16[32,512]{1,0:T(8,128)(2,1)S(1)}, u32[]{:S(2)}, u32[]{:S(2)}) collective-permute-start(bf16[32,512]{1,0:T(8,128)(2,1)S(1)} %dynamic-slice_bitcast_fusion), channel_id=1, source_target_pairs={{0,1},{1,0},{2,3},{3,2},{4,5},{5,4},{6,7},{7,6},{8,9},{9,8},{10,11... | collective-permute-start | bytes 98312 | tf_op jit(solution)/shard_map/ppermute | solution.py:47
  21.3 0.0 collective-permute-done.1.outer_ref
  21.4 0.8 collective-permute-done.inner_ref
  22.2 0.6 all-to-all-done
  22.8 1.0 broadcast_in_dim.15
  23.9 7.3 %all-to-all-start.1 = ((bf16[4,256,512]{2,1,0:T(8,128)(2,1)}), bf16[4,256,512]{2,1,0:T(8,128)(2,1)S(1)}, u32[]{:S(2)}, u32[]{:S(2)}) async-start(bf16[4,256,512]{2,1,0:T(8,128)(2,1)} %broadcast_in_dim.15), calls=%async_computation.1 | async-start | bytes 2097152 | tf_op jit(solution)/shard_map/all_to_all | solution.py:34
  31.2 0.0 copy-start
  31.2 0.0 copy-start.1
  31.9 5.6 %before.1 = (bf16[768,1664]{1,0:T(8,128)(2,1)}, bf16[1088,768]{1,0:T(8,128)(2,1)}) custom-call(s32[1,32]{1,0:T(1,128)} %src_ref.1, s32[1,32]{1,0:T(1,128)} %row_ref.1, s32[1,1]{1,0:T(1,128)S(6)} %copy.15.count_ref, s32[1,32]{1,0:T(1,128)} %skip_ref.1, s32[1]{0:T(128)} %bitcast.odd_ref, bf16[32,32,128]{2,1,0:T(8,128)(2,1)} %bitcast.30, ...), custom_call_target="tpu_custom_call" | custom-call | flops 805306368 | bytes 8388608 | tf_op jit(solution)/shard_map/before/pallas_call | solution.py:196
  37.6 10.7 %all-to-all-done.1 = bf16[4,256,512]{2,1,0:T(8,128)(2,1)S(1)} async-done(((bf16[4,256,512]{2,1,0:T(8,128)(2,1)}), bf16[4,256,512]{2,1,0:T(8,128)(2,1)S(1)}, u32[]{:S(2)}, u32[]{:S(2)}) %all-to-all-start.1) | async-done | bytes 1048608 | tf_op jit(solution)/shard_map/all_to_all | solution.py:34
  48.3 0.0 copy-done
  48.3 0.0 copy-done.1
  48.3 5.5 %after.1 = (bf16[768,512]{1,0:T(8,128)(2,1)}, bf16[768,512]{1,0:T(8,128)(2,1)S(1)}, bf16[32,48,512]{2,1,0:T(8,128)(2,1)S(1)}, bf16[2,32,512]{2,1,0:T(8,128)(2,1)S(1)}) custom-call(s32[1]{0:T(128)} %bitcast.odd_ref, bf16[768,1664]{1,0:T(8,128)(2,1)} %get-tuple-element.16.p_hbm, bf16[1088,768]{1,0:T(8,128)(2,1)} %get-tuple-element.17.pt_hbm, ...), custom_call_target="tpu_custom_call" | custom-call | flops 2868903936 | bytes 11534336 | tf_op jit(solution)/shard_map/after/pallas_call | solution.py:212
  53.8 24.6 %all_to_all.25 = bf16[4,384,512]{2,1,0:T(8,128)(2,1)S(1)} all-to-all(bf16[4,384,512]{2,1,0:T(8,128)(2,1)S(1)} %bitcast.22), channel_id=1, replica_groups={{0,128,256,384},{16,144,272,400},{32,160,288,416},{48,176,304,432},{64,..., dimensions={0} | all-to-all | bytes 3145728 | tf_op jit(solution)/shard_map/all_to_all | solution.py:34
  78.3 0.4 reduce_sum.21
  78.8 15.1 %all_to_all.26.got_ref = bf16[8,48,512]{2,1,0:T(8,128)(2,1)S(1)} all-to-all(bf16[8,48,512]{2,1,0:T(8,128)(2,1)S(1)} %bitcast.26), channel_id=1, replica_groups={{0,16,32,48,64,80,96,112},{128,144,160,176,192,208,224,240},{256,272,28..., dimensions={0} | all-to-all | bytes 786432 | tf_op jit(solution)/shard_map/all_to_all | solution.py:34
  93.9 0.7 last.1
  94.6 11.1 %all-to-all-start.4 = ((bf16[16,16,512]{2,1,0:T(8,128)(2,1)}), bf16[16,16,512]{2,1,0:T(8,128)(2,1)S(1)}, u32[]{:S(2)}, u32[]{:S(2)}) async-start(bf16[16,16,512]{2,1,0:T(8,128)(2,1)} %get-tuple-element.28), calls=%async_computation.4 | async-start | bytes 524288 | tf_op jit(solution)/shard_map/all_to_all | solution.py:255
  105.7 2.0 %collective-permute-start.2 = (bf16[32,512]{1,0:T(8,128)(2,1)S(1)}, bf16[32,512]{1,0:T(8,128)(2,1)S(1)}, u32[]{:S(2)}, u32[]{:S(2)}) collective-permute-start(bf16[32,512]{1,0:T(8,128)(2,1)S(1)} %get-tuple-element.29), channel_id=1, source_target_pairs={{0,1},{1,0},{2,3},{3,2},{4,5},{5,4},{6,7},{7,6},{8,9},{9,8},{10,11... | collective-permute-start | bytes 98312 | tf_op jit(solution)/shard_map/ppermute | solution.py:47
  107.7 3.6 %collective-permute-start.3 = (bf16[32,512]{1,0:T(8,128)(2,1)S(1)}, bf16[32,512]{1,0:T(8,128)(2,1)S(1)}, u32[]{:S(2)}, u32[]{:S(2)}) collective-permute-start(bf16[32,512]{1,0:T(8,128)(2,1)S(1)} %get-tuple-element.30), channel_id=1, source_target_pairs={{1,2},{2,1},{3,4},{4,3},{5,6},{6,5},{7,8},{8,7},{9,10},{10,9},{11,... | collective-permute-start | bytes 98312 | tf_op jit(solution)/shard_map/ppermute | solution.py:47
  111.3 0.1 copy.13
  111.4 0.0 collective-permute-done.2
  111.4 1.9 %collective-permute-done.3 = bf16[32,512]{1,0:T(8,128)(2,1)S(1)} collective-permute-done((bf16[32,512]{1,0:T(8,128)(2,1)S(1)}, bf16[32,512]{1,0:T(8,128)(2,1)S(1)}, u32[]{:S(2)}, u32[]{:S(2)}) %collective-permute-start.3) | collective-permute-done | bytes 32800 | tf_op jit(solution)/shard_map/ppermute | solution.py:47
  113.3 0.0 copy-start.2
  113.3 0.0 all-to-all-done.4
  113.3 0.8 convert_reduce_fusion
  114.1 0.1 copy-done.2
  (2 shorter events, 0.0 us)
Async XLA Ops:
  2.8 20.1 %all-to-all-start = ((bf16[8,32,512]{2,1,0:T(8,128)(2,1)}), bf16[8,32,512]{2,1,0:T(8,128)(2,1)S(1)}, u32[]{:S(2)}, u32[]{:S(2)}) async-start(bf16[8,32,512]{2,1,0:T(8,128)(2,1)} %broadcast_in_dim.14), calls=%async_computation | async-start | bytes 524288 | tf_op jit(solution)/shard_map/all_to_all | solution.py:34
  13.6 7.7 %collective-permute-start.1 = (bf16[32,512]{1,0:T(8,128)(2,1)S(1)}, bf16[32,512]{1,0:T(8,128)(2,1)S(1)}, u32[]{:S(2)}, u32[]{:S(2)}) collective-permute-start(bf16[32,512]{1,0:T(8,128)(2,1)S(1)} %dynamic-slice_bitcast_fusion), channel_id=1, source_target_pairs={{1,2},{2,1},{3,4},{4,3},{5,6},{6,5},{7,8},{8,7},{9,10},{10,9},{11,... | collective-permute-start | bytes 98312 | tf_op jit(solution)/shard_map/ppermute | solution.py:47
  15.6 6.6 %collective-permute-start = (bf16[32,512]{1,0:T(8,128)(2,1)S(1)}, bf16[32,512]{1,0:T(8,128)(2,1)S(1)}, u32[]{:S(2)}, u32[]{:S(2)}) collective-permute-start(bf16[32,512]{1,0:T(8,128)(2,1)S(1)} %dynamic-slice_bitcast_fusion), channel_id=1, source_target_pairs={{0,1},{1,0},{2,3},{3,2},{4,5},{5,4},{6,7},{7,6},{8,9},{9,8},{10,11... | collective-permute-start | bytes 98312 | tf_op jit(solution)/shard_map/ppermute | solution.py:47
  23.9 24.4 %all-to-all-start.1 = ((bf16[4,256,512]{2,1,0:T(8,128)(2,1)}), bf16[4,256,512]{2,1,0:T(8,128)(2,1)S(1)}, u32[]{:S(2)}, u32[]{:S(2)}) async-start(bf16[4,256,512]{2,1,0:T(8,128)(2,1)} %broadcast_in_dim.15), calls=%async_computation.1 | async-start | bytes 2097152 | tf_op jit(solution)/shard_map/all_to_all | solution.py:34
  31.2 17.1 %copy-start = (bf16[1,768,512]{2,1,0:T(8,128)(2,1)S(1)}, bf16[1,768,512]{2,1,0:T(8,128)(2,1)}, u32[]{:S(2)}) copy-start(bf16[1,768,512]{2,1,0:T(8,128)(2,1)} %param.19) | copy-start | bytes 2359300
  31.2 17.1 %copy-start.1 = (bf16[512,512]{1,0:T(8,128)(2,1)S(1)}, bf16[512,512]{1,0:T(8,128)(2,1)}, u32[]{:S(2)}) copy-start(bf16[512,512]{1,0:T(8,128)(2,1)} %weight_ref.1) | copy-start | bytes 1572868
  94.6 18.7 %all-to-all-start.4 = ((bf16[16,16,512]{2,1,0:T(8,128)(2,1)}), bf16[16,16,512]{2,1,0:T(8,128)(2,1)S(1)}, u32[]{:S(2)}, u32[]{:S(2)}) async-start(bf16[16,16,512]{2,1,0:T(8,128)(2,1)} %get-tuple-element.28), calls=%async_computation.4 | async-start | bytes 524288 | tf_op jit(solution)/shard_map/all_to_all | solution.py:255
  105.7 5.7 %collective-permute-start.2 = (bf16[32,512]{1,0:T(8,128)(2,1)S(1)}, bf16[32,512]{1,0:T(8,128)(2,1)S(1)}, u32[]{:S(2)}, u32[]{:S(2)}) collective-permute-start(bf16[32,512]{1,0:T(8,128)(2,1)S(1)} %get-tuple-element.29), channel_id=1, source_target_pairs={{0,1},{1,0},{2,3},{3,2},{4,5},{5,4},{6,7},{7,6},{8,9},{9,8},{10,11... | collective-permute-start | bytes 98312 | tf_op jit(solution)/shard_map/ppermute | solution.py:47
  107.7 5.5 %collective-permute-start.3 = (bf16[32,512]{1,0:T(8,128)(2,1)S(1)}, bf16[32,512]{1,0:T(8,128)(2,1)S(1)}, u32[]{:S(2)}, u32[]{:S(2)}) collective-permute-start(bf16[32,512]{1,0:T(8,128)(2,1)S(1)} %get-tuple-element.30), channel_id=1, source_target_pairs={{1,2},{2,1},{3,4},{4,3},{5,6},{6,5},{7,8},{8,7},{9,10},{10,9},{11,... | collective-permute-start | bytes 98312 | tf_op jit(solution)/shard_map/ppermute | solution.py:47
  113.3 0.9 copy-start.2
